TPU v7x, 32 devices: a whole 2x2x4 slice. The times are simulated.
32 devices in a mesh: seq: 16 (over z, x, core), tp: 2 (over y).
Axes of the slice: x: 2, y: 2, z: 4, core: 2. Of those that a mesh axis runs over, the one named last changes fastest.
Arguments:
- tokens: bfloat16 [8192, 2560], P('seq', 'tp'), may hold values from -4 to 4
- norm_gain: bfloat16 [2560], P('tp'), may hold values from 0.099609375 to 1.8984375
- w_query: bfloat16 [2560, 2560], P(None, 'tp')
- w_key: bfloat16 [2560, 640], P(None, 'tp')
- w_value: bfloat16 [2560, 640], P(None, 'tp'), may hold values from -0.125 to 0.125
- w_out: bfloat16 [2560, 2560], P('tp'), may hold values from -0.125 to 0.125
- prior_cache: bfloat16 [512, 8, 2, 80, 128], P('seq', 'tp'), may hold values from -6 to 6
- prior_lens: int32 [16, 16], P('seq'), may hold values from 1 to 256, 2048 in all within a row
- span_lens: int32 [16, 16], P('seq'), may hold values from 1 to 64, 512 in all within a row
- prior_table: int32 [16, 16, 2], P('seq'), may hold values from 0 to 31, as said below
- dest_device: int32 [16, 16], P('seq'), may hold values from 0 to 15, each once within a row
- dest_table: int32 [16, 16, 2], P('seq'), may hold values from 0 to 31, as said below
Outputs:
- hidden: bfloat16 [8192, 2560], P('seq', 'tp')
- decode_cache: bfloat16 [512, 8, 2, 80, 128], P('seq', 'tp')
Inputs may be any that keep to these rules, and one draw needn't show every extreme that they name: `prior_lens`: each row sums to 2048. `span_lens`: each row sums to 512. For each index s of seq, the entries prior_table[s] are a permutation of 0 to 31. `dest_device`: each row is a permutation of 0 to 15: every index of seq receives exactly one request from every index. For each receiving index d, the entries dest_table[d] are a permutation of 0 to 31.
All inputs are finite; a program needn't handle non-finite values.
Results may differ from a plain program's by a relative error of at most 0.0082.
Values may be sent and summed in bfloat16 or wider, within the bound.
No kernel may reach another device: no remote copies, remote signals or barrier semaphores. Data moves between devices by JAX's collectives and lax.ppermute only.
A program may use at most 128 MiB of HBM per device.

v0:
```python
import functools
import math

import jax
import jax.numpy as jnp
import numpy as np
from jax import lax
from jax.experimental import pallas as pl
from jax.experimental.pallas import tpu as pltpu
from jax.sharding import PartitionSpec as P

HEAD_DIM = 80
HALF = HEAD_DIM // 2
LANES = 128
WINDOW = 64
EPS = 1e-05
THETA = 1000000.0
MASKED = -1e30
ROWS = 32
NT = (((1,), (1,)), ((), ()))


def smem():
    return pl.BlockSpec(memory_space=pltpu.SMEM)


def vmem():
    return pl.BlockSpec(memory_space=pltpu.VMEM)


def hbm():
    return pl.BlockSpec(memory_space=pl.ANY)


def pack_body(dest_ref, lens_ref, table_ref, cache_ref, out_ref, buf, sem_in, sem_out):
    reqs = dest_ref.shape[1]
    per = table_ref.shape[2]
    block_len = cache_ref.shape[-1]

    def valid(r, j):
        return lens_ref[0, r] - j * block_len

    def fetch(r, j):
        return pltpu.make_async_copy(
            cache_ref.at[table_ref[0, r, j]], buf.at[r * per + j], sem_in.at[r * per + j]
        )

    def ship(r, j):
        return pltpu.make_async_copy(
            buf.at[r * per + j], out_ref.at[dest_ref[0, r], j], sem_out.at[r * per + j]
        )

    def start(r, carry):
        for j in range(per):
            @pl.when(valid(r, j) > 0)
            def _():
                fetch(r, j).start()
        return carry

    def finish(r, carry):
        for j in range(per):
            count = valid(r, j)

            @pl.when(count > 0)
            def _():
                fetch(r, j).wait()

            @pl.when(count < block_len)
            def _():
                block = buf[r * per + j]
                lane = lax.broadcasted_iota(jnp.int32, block.shape, block.ndim - 1)
                buf[r * per + j] = jnp.where(
                    (lane < count) & (count > 0), block.astype(jnp.float32), 0.0
                ).astype(jnp.bfloat16)

            ship(r, j).start()
        return carry

    def drain(r, carry):
        for j in range(per):
            ship(r, j).wait()
        return carry

    lax.fori_loop(0, reqs, start, 0)
    lax.fori_loop(0, reqs, finish, 0)
    lax.fori_loop(0, reqs, drain, 0)


def pack(dest, lens, table, cache):
    reqs, per = table.shape[1], table.shape[2]
    count = reqs * per
    return pl.pallas_call(
        pack_body,
        out_shape=jax.ShapeDtypeStruct((reqs, per) + cache.shape[1:], cache.dtype),
        in_specs=[smem(), smem(), smem(), hbm()],
        out_specs=hbm(),
        scratch_shapes=[
            pltpu.VMEM((count,) + cache.shape[1:], cache.dtype),
            pltpu.SemaphoreType.DMA((count,)),
            pltpu.SemaphoreType.DMA((count,)),
        ],
        compiler_params=pltpu.CompilerParams(vmem_limit_bytes=16 << 20),
        name="pack",
    )(dest, lens, table, cache)


def place_body(table_ref, in_ref, out_ref, sem):
    peers, per = table_ref.shape[1], table_ref.shape[2]

    def move(s, j):
        return pltpu.make_async_copy(
            in_ref.at[s, j], out_ref.at[table_ref[0, s, j]], sem.at[s * per + j]
        )

    def start(s, carry):
        for j in range(per):
            move(s, j).start()
        return carry

    def drain(s, carry):
        for j in range(per):
            move(s, j).wait()
        return carry

    lax.fori_loop(0, peers, start, 0)
    lax.fori_loop(0, peers, drain, 0)


def place(table, incoming):
    peers, per = incoming.shape[:2]
    return pl.pallas_call(
        place_body,
        out_shape=jax.ShapeDtypeStruct((peers * per,) + incoming.shape[2:], incoming.dtype),
        in_specs=[smem(), hbm()],
        out_specs=hbm(),
        scratch_shapes=[pltpu.SemaphoreType.DMA((peers * per,))],
        name="place",
    )(table, incoming)


def layer_body(ways, q_heads, kv_heads, *refs):
    (span_ref, lens_ref, table_ref, inv_ref) = refs[:4]
    gains = refs[4 : 4 + ways]
    xs = refs[4 + ways : 4 + 2 * ways]
    wq_ref, wk_ref, wv_ref, wo_ref, cache_ref = refs[4 + 2 * ways : 9 + 2 * ways]
    base_ref = refs[9 + 2 * ways]
    sends = refs[10 + 2 * ways : 9 + 3 * ways]
    (
        x_s, nrm_s, wq_s, wk_s, wv_s, wo_s, kv_s, acc_s, q_s, k_s, v_s, att_s, flat_s,
        cos_s, low_s, high_s, x_sem, w_sem, o_sem, kv_sem,
    ) = refs[9 + 3 * ways :]
    rows, feats = xs[0].shape
    reqs, per = table_ref.shape[1], table_ref.shape[2]
    block_len = cache_ref.shape[-1]
    group = q_heads // kv_heads
    me = lax.axis_index("tp")

    def x_copy(t):
        return pltpu.make_async_copy(xs[t], x_s.at[t], x_sem.at[t])

    w_copies = [
        pltpu.make_async_copy(wq_ref, wq_s, w_sem.at[0]),
        pltpu.make_async_copy(wk_ref, wk_s, w_sem.at[1]),
        pltpu.make_async_copy(wv_ref, wv_s, w_sem.at[2]),
    ]

    def o_copy(t):
        col = pl.multiple_of(lax.rem(me + t, ways) * feats, LANES)
        return pltpu.make_async_copy(wo_ref.at[:, pl.ds(col, feats)], wo_s.at[t], o_sem.at[t])

    def kv_copy(r, j):
        return pltpu.make_async_copy(
            cache_ref.at[table_ref[0, r, j]],
            kv_s.at[r, :, :, pl.ds(0, HEAD_DIM), pl.ds(j * block_len, block_len)],
            kv_sem.at[r * per + j],
        )

    for t in range(ways):
        x_copy(t).start()
    for copy in w_copies:
        copy.start()

    def kv_start(r, carry):
        for j in range(per):
            kv_copy(r, j).start()
        return carry

    lax.fori_loop(0, reqs, kv_start, 0)
    for t in range(ways):
        o_copy(t).start()

    row_id = lax.broadcasted_iota(jnp.int32, (rows, LANES), 0)

    def shift_of(r, carry):
        offset, shift = carry
        shift = jnp.where(row_id >= offset, lens_ref[0, r] - offset, shift)
        return offset + span_ref[0, r], shift

    _, shift = lax.fori_loop(0, reqs, shift_of, (jnp.int32(0), jnp.zeros_like(row_id)))
    angle = (row_id + shift).astype(jnp.float32) * inv_ref[...]
    lane = lax.broadcasted_iota(jnp.int32, (rows, LANES), 1)
    cos_s[...] = jnp.where(lane < HEAD_DIM, jnp.cos(angle), 0.0)
    sine = jnp.sin(angle)
    low_s[...] = jnp.where(lane < HALF, -sine, 0.0)
    high_s[...] = jnp.where((lane >= HALF) & (lane < HEAD_DIM), sine, 0.0)

    pad = kv_s.shape[3] - HEAD_DIM
    zeros_kv = jnp.zeros((2, pad, kv_s.shape[4]), kv_s.dtype)

    def kv_zero(r, carry):
        for g in range(kv_heads):
            kv_s[r, g, :, HEAD_DIM:, :] = zeros_kv
        return carry

    lax.fori_loop(0, reqs, kv_zero, 0)
    acc_s[...] = jnp.zeros(acc_s.shape, acc_s.dtype)
    att_s[...] = jnp.zeros(att_s.shape, att_s.dtype)

    for t in range(ways):
        x_copy(t).wait()
    step = 64

    def norm_rows(m, carry):
        here = pl.ds(pl.multiple_of(m * step, step), step)
        wide = [x_s[t, here, :].astype(jnp.float32) for t in range(ways)]
        total = sum(jnp.sum(w * w, axis=1, keepdims=True) for w in wide)
        scale = lax.rsqrt(total / (ways * feats) + EPS)
        for t in range(ways):
            nrm_s[lax.rem(me + t, ways), here, :] = (
                wide[t] * scale * gains[t][...].astype(jnp.float32)
            ).astype(jnp.bfloat16)
        return carry

    lax.fori_loop(0, rows // step, norm_rows, 0)

    tall = 256

    def project(w_s, first, width, here):
        total = None
        for c in range(ways):
            part = jnp.dot(
                nrm_s[c, here, :],
                w_s[c * feats : (c + 1) * feats, first : first + width],
                preferred_element_type=jnp.float32,
            )
            total = part if total is None else total + part
        acc_s[:, :width] = total

    def head_of(h):
        base = HEAD_DIM * h // LANES * LANES
        shift = HEAD_DIM * h - base
        wide = acc_s[:, base : base + 2 * LANES]
        if shift:
            wide = pltpu.roll(wide, 2 * LANES - shift, 1)
        return wide[:, :LANES]

    def rotated(h, here):
        value = head_of(h)
        return (
            value * cos_s[here, :]
            + pltpu.roll(value, LANES - HALF, 1) * low_s[here, :]
            + pltpu.roll(value, HALF, 1) * high_s[here, :]
        ).astype(jnp.bfloat16)

    for copy in w_copies:
        copy.wait()
    block_heads = min(8, q_heads)

    def project_rows(m, carry):
        here = pl.ds(pl.multiple_of(m * tall, tall), tall)
        project(wk_s, 0, kv_heads * HEAD_DIM, here)
        for g in range(kv_heads):
            k_s[g, here, :] = rotated(g, here)
        project(wv_s, 0, kv_heads * HEAD_DIM, here)
        narrow = lax.broadcasted_iota(jnp.int32, (tall, LANES), 1) < HEAD_DIM
        for g in range(kv_heads):
            v_s[g, here, :] = jnp.where(narrow, head_of(g), 0.0).astype(jnp.bfloat16)
        for block in range(q_heads // block_heads):
            project(wq_s, block * block_heads * HEAD_DIM, block_heads * HEAD_DIM, here)
            for h in range(block_heads):
                q_s[block * block_heads + h, here, :] = rotated(h, here)
        return carry

    lax.fori_loop(0, rows // tall, project_rows, 0)

    log_scale = (1.0 / math.sqrt(HEAD_DIM)) * math.log2(math.e)
    keys_old = per * block_len

    def request(r, offset):
        span = span_ref[0, r]
        prior = lens_ref[0, r]
        for j in range(per):
            kv_copy(r, j).wait()
        first = offset // 16 * 16
        key_first = pl.multiple_of(jnp.minimum(first, rows - LANES), 16)
        old_ok = lax.broadcasted_iota(jnp.int32, (1, keys_old), 1) < prior

        def tile(i, carry):
            begin = pl.multiple_of(first + i * ROWS, 16)
            here = pl.ds(begin, ROWS)
            row = begin + lax.broadcasted_iota(jnp.int32, (ROWS, LANES), 0)
            key = key_first + lax.broadcasted_iota(jnp.int32, (ROWS, LANES), 1)
            new_ok = ((key <= row) & (key >= offset))[None]
            keep = ((row >= offset) & (row < offset + span))[None]
            for g in range(kv_heads):
                heads = slice(g * group, (g + 1) * group)
                query = q_s[heads, here, :].reshape(group * ROWS, LANES)
                old = jnp.dot(query, kv_s[r, g, 0], preferred_element_type=jnp.float32)
                new = lax.dot_general(
                    query, k_s[g, pl.ds(key_first, LANES), :], NT,
                    preferred_element_type=jnp.float32,
                )
                old = jnp.where(old_ok, old, MASKED)
                new = jnp.where(new_ok, new.reshape(group, ROWS, LANES), MASKED)
                new = new.reshape(group * ROWS, LANES)
                top = jnp.maximum(
                    jnp.max(old, axis=1, keepdims=True), jnp.max(new, axis=1, keepdims=True)
                )
                old = jnp.exp2((old - top) * log_scale)
                new = jnp.exp2((new - top) * log_scale)
                total = jnp.sum(old, axis=1, keepdims=True) + jnp.sum(new, axis=1, keepdims=True)
                mixed = lax.dot_general(
                    old.astype(jnp.bfloat16), kv_s[r, g, 1], NT,
                    preferred_element_type=jnp.float32,
                ) + jnp.dot(
                    new.astype(jnp.bfloat16), v_s[g, pl.ds(key_first, LANES), :],
                    preferred_element_type=jnp.float32,
                )
                mixed = (mixed / total).reshape(group, ROWS, LANES)
                att_s[heads, here, :] = jnp.where(keep, mixed, att_s[heads, here, :])
            return carry

        lax.fori_loop(0, (offset - first + span + ROWS - 1) // ROWS, tile, 0)
        return offset + span

    lax.fori_loop(0, reqs, request, jnp.int32(0))

    for t in range(ways):
        o_copy(t).wait()

    def out_rows(m, carry):
        here = pl.ds(pl.multiple_of(m * tall, tall), tall)
        flat_s[...] = jnp.zeros(flat_s.shape, flat_s.dtype)
        for h in range(q_heads):
            base = HEAD_DIM * h // LANES * LANES
            shift = HEAD_DIM * h - base
            value = att_s[h, here, :]
            wide = jnp.concatenate([value, jnp.zeros_like(value)], axis=1)
            if shift:
                wide = pltpu.roll(wide, shift, 1)
            flat_s[:, base : base + 2 * LANES] += wide
        flat = flat_s[:, : q_heads * HEAD_DIM].astype(jnp.bfloat16)
        for t in range(ways):
            part = jnp.dot(flat, wo_s[t], preferred_element_type=jnp.float32)
            if t == 0:
                base_ref[here, :] = x_s[0, here, :].astype(jnp.float32) + part
            else:
                sends[t - 1][here, :] = part.astype(jnp.bfloat16)
        return carry

    lax.fori_loop(0, rows // tall, out_rows, 0)


def layer(ways, spans, lens, table, gains, xs, w_query, w_key, w_value, w_out, cache):
    rows, feats = xs[0].shape
    q_heads = w_query.shape[1] // HEAD_DIM
    kv_heads = w_key.shape[1] // HEAD_DIM
    reqs, per = table.shape[1], table.shape[2]
    keys = per * cache.shape[-1]
    pairs = np.arange(LANES) % HALF
    inverse = np.where(
        np.arange(LANES) < HEAD_DIM, np.float64(THETA) ** (-2.0 * pairs / HEAD_DIM), 0.0
    ).astype(np.float32)[None]
    bf, f32 = jnp.bfloat16, jnp.float32
    outs = pl.pallas_call(
        functools.partial(layer_body, ways, q_heads, kv_heads),
        out_shape=[jax.ShapeDtypeStruct((rows, feats), f32)]
        + [jax.ShapeDtypeStruct((rows, feats), bf)] * (ways - 1),
        in_specs=[smem(), smem(), smem(), vmem()] + [vmem()] * ways + [hbm()] * (ways + 5),
        out_specs=[vmem()] * ways,
        scratch_shapes=[
            pltpu.VMEM((ways, rows, feats), bf),
            pltpu.VMEM((ways, rows, feats), bf),
            pltpu.VMEM(w_query.shape, bf),
            pltpu.VMEM(w_key.shape, bf),
            pltpu.VMEM(w_value.shape, bf),
            pltpu.VMEM((ways, w_out.shape[0], feats), bf),
            pltpu.VMEM((reqs, kv_heads, 2, LANES, keys), bf),
            pltpu.VMEM((256, min(8, q_heads) * HEAD_DIM + LANES), f32),
            pltpu.VMEM((q_heads, rows + ROWS, LANES), bf),
            pltpu.VMEM((kv_heads, rows, LANES), bf),
            pltpu.VMEM((kv_heads, rows, LANES), bf),
            pltpu.VMEM((q_heads, rows + ROWS, LANES), f32),
            pltpu.VMEM((256, q_heads * HEAD_DIM + LANES), f32),
            pltpu.VMEM((rows, LANES), f32),
            pltpu.VMEM((rows, LANES), f32),
            pltpu.VMEM((rows, LANES), f32),
            pltpu.SemaphoreType.DMA((ways,)),
            pltpu.SemaphoreType.DMA((3,)),
            pltpu.SemaphoreType.DMA((ways,)),
            pltpu.SemaphoreType.DMA((reqs * per,)),
        ],
        compiler_params=pltpu.CompilerParams(vmem_limit_bytes=58 << 20),
        name="layer",
    )(spans, lens, table, jnp.asarray(inverse), *gains, *xs, w_query, w_key, w_value, w_out, cache)
    return outs[0], outs[1:]


def local(
    tokens,
    norm_gain,
    w_query,
    w_key,
    w_value,
    w_out,
    prior_cache,
    prior_lens,
    span_lens,
    prior_table,
    dest_device,
    dest_table,
):
    ways = lax.axis_size("tp")
    gain = norm_gain[None, :]

    def from_peer(value, t):
        return lax.ppermute(value, "tp", [((d + t) % ways, d) for d in range(ways)])

    def to_peer(value, t):
        return lax.ppermute(value, "tp", [(d, (d + t) % ways) for d in range(ways)])

    outgoing = pack(dest_device, prior_lens, prior_table, prior_cache)
    incoming = lax.all_to_all(outgoing, "seq", split_axis=0, concat_axis=0, tiled=True)
    xs = [tokens] + [from_peer(tokens, t) for t in range(1, ways)]
    gains = [gain] + [from_peer(gain, t) for t in range(1, ways)]
    base, sends = layer(
        ways, span_lens, prior_lens, prior_table, gains, xs,
        w_query, w_key, w_value, w_out, prior_cache,
    )
    total = base
    for t in range(1, ways):
        total = total + to_peer(sends[t - 1], t).astype(jnp.float32)
    hidden = total.astype(jnp.bfloat16)
    decode_cache = place(dest_table, incoming)
    return (hidden, decode_cache)


def solution(mesh):
    in_specs = (
        P("seq", "tp"),
        P("tp"),
        P(None, "tp"),
        P(None, "tp"),
        P(None, "tp"),
        P("tp", None),
        P("seq", "tp", None, None, None),
        P("seq", None),
        P("seq", None),
        P("seq", None, None),
        P("seq", None),
        P("seq", None, None),
    )
    out_specs = (P("seq", "tp"), P("seq", "tp", None, None, None))
    return jax.shard_map(local, mesh=mesh, in_specs=in_specs, out_specs=out_specs, check_vma=False)
```

profile of v0, /device:TPU:19, one launch (start us, length us, event | category | flops | bytes accessed | tf_op | source)
XLA Modules:
  0.0 309.8 jit_solution(16159693642263453895)
XLA Ops:
  0.6 0.8 copy.15.refs_2_.table_ref
  1.4 0.0 copy-start
  1.4 2.5 copy-done
  3.9 0.0 copy-start.3
  3.9 0.7 copy-done.3
  4.5 0.0 copy-start.4
  4.5 0.7 copy-done.4
  5.2 0.0 copy-start.2
  5.2 14.5 %pack.1 = bf16[16,2,4,2,80,128]{5,4,3,2,1,0:T(8,128)(2,1)S(1)} custom-call(s32[1,16]{1,0:T(1,128)S(1)} %copy-done.4, s32[1,16]{1,0:T(1,128)S(1)} %copy-done.3, s32[1,16,2]{2,1,0:T(8,128)S(1)} %copy.15.refs_2_.table_ref, bf16[32,4,2,80,128]{4,3,2,1,0:T(8,128)(2,1)S(1)} %copy-done), custom_call_target="tpu_custom_call" | custom-call | tf_op jit(solution)/shard_map/pack/pallas_call | solution.py:92
  19.7 0.0 copy-done.2
  19.7 0.0 copy-start.1
  19.7 2.3 copy-done.1
  22.0 0.0 copy-start.9
  22.0 0.0 copy-start.5
  22.0 6.6 %all-to-all-start = ((bf16[16,2,4,2,80,128]{5,4,3,2,1,0:T(8,128)(2,1)}), bf16[16,2,4,2,80,128]{5,4,3,2,1,0:T(8,128)(2,1)}, u32[]{:S(2)}, u32[]{:S(2)}) async-start(bf16[16,2,4,2,80,128]{5,4,3,2,1,0:T(8,128)(2,1)} %copy-done.1), calls=%async_computation | async-start | bytes 10485760 | tf_op jit(solution)/shard_map/all_to_all | solution.py:433
  28.6 0.0 copy-start.6
  28.6 1.3 collective-permute-start.1
  29.9 0.0 copy-done.9
  29.9 0.0 copy-start.7
  29.9 0.3 collective-permute-start
  30.2 0.0 copy-done.5
  30.2 2.4 copy.16.refs_9_
  32.7 0.0 copy-done.6
  32.7 2.4 copy.17.refs_10_
  35.1 0.0 copy-done.7
  35.1 0.0 copy-start.10
  35.1 24.0 %collective-permute-done.refs_5_ = bf16[1,1280]{1,0:T(2,128)(2,1)S(1)} collective-permute-done((bf16[1,1280]{1,0:T(2,128)(2,1)S(1)}, bf16[1,1280]{1,0:T(2,128)(2,1)S(1)}, u32[]{:S(2)}, u32[]{:S(2)}) %collective-permute-start) | collective-permute-done | bytes 2592 | tf_op jit(solution)/shard_map/ppermute | solution.py:427
  59.1 0.0 copy-start.8
  59.1 0.0 collective-permute-done.1.refs_7_
  59.1 0.6 copy-done.8
  59.7 56.6 %layer.1 = (f32[512,1280]{1,0:T(8,128)}, bf16[512,1280]{1,0:T(8,128)(2,1)}) custom-call(s32[1,16]{1,0:T(1,128)} %refs_0_.1, s32[1,16]{1,0:T(1,128)} %lens_ref.1, s32[1,16,2]{2,1,0:T(8,128)} %copy-done.2, f32[1,128]{1,0:T(1,128)} %constant.2.clone.refs_3_, bf16[1,1280]{1,0:T(2,128)(2,1)} %copy-done.7, bf16[1,1280]{1,0:T(2,128)(2,1)} %copy-done.8, ...), custom_call_target="tpu_custom_call" | custom-call | tf_op jit(solution)/shard_map/layer/pallas_call | solution.py:375
  116.3 1.3 collective-permute-start.2
  117.6 0.0 copy-done.10
  117.6 0.7 copy.19.table_ref
  118.3 27.4 %collective-permute-done.2 = bf16[512,1280]{1,0:T(8,128)(2,1)S(1)} collective-permute-done((bf16[512,1280]{1,0:T(8,128)(2,1)}, bf16[512,1280]{1,0:T(8,128)(2,1)S(1)}, u32[]{:S(2)}, u32[]{:S(2)}) %collective-permute-start.2) | collective-permute-done | bytes 1310752 | tf_op jit(solution)/shard_map/ppermute | solution.py:430
  145.8 3.1 add_convert_fusion
  148.8 0.0 all-to-all-done.in_ref
  148.8 161.0 %place.1 = bf16[32,4,2,80,128]{4,3,2,1,0:T(8,128)(2,1)} custom-call(s32[1,16,2]{2,1,0:T(8,128)} %copy.19.table_ref, bf16[16,2,4,2,80,128]{5,4,3,2,1,0:T(8,128)(2,1)} %all-to-all-done.in_ref), custom_call_target="tpu_custom_call" | custom-call | tf_op jit(solution)/shard_map/place/pallas_call | solution.py:131
  (1 shorter events, 0.0 us)
Async XLA Ops:
  1.4 2.5 copy-start
  3.9 0.7 copy-start.3
  4.5 0.7 copy-start.4
  5.2 14.5 %copy-start.2 = (s32[1,16,2]{2,1,0:T(8,128)}, s32[1,16,2]{2,1,0:T(8,128)S(1)}, u32[]{:S(2)}) copy-start(s32[1,16,2]{2,1,0:T(8,128)S(1)} %copy.15.refs_2_.table_ref) | copy-start | bytes 388
  19.7 2.4 copy-start.1
  22.0 7.9 %copy-start.9 = (bf16[1280]{0:T(1024)(128)(2,1)S(1)}, bf16[1280]{0:T(1024)(128)(2,1)}, u32[]{:S(2)}) copy-start(bf16[1280]{0:T(1024)(128)(2,1)} %param.14) | copy-start | bytes 7684
  22.0 8.2 %copy-start.5 = (bf16[2560,320]{0,1:T(8,128)(2,1)S(1)}, bf16[2560,320]{0,1:T(8,128)(2,1)}, u32[]{:S(2)}) copy-start(bf16[2560,320]{0,1:T(8,128)(2,1)} %param.16) | copy-start | bytes 4915204
  22.0 126.8 %all-to-all-start = ((bf16[16,2,4,2,80,128]{5,4,3,2,1,0:T(8,128)(2,1)}), bf16[16,2,4,2,80,128]{5,4,3,2,1,0:T(8,128)(2,1)}, u32[]{:S(2)}, u32[]{:S(2)}) async-start(bf16[16,2,4,2,80,128]{5,4,3,2,1,0:T(8,128)(2,1)} %copy-done.1), calls=%async_computation | async-start | bytes 10485760 | tf_op jit(solution)/shard_map/all_to_all | solution.py:433
  28.6 4.1 %copy-start.6 = (bf16[2560,320]{0,1:T(8,128)(2,1)S(1)}, bf16[2560,320]{0,1:T(8,128)(2,1)}, u32[]{:S(2)}) copy-start(bf16[2560,320]{0,1:T(8,128)(2,1)} %param.17) | copy-start | bytes 4915204
  28.6 30.5 %collective-permute-start.1 = (bf16[512,1280]{1,0:T(8,128)(2,1)}, bf16[512,1280]{1,0:T(8,128)(2,1)}, u32[]{:S(2)}, u32[]{:S(2)}) collective-permute-start(bf16[512,1280]{1,0:T(8,128)(2,1)} %refs_6_.1), channel_id=1, source_target_pairs={{1,0},{0,1},{3,2},{2,3},{5,4},{4,5},{7,6},{6,7},{9,8},{8,9},{11,10... | collective-permute-start | bytes 3932168 | tf_op jit(solution)/shard_map/ppermute | solution.py:427
  29.9 5.2 %copy-start.7 = (bf16[1,1280]{1,0:T(2,128)(2,1)}, bf16[1,1280]{1,0:T(2,128)(2,1)S(1)}, u32[]{:S(2)}) copy-start(bf16[1,1280]{1,0:T(2,128)(2,1)S(1)} %broadcast_in_dim.3.refs_4_) | copy-start | bytes 7684
  29.9 29.2 %collective-permute-start = (bf16[1,1280]{1,0:T(2,128)(2,1)S(1)}, bf16[1,1280]{1,0:T(2,128)(2,1)S(1)}, u32[]{:S(2)}, u32[]{:S(2)}) collective-permute-start(bf16[1,1280]{1,0:T(2,128)(2,1)S(1)} %broadcast_in_dim.3.refs_4_), channel_id=1, source_target_pairs={{1,0},{0,1},{3,2},{2,3},{5,4},{4,5},{7,6},{6,7},{9,8},{8,9},{11,10... | collective-permute-start | bytes 7688 | tf_op jit(solution)/shard_map/ppermute | solution.py:427
  35.1 82.5 %copy-start.10 = (s32[1,16,2]{1,2,0:T(2,128)S(1)}, s32[1,16,2]{1,2,0:T(2,128)}, u32[]{:S(2)}) copy-start(s32[1,16,2]{1,2,0:T(2,128)} %param.24) | copy-start | bytes 388
  59.1 0.6 copy-start.8
  116.3 29.4 %collective-permute-start.2 = (bf16[512,1280]{1,0:T(8,128)(2,1)}, bf16[512,1280]{1,0:T(8,128)(2,1)S(1)}, u32[]{:S(2)}, u32[]{:S(2)}) collective-permute-start(bf16[512,1280]{1,0:T(8,128)(2,1)} %get-tuple-element.5), channel_id=1, source_target_pairs={{0,1},{1,0},{2,3},{3,2},{4,5},{5,4},{6,7},{7,6},{8,9},{9,8},{10,11... | collective-permute-start | bytes 3932168 | tf_op jit(solution)/shard_map/ppermute | solution.py:430
where the time goes:
time: 312 us; the launch traced here: 310 us
  Pallas kernels  232 us (74%)
  waiting for transfers between devices  51.5 us (17%)
  local copies, waits for them, and re-layouts  13 us (4%)
  starting transfers between devices  9.47 us (3%)
    pallas_call x1, Pallas kernels, place(): pl.pallas_call(place_body, out_shape=jax.ShapeDtypeStruct((peers * per,)...  161 us
    pallas_call x1, Pallas kernels, layer(): pl.pallas_call(functools.partial(layer_body, ways, q_heads, kv_heads), ou...  56.6 us
    ppermute x1, waiting for transfers between devices, to_peer(): return lax.ppermute(value, 'tp', [(d, (d + t) % ways) for d in range(ways)])  27.4 us
    ppermute x2, waiting for transfers between devices, from_peer(): return lax.ppermute(value, 'tp', [((d + t) % ways, d) for d in range(ways)])  24 us
    pallas_call x1, Pallas kernels, pack(): pl.pallas_call(pack_body, out_shape=jax.ShapeDtypeStruct((reqs, per) + ca...  14.5 us
    unnamed x26, local copies, waits for them, and re-layouts  13 us
    all_to_all x1, starting transfers between devices, local(): lax.all_to_all(outgoing, 'seq', split_axis=0, concat_axis=0, tiled=True)  6.57 us
  transfers between devices with their start and end apart: 4, of which 2 were waited for; matrix products, arithmetic and copies ran while one was open for 3% of the time, Pallas kernels for 18%

commit v1 on v0

--- a/solution.py
+++ b/solution.py
@@ -34,7 +34,7 @@
 
 def pack_body(dest_ref, lens_ref, table_ref, cache_ref, out_ref, buf, sem_in, sem_out):
     reqs = dest_ref.shape[1]
-    per = table_ref.shape[2]
+    per = table_ref.shape[1]
     block_len = cache_ref.shape[-1]
 
     def valid(r, j):
@@ -42,7 +42,7 @@
 
     def fetch(r, j):
         return pltpu.make_async_copy(
-            cache_ref.at[table_ref[0, r, j]], buf.at[r * per + j], sem_in.at[r * per + j]
+            cache_ref.at[table_ref[0, j, r]], buf.at[r * per + j], sem_in.at[r * per + j]
         )
 
     def ship(r, j):
@@ -87,7 +87,7 @@
 
 
 def pack(dest, lens, table, cache):
-    reqs, per = table.shape[1], table.shape[2]
+    per, reqs = table.shape[1], table.shape[2]
     count = reqs * per
     return pl.pallas_call(
         pack_body,
@@ -99,41 +99,59 @@
             pltpu.SemaphoreType.DMA((count,)),
             pltpu.SemaphoreType.DMA((count,)),
         ],
-        compiler_params=pltpu.CompilerParams(vmem_limit_bytes=16 << 20),
+        compiler_params=pltpu.CompilerParams(vmem_limit_bytes=60 << 20),
         name="pack",
     )(dest, lens, table, cache)
 
 
-def place_body(table_ref, in_ref, out_ref, sem):
-    peers, per = table_ref.shape[1], table_ref.shape[2]
-
-    def move(s, j):
+def place_body(table_ref, in_ref, out_ref, buf, sem_in, sem_out):
+    per, peers = table_ref.shape[1], table_ref.shape[2]
+
+    def fetch(s, j):
         return pltpu.make_async_copy(
-            in_ref.at[s, j], out_ref.at[table_ref[0, s, j]], sem.at[s * per + j]
+            in_ref.at[s, j], buf.at[s * per + j], sem_in.at[s * per + j]
         )
 
+    def ship(s, j):
+        return pltpu.make_async_copy(
+            buf.at[s * per + j], out_ref.at[table_ref[0, j, s]], sem_out.at[s * per + j]
+        )
+
     def start(s, carry):
         for j in range(per):
-            move(s, j).start()
+            fetch(s, j).start()
+        return carry
+
+    def turn(s, carry):
+        for j in range(per):
+            fetch(s, j).wait()
+            ship(s, j).start()
         return carry
 
     def drain(s, carry):
         for j in range(per):
-            move(s, j).wait()
+            ship(s, j).wait()
         return carry
 
     lax.fori_loop(0, peers, start, 0)
+    lax.fori_loop(0, peers, turn, 0)
     lax.fori_loop(0, peers, drain, 0)
 
 
 def place(table, incoming):
     peers, per = incoming.shape[:2]
+    count = peers * per
     return pl.pallas_call(
         place_body,
-        out_shape=jax.ShapeDtypeStruct((peers * per,) + incoming.shape[2:], incoming.dtype),
+        out_shape=jax.ShapeDtypeStruct((count,) + incoming.shape[2:], incoming.dtype),
         in_specs=[smem(), hbm()],
         out_specs=hbm(),
-        scratch_shapes=[pltpu.SemaphoreType.DMA((peers * per,))],
+        scratch_shapes=[
+            pltpu.VMEM((count,) + incoming.shape[2:], incoming.dtype),
+            pltpu.SemaphoreType.DMA((count,)),
+            pltpu.SemaphoreType.DMA((count,)),
+        ],
+        compiler_params=pltpu.CompilerParams(vmem_limit_bytes=60 << 20),
         name="place",
     )(table, incoming)
 
@@ -150,7 +168,7 @@
         cos_s, low_s, high_s, x_sem, w_sem, o_sem, kv_sem,
     ) = refs[9 + 3 * ways :]
     rows, feats = xs[0].shape
-    reqs, per = table_ref.shape[1], table_ref.shape[2]
+    per, reqs = table_ref.shape[1], table_ref.shape[2]
     block_len = cache_ref.shape[-1]
     group = q_heads // kv_heads
     me = lax.axis_index("tp")
@@ -170,7 +188,7 @@
 
     def kv_copy(r, j):
         return pltpu.make_async_copy(
-            cache_ref.at[table_ref[0, r, j]],
+            cache_ref.at[table_ref[0, j, r]],
             kv_s.at[r, :, :, pl.ds(0, HEAD_DIM), pl.ds(j * block_len, block_len)],
             kv_sem.at[r * per + j],
         )
@@ -238,11 +256,16 @@
     def project(w_s, first, width, here):
         total = None
         for c in range(ways):
-            part = jnp.dot(
-                nrm_s[c, here, :],
-                w_s[c * feats : (c + 1) * feats, first : first + width],
-                preferred_element_type=jnp.float32,
-            )
+            deep = slice(c * feats, (c + 1) * feats)
+            if first is None:
+                part = lax.dot_general(
+                    nrm_s[c, here, :], w_s[:, deep], NT, preferred_element_type=jnp.float32
+                )
+            else:
+                part = jnp.dot(
+                    nrm_s[c, here, :], w_s[deep, first : first + width],
+                    preferred_element_type=jnp.float32,
+                )
             total = part if total is None else total + part
         acc_s[:, :width] = total
 
@@ -268,10 +291,10 @@
 
     def project_rows(m, carry):
         here = pl.ds(pl.multiple_of(m * tall, tall), tall)
-        project(wk_s, 0, kv_heads * HEAD_DIM, here)
+        project(wk_s, None, kv_heads * HEAD_DIM, here)
         for g in range(kv_heads):
             k_s[g, here, :] = rotated(g, here)
-        project(wv_s, 0, kv_heads * HEAD_DIM, here)
+        project(wv_s, None, kv_heads * HEAD_DIM, here)
         narrow = lax.broadcasted_iota(jnp.int32, (tall, LANES), 1) < HEAD_DIM
         for g in range(kv_heads):
             v_s[g, here, :] = jnp.where(narrow, head_of(g), 0.0).astype(jnp.bfloat16)
@@ -364,8 +387,8 @@
 def layer(ways, spans, lens, table, gains, xs, w_query, w_key, w_value, w_out, cache):
     rows, feats = xs[0].shape
     q_heads = w_query.shape[1] // HEAD_DIM
-    kv_heads = w_key.shape[1] // HEAD_DIM
-    reqs, per = table.shape[1], table.shape[2]
+    kv_heads = w_key.shape[0] // HEAD_DIM
+    per, reqs = table.shape[1], table.shape[2]
     keys = per * cache.shape[-1]
     pairs = np.arange(LANES) % HALF
     inverse = np.where(
@@ -400,7 +423,12 @@
             pltpu.SemaphoreType.DMA((ways,)),
             pltpu.SemaphoreType.DMA((reqs * per,)),
         ],
-        compiler_params=pltpu.CompilerParams(vmem_limit_bytes=58 << 20),
+        compiler_params=pltpu.CompilerParams(vmem_limit_bytes=60 << 20),
+        cost_estimate=pl.CostEstimate(
+            flops=100 * 2 * rows * ways * feats * 2 * w_query.shape[1],
+            transcendentals=0,
+            bytes_accessed=4 * w_query.size,
+        ),
         name="layer",
     )(spans, lens, table, jnp.asarray(inverse), *gains, *xs, w_query, w_key, w_value, w_out, cache)
     return outs[0], outs[1:]
@@ -422,6 +450,9 @@
 ):
     ways = lax.axis_size("tp")
     gain = norm_gain[None, :]
+    w_key, w_value = w_key.T, w_value.T
+    prior_table = prior_table.transpose(0, 2, 1)
+    dest_table = dest_table.transpose(0, 2, 1)
 
     def from_peer(value, t):
         return lax.ppermute(value, "tp", [((d + t) % ways, d) for d in range(ways)])

time: 312 us -> 136 us (0.44)
  Pallas kernels: 232 us -> 67.1 us
  local copies, waits for them, and re-layouts: 13 us -> 1.75 us
    pallas_call x1, Pallas kernels: 161 us -> 5.86 us  [place(): pl.pallas_call(place_body, out_shape=jax.ShapeDtypeStruct((count,) + inco...]
    unnamed x26 -> x6, local copies, waits for them, and re-layouts: 13 us -> 1.06 us
    pallas_call x1, Pallas kernels: 14.5 us -> 4.83 us  [pack(): pl.pallas_call(pack_body, out_shape=jax.ShapeDtypeStruct((reqs, per) + ca...]
    ppermute x2, waiting for transfers between devices: 24 us -> 15.8 us  [from_peer(): return lax.ppermute(value, 'tp', [((d + t) % ways, d) for d in range(ways)])]
    all_to_all x1, waiting for transfers between devices: 0.01 us -> 7.59 us  [local(): lax.all_to_all(outgoing, 'seq', split_axis=0, concat_axis=0, tiled=True)]
  transfers between devices with their start and end apart: 4 -> 4, of which waited for: 2 -> 3; matrix products, arithmetic and copies ran while one was open for 3% -> 3% of each run, Pallas kernels for 18% -> 46%
where the time goes in v1:
time: 136 us; the launch traced here: 134 us
  Pallas kernels  67.1 us (49%)
  waiting for transfers between devices  51 us (38%)
  starting transfers between devices  10.1 us (7%)
  other arithmetic  3.1 us (2%)
  local copies, waits for them, and re-layouts  1.75 us (1%)
    pallas_call x1, Pallas kernels, layer(): pl.pallas_call(functools.partial(layer_body, ways, q_heads, kv_heads), ou...  56.4 us
    ppermute x1, waiting for transfers between devices, to_peer(): return lax.ppermute(value, 'tp', [(d, (d + t) % ways) for d in range(ways)])  27.6 us
    ppermute x2, waiting for transfers between devices, from_peer(): return lax.ppermute(value, 'tp', [((d + t) % ways, d) for d in range(ways)])  15.8 us
    all_to_all x1, waiting for transfers between devices, local(): lax.all_to_all(outgoing, 'seq', split_axis=0, concat_axis=0, tiled=True)  7.59 us
    all_to_all x1, starting transfers between devices, local(): lax.all_to_all(outgoing, 'seq', split_axis=0, concat_axis=0, tiled=True)  7.25 us
    pallas_call x1, Pallas kernels, place(): pl.pallas_call(place_body, out_shape=jax.ShapeDtypeStruct((count,) + inco...  5.86 us
    pallas_call x1, Pallas kernels, pack(): pl.pallas_call(pack_body, out_shape=jax.ShapeDtypeStruct((reqs, per) + ca...  4.83 us
    convert_element_type x1, other arithmetic, local(): hidden = total.astype(jnp.bfloat16)  3.1 us
  transfers between devices with their start and end apart: 4, of which 3 were waited for; matrix products, arithmetic and copies ran while one was open for 3% of the time, Pallas kernels for 46%

profile of v1, /device:TPU:19, one launch (start us, length us, event | category | flops | bytes accessed | tf_op | source)
XLA Modules:
  0.0 133.7 jit_solution(10285372159623500853)
XLA Ops:
  0.6 1.3 collective-permute-start.1
  1.9 0.7 broadcast_in_dim.3.refs_4_
  2.6 0.0 copy-start
  2.6 0.2 collective-permute-start
  2.9 4.8 %pack.1 = bf16[16,2,4,2,80,128]{5,4,3,2,1,0:T(8,128)(2,1)} custom-call(s32[1,16]{1,0:T(1,128)} %dest_ref.1, s32[1,16]{1,0:T(1,128)} %lens_ref.1, s32[1,2,16]{2,1,0:T(2,128)} %bitcast.4, bf16[32,4,2,80,128]{4,3,2,1,0:T(8,128)(2,1)} %cache_ref.1), custom_call_target="tpu_custom_call" | custom-call | tf_op jit(solution)/shard_map/pack/pallas_call | solution.py:92
  7.7 0.0 copy-done
  7.7 7.3 %all-to-all-start = ((bf16[16,2,4,2,80,128]{5,4,3,2,1,0:T(8,128)(2,1)}), bf16[16,2,4,2,80,128]{5,4,3,2,1,0:T(8,128)(2,1)}, u32[]{:S(2)}, u32[]{:S(2)}) async-start(bf16[16,2,4,2,80,128]{5,4,3,2,1,0:T(8,128)(2,1)} %pack.1), calls=%async_computation | async-start | bytes 10485760 | tf_op jit(solution)/shard_map/all_to_all | solution.py:464
  15.0 15.8 %collective-permute-done.refs_5_ = bf16[1,1280]{1,0:T(2,128)(2,1)S(1)} collective-permute-done((bf16[1,1280]{1,0:T(2,128)(2,1)S(1)}, bf16[1,1280]{1,0:T(2,128)(2,1)S(1)}, u32[]{:S(2)}, u32[]{:S(2)}) %collective-permute-start) | collective-permute-done | bytes 2592 | tf_op jit(solution)/shard_map/ppermute | solution.py:458
  30.8 0.0 copy-start.2
  30.8 0.0 collective-permute-done.1.refs_7_
  30.8 0.0 copy-start.1
  30.8 0.6 copy-done.2
  31.4 0.5 copy-done.1
  31.8 56.4 %layer.1 = (f32[512,1280]{1,0:T(8,128)}, bf16[512,1280]{1,0:T(8,128)(2,1)}) custom-call(s32[1,16]{1,0:T(1,128)} %refs_0_.1, s32[1,16]{1,0:T(1,128)} %lens_ref.1, s32[1,2,16]{2,1,0:T(2,128)} %bitcast.5, f32[1,128]{1,0:T(1,128)} %constant.2.clone.refs_3_, bf16[1,1280]{1,0:T(2,128)(2,1)} %copy-done, bf16[1,1280]{1,0:T(2,128)(2,1)} %copy-done.2, ...), custom_call_target="tpu_custom_call" | custom-call | flops 671088640000 | bytes 13107200 | tf_op jit(solution)/shard_map/layer/pallas_call | solution.py:398
  88.2 1.3 collective-permute-start.2
  89.5 27.6 %collective-permute-done.2 = bf16[512,1280]{1,0:T(8,128)(2,1)S(1)} collective-permute-done((bf16[512,1280]{1,0:T(8,128)(2,1)}, bf16[512,1280]{1,0:T(8,128)(2,1)S(1)}, u32[]{:S(2)}, u32[]{:S(2)}) %collective-permute-start.2) | collective-permute-done | bytes 1310752 | tf_op jit(solution)/shard_map/ppermute | solution.py:461
  117.1 3.1 %add_convert_fusion = bf16[512,1280]{1,0:T(8,128)(2,1)} fusion(f32[512,1280]{1,0:T(8,128)} %get-tuple-element.4, bf16[512,1280]{1,0:T(8,128)(2,1)S(1)} %collective-permute-done.2), kind=kLoop, calls=%fused_computation | loop fusion | flops 1966080 | bytes 5242880 | tf_op jit(solution)/shard_map/convert_element_type | solution.py:474
  120.2 7.6 %all-to-all-done.in_ref = bf16[16,2,4,2,80,128]{5,4,3,2,1,0:T(8,128)(2,1)} async-done(((bf16[16,2,4,2,80,128]{5,4,3,2,1,0:T(8,128)(2,1)}), bf16[16,2,4,2,80,128]{5,4,3,2,1,0:T(8,128)(2,1)}, u32[]{:S(2)}, u32[]{:S(2)}) %all-to-all-start) | async-done | bytes 5242912 | tf_op jit(solution)/shard_map/all_to_all | solution.py:464
  127.8 5.9 %place.1 = bf16[32,4,2,80,128]{4,3,2,1,0:T(8,128)(2,1)} custom-call(s32[1,2,16]{2,1,0:T(2,128)} %bitcast.6, bf16[16,2,4,2,80,128]{5,4,3,2,1,0:T(8,128)(2,1)} %all-to-all-done.in_ref), custom_call_target="tpu_custom_call" | custom-call | tf_op jit(solution)/shard_map/place/pallas_call | solution.py:144
Async XLA Ops:
  0.6 30.1 %collective-permute-start.1 = (bf16[512,1280]{1,0:T(8,128)(2,1)}, bf16[512,1280]{1,0:T(8,128)(2,1)S(1)}, u32[]{:S(2)}, u32[]{:S(2)}) collective-permute-start(bf16[512,1280]{1,0:T(8,128)(2,1)} %refs_6_.1), channel_id=1, source_target_pairs={{1,0},{0,1},{3,2},{2,3},{5,4},{4,5},{7,6},{6,7},{9,8},{8,9},{11,10... | collective-permute-start | bytes 3932168 | tf_op jit(solution)/shard_map/ppermute | solution.py:458
  2.6 5.1 %copy-start = (bf16[1,1280]{1,0:T(2,128)(2,1)}, bf16[1,1280]{1,0:T(2,128)(2,1)S(1)}, u32[]{:S(2)}) copy-start(bf16[1,1280]{1,0:T(2,128)(2,1)S(1)} %broadcast_in_dim.3.refs_4_) | copy-start | bytes 7684
  2.6 28.1 %collective-permute-start = (bf16[1,1280]{1,0:T(2,128)(2,1)S(1)}, bf16[1,1280]{1,0:T(2,128)(2,1)S(1)}, u32[]{:S(2)}, u32[]{:S(2)}) collective-permute-start(bf16[1,1280]{1,0:T(2,128)(2,1)S(1)} %broadcast_in_dim.3.refs_4_), channel_id=1, source_target_pairs={{1,0},{0,1},{3,2},{2,3},{5,4},{4,5},{7,6},{6,7},{9,8},{8,9},{11,10... | collective-permute-start | bytes 7688 | tf_op jit(solution)/shard_map/ppermute | solution.py:458
  7.7 120.1 %all-to-all-start = ((bf16[16,2,4,2,80,128]{5,4,3,2,1,0:T(8,128)(2,1)}), bf16[16,2,4,2,80,128]{5,4,3,2,1,0:T(8,128)(2,1)}, u32[]{:S(2)}, u32[]{:S(2)}) async-start(bf16[16,2,4,2,80,128]{5,4,3,2,1,0:T(8,128)(2,1)} %pack.1), calls=%async_computation | async-start | bytes 10485760 | tf_op jit(solution)/shard_map/all_to_all | solution.py:464
  30.8 0.6 copy-start.2
  30.8 1.1 copy-start.1
  88.2 28.9 %collective-permute-start.2 = (bf16[512,1280]{1,0:T(8,128)(2,1)}, bf16[512,1280]{1,0:T(8,128)(2,1)S(1)}, u32[]{:S(2)}, u32[]{:S(2)}) collective-permute-start(bf16[512,1280]{1,0:T(8,128)(2,1)} %get-tuple-element.5), channel_id=1, source_target_pairs={{0,1},{1,0},{2,3},{3,2},{4,5},{5,4},{6,7},{7,6},{8,9},{9,8},{10,11... | collective-permute-start | bytes 3932168 | tf_op jit(solution)/shard_map/ppermute | solution.py:461

commit v2 on v1

--- a/solution.py
+++ b/solution.py
@@ -16,7 +16,9 @@
 EPS = 1e-05
 THETA = 1000000.0
 MASKED = -1e30
-ROWS = 32
+ROWS = 64
+SIDE_VMEM = 62 << 20
+LAYER_VMEM = 62 << 20
 NT = (((1,), (1,)), ((), ()))
 
 
@@ -32,128 +34,180 @@
     return pl.BlockSpec(memory_space=pl.ANY)
 
 
-def pack_body(dest_ref, lens_ref, table_ref, cache_ref, out_ref, buf, sem_in, sem_out):
+def pack_body(hops, dest_ref, lens_ref, table_ref, cache_ref, *refs):
+    outs = refs[: len(hops)]
+    inverse, buf, sem_in, sem_out = refs[-4:]
     reqs = dest_ref.shape[1]
     per = table_ref.shape[1]
     block_len = cache_ref.shape[-1]
-
-    def valid(r, j):
-        return lens_ref[0, r] - j * block_len
-
-    def fetch(r, j):
-        return pltpu.make_async_copy(
-            cache_ref.at[table_ref[0, j, r]], buf.at[r * per + j], sem_in.at[r * per + j]
-        )
-
-    def ship(r, j):
-        return pltpu.make_async_copy(
-            buf.at[r * per + j], out_ref.at[dest_ref[0, r], j], sem_out.at[r * per + j]
-        )
-
-    def start(r, carry):
-        for j in range(per):
-            @pl.when(valid(r, j) > 0)
-            def _():
-                fetch(r, j).start()
+    me = lax.axis_index("seq")
+
+    def invert(r, carry):
+        inverse[dest_ref[0, r]] = r
         return carry
 
-    def finish(r, carry):
-        for j in range(per):
-            count = valid(r, j)
-
-            @pl.when(count > 0)
-            def _():
-                fetch(r, j).wait()
-
-            @pl.when(count < block_len)
-            def _():
-                block = buf[r * per + j]
-                lane = lax.broadcasted_iota(jnp.int32, block.shape, block.ndim - 1)
-                buf[r * per + j] = jnp.where(
-                    (lane < count) & (count > 0), block.astype(jnp.float32), 0.0
-                ).astype(jnp.bfloat16)
-
-            ship(r, j).start()
-        return carry
-
-    def drain(r, carry):
-        for j in range(per):
-            ship(r, j).wait()
-        return carry
-
-    lax.fori_loop(0, reqs, start, 0)
-    lax.fori_loop(0, reqs, finish, 0)
-    lax.fori_loop(0, reqs, drain, 0)
-
-
-def pack(dest, lens, table, cache):
+    lax.fori_loop(0, reqs, invert, 0)
+    steps = []
+    for ref, group in zip(outs, hops):
+        for e, hop in enumerate(group):
+            for j in range(per):
+                steps.append((len(steps), ref, e, hop, j))
+
+    def count_of(hop, j):
+        return lens_ref[0, inverse[jnp.bitwise_xor(me, hop)]] - j * block_len
+
+    def fetch(i, hop, j):
+        row = table_ref[0, j, inverse[jnp.bitwise_xor(me, hop)]]
+        return pltpu.make_async_copy(cache_ref.at[row], buf.at[i], sem_in.at[i])
+
+    def ship(i, ref, e, j):
+        return pltpu.make_async_copy(buf.at[i], ref.at[e, j], sem_out.at[i])
+
+    for i, ref, e, hop, j in steps:
+        @pl.when(count_of(hop, j) > 0)
+        def _():
+            fetch(i, hop, j).start()
+
+    for i, ref, e, hop, j in steps:
+        count = count_of(hop, j)
+
+        @pl.when(count > 0)
+        def _():
+            fetch(i, hop, j).wait()
+
+        @pl.when(count < block_len)
+        def _():
+            block = buf[i]
+            lane = lax.broadcasted_iota(jnp.int32, block.shape, block.ndim - 1)
+            buf[i] = jnp.where(lane < count, block.astype(jnp.float32), 0.0).astype(jnp.bfloat16)
+
+        ship(i, ref, e, j).start()
+
+    for i, ref, e, hop, j in steps:
+        ship(i, ref, e, j).wait()
+
+
+def pack(hops, dest, lens, table, cache, after):
     per, reqs = table.shape[1], table.shape[2]
-    count = reqs * per
+    count = sum(len(group) for group in hops) * per
+    tail = cache.shape[1:]
+
+    def body(*refs):
+        pack_body(hops, *refs[:4], *refs[4 + len(after) :])
+
     return pl.pallas_call(
-        pack_body,
-        out_shape=jax.ShapeDtypeStruct((reqs, per) + cache.shape[1:], cache.dtype),
-        in_specs=[smem(), smem(), smem(), hbm()],
-        out_specs=hbm(),
+        body,
+        out_shape=[jax.ShapeDtypeStruct((len(group), per) + tail, cache.dtype) for group in hops],
+        in_specs=[smem(), smem(), smem(), hbm()] + [hbm()] * len(after),
+        out_specs=[hbm()] * len(hops),
         scratch_shapes=[
-            pltpu.VMEM((count,) + cache.shape[1:], cache.dtype),
+            pltpu.SMEM((reqs,), jnp.int32),
+            pltpu.VMEM((count,) + tail, cache.dtype),
             pltpu.SemaphoreType.DMA((count,)),
             pltpu.SemaphoreType.DMA((count,)),
         ],
-        compiler_params=pltpu.CompilerParams(vmem_limit_bytes=60 << 20),
+        compiler_params=pltpu.CompilerParams(vmem_limit_bytes=SIDE_VMEM),
         name="pack",
-    )(dest, lens, table, cache)
-
-
-def place_body(table_ref, in_ref, out_ref, buf, sem_in, sem_out):
-    per, peers = table_ref.shape[1], table_ref.shape[2]
-
-    def fetch(s, j):
-        return pltpu.make_async_copy(
-            in_ref.at[s, j], buf.at[s * per + j], sem_in.at[s * per + j]
-        )
-
-    def ship(s, j):
-        return pltpu.make_async_copy(
-            buf.at[s * per + j], out_ref.at[table_ref[0, j, s]], sem_out.at[s * per + j]
-        )
-
-    def start(s, carry):
-        for j in range(per):
-            fetch(s, j).start()
-        return carry
-
-    def turn(s, carry):
-        for j in range(per):
-            fetch(s, j).wait()
-            ship(s, j).start()
-        return carry
-
-    def drain(s, carry):
-        for j in range(per):
-            ship(s, j).wait()
-        return carry
-
-    lax.fori_loop(0, peers, start, 0)
-    lax.fori_loop(0, peers, turn, 0)
-    lax.fori_loop(0, peers, drain, 0)
-
-
-def place(table, incoming):
-    peers, per = incoming.shape[:2]
-    count = peers * per
+    )(dest, lens, table, cache, *after)
+
+
+def relay_body(*refs):
+    out_ref, buf, sem_in, sem_out = refs[-4:]
+    ins = refs[: out_ref.shape[0]]
+    for i, ref in enumerate(ins):
+        pltpu.make_async_copy(ref.at[ref.shape[0] - 1], buf.at[i], sem_in.at[i]).start()
+    for i, ref in enumerate(ins):
+        pltpu.make_async_copy(ref.at[ref.shape[0] - 1], buf.at[i], sem_in.at[i]).wait()
+        pltpu.make_async_copy(buf.at[i], out_ref.at[i], sem_out.at[i]).start()
+    for i, ref in enumerate(ins):
+        pltpu.make_async_copy(buf.at[i], out_ref.at[i], sem_out.at[i]).wait()
+
+
+def relay(arrays, after):
+    shape = (len(arrays),) + arrays[0].shape[1:]
     return pl.pallas_call(
-        place_body,
-        out_shape=jax.ShapeDtypeStruct((count,) + incoming.shape[2:], incoming.dtype),
-        in_specs=[smem(), hbm()],
+        relay_body,
+        out_shape=jax.ShapeDtypeStruct(shape, arrays[0].dtype),
+        in_specs=[hbm()] * (len(arrays) + len(after)),
         out_specs=hbm(),
         scratch_shapes=[
-            pltpu.VMEM((count,) + incoming.shape[2:], incoming.dtype),
+            pltpu.VMEM(shape, arrays[0].dtype),
+            pltpu.SemaphoreType.DMA((len(arrays),)),
+            pltpu.SemaphoreType.DMA((len(arrays),)),
+        ],
+        compiler_params=pltpu.CompilerParams(vmem_limit_bytes=SIDE_VMEM),
+        name="relay",
+    )(*arrays, *after)
+
+
+def place(table, arrays, sources, rows):
+    per = table.shape[1]
+    count = len(sources) * per
+    tail = arrays[0].shape[2:]
+    moves = [(which, e, hop, j) for which, e, hop in sources for j in range(per)]
+
+    def body(table_ref, *refs):
+        ins = refs[: len(arrays)]
+        out_ref, buf, sem_in, sem_out = refs[-4:]
+        me = lax.axis_index("seq")
+
+        def fetch(i, which, e, j):
+            return pltpu.make_async_copy(ins[which].at[e, j], buf.at[i], sem_in.at[i])
+
+        def ship(i, hop, j):
+            row = table_ref[0, j, jnp.bitwise_xor(me, hop)]
+            return pltpu.make_async_copy(buf.at[i], out_ref.at[row], sem_out.at[i])
+
+        for i, (which, e, hop, j) in enumerate(moves):
+            fetch(i, which, e, j).start()
+        for i, (which, e, hop, j) in enumerate(moves):
+            fetch(i, which, e, j).wait()
+            ship(i, hop, j).start()
+        for i, (which, e, hop, j) in enumerate(moves):
+            ship(i, hop, j).wait()
+
+    return pl.pallas_call(
+        body,
+        out_shape=jax.ShapeDtypeStruct((rows,) + tail, arrays[0].dtype),
+        in_specs=[smem()] + [hbm()] * len(arrays),
+        out_specs=hbm(),
+        scratch_shapes=[
+            pltpu.VMEM((count,) + tail, arrays[0].dtype),
             pltpu.SemaphoreType.DMA((count,)),
             pltpu.SemaphoreType.DMA((count,)),
         ],
-        compiler_params=pltpu.CompilerParams(vmem_limit_bytes=60 << 20),
+        compiler_params=pltpu.CompilerParams(vmem_limit_bytes=SIDE_VMEM),
         name="place",
-    )(table, incoming)
+    )(table, *arrays)
+
+
+def place_last(table, arrays, hops, made):
+    per = table.shape[1]
+    moves = [(which, hop, j) for which, hop in enumerate(hops) for j in range(per)]
+
+    def body(table_ref, *refs):
+        out_ref, sem = refs[-2:]
+        me = lax.axis_index("seq")
+
+        def ship(i, which, hop, j):
+            row = table_ref[0, j, jnp.bitwise_xor(me, hop)]
+            return pltpu.make_async_copy(refs[which].at[0, j], out_ref.at[row], sem.at[i])
+
+        for i, move in enumerate(moves):
+            ship(i, *move).start()
+        for i, move in enumerate(moves):
+            ship(i, *move).wait()
+
+    return pl.pallas_call(
+        body,
+        out_shape=jax.ShapeDtypeStruct(made.shape, made.dtype),
+        in_specs=[smem()] + [vmem()] * len(arrays) + [hbm()],
+        out_specs=hbm(),
+        scratch_shapes=[pltpu.SemaphoreType.DMA((len(moves),))],
+        input_output_aliases={1 + len(arrays): 0},
+        compiler_params=pltpu.CompilerParams(vmem_limit_bytes=4 << 20),
+        name="place_last",
+    )(table, *arrays, made)
 
 
 def layer_body(ways, q_heads, kv_heads, *refs):
@@ -232,7 +286,6 @@
 
     lax.fori_loop(0, reqs, kv_zero, 0)
     acc_s[...] = jnp.zeros(acc_s.shape, acc_s.dtype)
-    att_s[...] = jnp.zeros(att_s.shape, att_s.dtype)
 
     for t in range(ways):
         x_copy(t).wait()
@@ -325,6 +378,7 @@
             key = key_first + lax.broadcasted_iota(jnp.int32, (ROWS, LANES), 1)
             new_ok = ((key <= row) & (key >= offset))[None]
             keep = ((row >= offset) & (row < offset + span))[None]
+            scores = []
             for g in range(kv_heads):
                 heads = slice(g * group, (g + 1) * group)
                 query = q_s[heads, here, :].reshape(group * ROWS, LANES)
@@ -333,20 +387,26 @@
                     query, k_s[g, pl.ds(key_first, LANES), :], NT,
                     preferred_element_type=jnp.float32,
                 )
+                scores.append((old, new))
+            probs = []
+            for old, new in scores:
                 old = jnp.where(old_ok, old, MASKED)
                 new = jnp.where(new_ok, new.reshape(group, ROWS, LANES), MASKED)
                 new = new.reshape(group * ROWS, LANES)
-                top = jnp.maximum(
-                    jnp.max(old, axis=1, keepdims=True), jnp.max(new, axis=1, keepdims=True)
-                )
+                wide = jnp.maximum(jnp.maximum(old[:, :LANES], old[:, LANES:]), new)
+                top = jnp.max(wide, axis=1, keepdims=True)
                 old = jnp.exp2((old - top) * log_scale)
                 new = jnp.exp2((new - top) * log_scale)
-                total = jnp.sum(old, axis=1, keepdims=True) + jnp.sum(new, axis=1, keepdims=True)
+                wide = old[:, :LANES] + old[:, LANES:] + new
+                total = jnp.sum(wide, axis=1, keepdims=True)
+                probs.append((old.astype(jnp.bfloat16), new.astype(jnp.bfloat16), total))
+            for g in range(kv_heads):
+                heads = slice(g * group, (g + 1) * group)
+                old, new, total = probs[g]
                 mixed = lax.dot_general(
-                    old.astype(jnp.bfloat16), kv_s[r, g, 1], NT,
-                    preferred_element_type=jnp.float32,
+                    old, kv_s[r, g, 1], NT, preferred_element_type=jnp.float32,
                 ) + jnp.dot(
-                    new.astype(jnp.bfloat16), v_s[g, pl.ds(key_first, LANES), :],
+                    new, v_s[g, pl.ds(key_first, LANES), :],
                     preferred_element_type=jnp.float32,
                 )
                 mixed = (mixed / total).reshape(group, ROWS, LANES)
@@ -423,7 +483,7 @@
             pltpu.SemaphoreType.DMA((ways,)),
             pltpu.SemaphoreType.DMA((reqs * per,)),
         ],
-        compiler_params=pltpu.CompilerParams(vmem_limit_bytes=60 << 20),
+        compiler_params=pltpu.CompilerParams(vmem_limit_bytes=LAYER_VMEM),
         cost_estimate=pl.CostEstimate(
             flops=100 * 2 * rows * ways * feats * 2 * w_query.shape[1],
             transcendentals=0,
@@ -449,30 +509,66 @@
     dest_table,
 ):
     ways = lax.axis_size("tp")
-    gain = norm_gain[None, :]
     w_key, w_value = w_key.T, w_value.T
     prior_table = prior_table.transpose(0, 2, 1)
     dest_table = dest_table.transpose(0, 2, 1)
-
     def from_peer(value, t):
         return lax.ppermute(value, "tp", [((d + t) % ways, d) for d in range(ways)])
 
     def to_peer(value, t):
         return lax.ppermute(value, "tp", [(d, (d + t) % ways) for d in range(ways)])
 
-    outgoing = pack(dest_device, prior_lens, prior_table, prior_cache)
-    incoming = lax.all_to_all(outgoing, "seq", split_axis=0, concat_axis=0, tiled=True)
+    peers = lax.axis_size("seq")
+    pairs = peers // 2
+
+    def to_hop(value, hop):
+        return lax.ppermute(value, "seq", [(d, d ^ hop) for d in range(peers)])
+
+    barrier = lax.optimization_barrier
+    far = list(range(pairs // 2, pairs))
+    near = list(range(1, pairs // 2))
+    args = (dest_device, prior_lens, prior_table, prior_cache)
+    begin = [far[0]] + near[:-1]
+    middle = far[1:-2] + near[-1:]
+    direct = [2 * far[-1]]
+    late = [2 * far[-2], 2 * far[-2] + 1, 2 * far[-1] + 1]
+    pair = lambda k: (2 * k, 2 * k + 1)
     xs = [tokens] + [from_peer(tokens, t) for t in range(1, ways)]
+    begin_out = pack([pair(begin[0])], *args, [])
+    begin_out += pack([pair(k) for k in begin[1:]], *args, begin_out)
+    begin_in = [to_hop(value, 2 * k) for k, value in zip(begin, begin_out)]
+    hops = [pair(k) for k in middle] + [(hop,) for hop in direct + late] + [(0, 1)]
+    rest = pack(hops, *args, begin_out[-1:])
+    own = rest[-1]
+    gain = barrier((norm_gain, own))[0][None, :]
     gains = [gain] + [from_peer(gain, t) for t in range(1, ways)]
+
+    ended = begin_in[:1] + [xs[-1]] + begin_in[1:]
+    middle_in = []
+    for i, value in enumerate(rest[: len(middle) + 1]):
+        value = barrier((value, ended[i % len(ended)]))[0]
+        middle_in.append(to_hop(value, hops[i][0]))
+    xs, begin_in = barrier((xs, begin_in))
     base, sends = layer(
         ways, span_lens, prior_lens, prior_table, gains, xs,
         w_query, w_key, w_value, w_out, prior_cache,
     )
+    sends, middle_in, late_out = barrier((sends, middle_in, rest[len(middle) + 1 : -1]))
+    late_in = [to_hop(value, hop) for hop, value in zip(late, late_out)]
     total = base
     for t in range(1, ways):
         total = total + to_peer(sends[t - 1], t).astype(jnp.float32)
     hidden = total.astype(jnp.bfloat16)
-    decode_cache = place(dest_table, incoming)
+
+    arrived = begin_in + middle_in[:-1]
+    other = to_hop(relay(arrived + [own], [base]), 1)
+    rows = prior_cache.shape[0]
+    reach = [2 * k for k in begin + middle] + [0]
+    sources = [(i, 0, hop) for i, hop in enumerate(reach)]
+    sources += [(len(reach), i, hop + 1) for i, hop in enumerate(reach)]
+    sources += [(len(reach) + 1, 0, direct[0])]
+    made = place(dest_table, arrived + [own, other, middle_in[-1]], sources, rows)
+    decode_cache = place_last(dest_table, late_in, late, made)
     return (hidden, decode_cache)
 
 

time: 136 us -> 133 us (0.978)
  Pallas kernels: 67.1 us -> 55.5 us
  starting transfers between devices: 10.1 us -> 16.3 us
  waiting for transfers between devices: 51 us -> 53 us
    ppermute x0 -> x10, waiting for transfers between devices: none -> 30.9 us  [to_hop(): return lax.ppermute(value, 'seq', [(d, d ^ hop) for d in range(peers)])]
    pallas_call x1, Pallas kernels: 56.4 us -> 36.5 us  [layer(): pl.pallas_call(functools.partial(layer_body, ways, q_heads, kv_heads), ou...]
    ppermute x2, waiting for transfers between devices: 15.8 us -> 0.01 us  [from_peer(): return lax.ppermute(value, 'tp', [((d + t) % ways, d) for d in range(ways)])]
    ppermute x0 -> x10, starting transfers between devices: none -> 14.4 us  [to_hop(): return lax.ppermute(value, 'seq', [(d, d ^ hop) for d in range(peers)])]
    pallas_call x2 -> x6, Pallas kernels: 10.7 us -> 19 us  [the longest x3 9.63 us: pack(): pl.pallas_call(body, out_shape=[jax.ShapeDtypeStruct((len(group), per) +...]
    all_to_all x1 -> x0, waiting for transfers between devices: 7.59 us -> none  [local(): lax.all_to_all(outgoing, 'seq', split_axis=0, concat_axis=0, tiled=True)]
    all_to_all x1 -> x0, starting transfers between devices: 7.25 us -> none  [local(): lax.all_to_all(outgoing, 'seq', split_axis=0, concat_axis=0, tiled=True)]
    ppermute x1, waiting for transfers between devices: 27.6 us -> 22 us  [to_peer(): return lax.ppermute(value, 'tp', [(d, (d + t) % ways) for d in range(ways)])]
  transfers between devices with their start and end apart: 4 -> 13, of which waited for: 3 -> 5; matrix products, arithmetic and copies ran while one was open for 3% -> 3% of each run, Pallas kernels for 46% -> 41%
where the time goes in v2:
time: 133 us; the launch traced here: 131 us
  Pallas kernels  55.5 us (42%)
  waiting for transfers between devices  53 us (40%)
  starting transfers between devices  16.3 us (12%)
  other arithmetic  3.42 us (3%)
  local copies, waits for them, and re-layouts  2.02 us (2%)
    pallas_call x1, Pallas kernels, layer(): pl.pallas_call(functools.partial(layer_body, ways, q_heads, kv_heads), ou...  36.5 us
    ppermute x10, waiting for transfers between devices, to_hop(): return lax.ppermute(value, 'seq', [(d, d ^ hop) for d in range(peers)])  30.9 us
    ppermute x1, waiting for transfers between devices, to_peer(): return lax.ppermute(value, 'tp', [(d, (d + t) % ways) for d in range(ways)])  22 us
    ppermute x10, starting transfers between devices, to_hop(): return lax.ppermute(value, 'seq', [(d, d ^ hop) for d in range(peers)])  14.4 us
    pallas_call x3, Pallas kernels, pack(): pl.pallas_call(body, out_shape=[jax.ShapeDtypeStruct((len(group), per) +...  9.63 us
    pallas_call x1, Pallas kernels, place(): pl.pallas_call(body, out_shape=jax.ShapeDtypeStruct((rows,) + tail, array...  5.36 us
    convert_element_type x1, other arithmetic, local(): hidden = total.astype(jnp.bfloat16)  3.42 us
  transfers between devices with their start and end apart: 13, of which 5 were waited for; matrix products, arithmetic and copies ran while one was open for 3% of the time, Pallas kernels for 41%

profile of v2, /device:TPU:19, one launch (start us, length us, event | category | flops | bytes accessed | tf_op | source)
XLA Modules:
  0.0 131.0 jit_solution(14203778559173324000)
XLA Ops:
  0.6 1.3 collective-permute-start.1
  1.9 2.7 %pack.3.refs_4_ = bf16[2,2,4,2,80,128]{5,4,3,2,1,0:T(8,128)(2,1)} custom-call(s32[1,16]{1,0:T(1,128)} %refs_0_.6, s32[1,16]{1,0:T(1,128)} %refs_1_.7, s32[1,2,16]{2,1,0:T(2,128)} %bitcast.6, bf16[32,4,2,80,128]{4,3,2,1,0:T(8,128)(2,1)} %refs_12_.1), custom_call_target="tpu_custom_call" | custom-call | tf_op jit(solution)/shard_map/pack/pallas_call | solution.py:98
  4.7 0.2 collective-permute-start.2
  4.8 3.0 %pack.4 = (bf16[2,2,4,2,80,128]{5,4,3,2,1,0:T(8,128)(2,1)}, bf16[2,2,4,2,80,128]{5,4,3,2,1,0:T(8,128)(2,1)}) custom-call(s32[1,16]{1,0:T(1,128)} %refs_0_.6, s32[1,16]{1,0:T(1,128)} %refs_1_.7, s32[1,2,16]{2,1,0:T(2,128)} %bitcast.7, bf16[32,4,2,80,128]{4,3,2,1,0:T(8,128)(2,1)} %refs_12_.1, bf16[2,2,4,2,80,128]{5,4,3,2,1,0:T(8,128)(2,1)} %pack.3.refs_4_), custom_call_target="tpu_custom_call" | custom-call | tf_op jit(solution)/shard_map/pack/pallas_call | solution.py:98
  7.9 0.3 collective-permute-start.3
  8.2 0.0 copy-start.6
  8.2 1.2 collective-permute-start.4
  9.5 3.9 %pack.5 = (bf16[2,2,4,2,80,128]{5,4,3,2,1,0:T(8,128)(2,1)}, bf16[2,2,4,2,80,128]{5,4,3,2,1,0:T(8,128)(2,1)}, bf16[1,2,4,2,80,128]{5,4,3,2,1,0:T(8,128)(2,1)}, bf...) custom-call(s32[1,16]{1,0:T(1,128)} %refs_0_.6, ...), custom_call_target="tpu_custom_call" | custom-call | tf_op jit(solution)/shard_map/pack/pallas_call | solution.py:98
  13.3 0.0 copy-done.6
  13.4 0.0 copy-start.5
  13.4 0.3 collective-permute-start
  13.7 19.0 %collective-permute-done.2.refs_0_ = bf16[2,2,4,2,80,128]{5,4,3,2,1,0:T(8,128)(2,1)S(1)} collective-permute-done((bf16[2,2,4,2,80,128]{5,4,3,2,1,0:T(8,128)(2,1)}, bf16[2,2,4,2,80,128]{5,4,3,2,1,0:T(8,128)(2,1)S(1)}, u32[]{:S(2)}, u32[]{:S(2)}) %collective-permute-start.2) | collective-permute-done | bytes 655392 | tf_op jit(solution)/shard_map/ppermute | solution.py:525
  32.7 0.0 collective-permute-done.3.refs_1_
  32.7 3.3 %collective-permute-start.7 = (bf16[1,2,4,2,80,128]{5,4,3,2,1,0:T(8,128)(2,1)}, bf16[1,2,4,2,80,128]{5,4,3,2,1,0:T(8,128)(2,1)}, u32[]{:S(2)}, u32[]{:S(2)}) collective-permute-start(bf16[1,2,4,2,80,128]{5,4,3,2,1,0:T(8,128)(2,1)} %get-tuple-element.42), channel_id=1, source_target_pairs={{0,28},{2,30},{4,24},{6,26},{8,20},{10,22},{12,16},{14,18},{16,12}... | collective-permute-start | bytes 983048 | tf_op jit(solution)/shard_map/ppermute | solution.py:525
  35.9 4.9 %collective-permute-start.5 = (bf16[2,2,4,2,80,128]{5,4,3,2,1,0:T(8,128)(2,1)}, bf16[2,2,4,2,80,128]{5,4,3,2,1,0:T(8,128)(2,1)}, u32[]{:S(2)}, u32[]{:S(2)}) collective-permute-start(bf16[2,2,4,2,80,128]{5,4,3,2,1,0:T(8,128)(2,1)} %get-tuple-element.38), channel_id=1, source_target_pairs={{0,20},{2,22},{4,16},{6,18},{8,28},{10,30},{12,24},{14,26},{16,4},... | collective-permute-start | bytes 1966088 | tf_op jit(solution)/shard_map/ppermute | solution.py:525
  40.8 0.0 collective-permute-done.4.refs_2_
  40.8 0.0 collective-permute-done.1.refs_7_
  40.8 0.1 collective-permute-start.6
  40.9 0.0 collective-permute-done.refs_5_
  40.9 0.0 copy-start.10
  40.9 0.0 copy-done.5
  40.9 0.7 copy-done.10
  41.6 36.5 %layer.1 = (f32[512,1280]{1,0:T(8,128)}, bf16[512,1280]{1,0:T(8,128)(2,1)}) custom-call(s32[1,16]{1,0:T(1,128)} %refs_0_.7, s32[1,16]{1,0:T(1,128)} %refs_1_.7, s32[1,2,16]{2,1,0:T(2,128)} %bitcast.9, f32[1,128]{1,0:T(1,128)} %constant.2.clone.refs_3_, bf16[1,1280]{1,0:T(2,128)(2,1)} %copy-done.5, bf16[1,1280]{1,0:T(2,128)(2,1)} %copy-done.10, ...), custom_call_target="tpu_custom_call" | custom-call | flops 671088640000 | bytes 13107200 | tf_op jit(solution)/shard_map/layer/pallas_call | solution.py:458
  78.1 0.0 copy-done.1
  78.2 0.0 copy-done.2
  78.2 0.0 copy-done.3
  78.2 0.0 collective-permute-done.7.refs_7_
  78.2 2.4 %collective-permute-done.5.refs_3_ = bf16[2,2,4,2,80,128]{5,4,3,2,1,0:T(8,128)(2,1)} collective-permute-done((bf16[2,2,4,2,80,128]{5,4,3,2,1,0:T(8,128)(2,1)}, bf16[2,2,4,2,80,128]{5,4,3,2,1,0:T(8,128)(2,1)}, u32[]{:S(2)}, u32[]{:S(2)}) %collective-permute-start.5) | collective-permute-done | bytes 655392 | tf_op jit(solution)/shard_map/ppermute | solution.py:525
  80.5 0.0 collective-permute-done.6.refs_4_
  80.5 0.3 collective-permute-start.8
  80.8 2.5 %relay.1 = bf16[6,2,4,2,80,128]{5,4,3,2,1,0:T(8,128)(2,1)} custom-call(bf16[2,2,4,2,80,128]{5,4,3,2,1,0:T(8,128)(2,1)} %copy-done.1, bf16[2,2,4,2,80,128]{5,4,3,2,1,0:T(8,128)(2,1)} %copy-done.2, bf16[2,2,4,2,80,128]{5,4,3,2,1,0:T(8,128)(2,1)} %copy-done.3, bf16[2,2,4,2,80,128]{5,4,3,2,1,0:T(8,128)(2,1)} %collective-permute-done.5.refs_3_, ...), custom_call_target="tpu_custom_call" | custom-call | tf_op jit(solution)/shard_map/relay/pallas_call | solution.py:128
  83.3 1.7 %collective-permute-start.12 = (bf16[6,2,4,2,80,128]{5,4,3,2,1,0:T(8,128)(2,1)}, bf16[6,2,4,2,80,128]{5,4,3,2,1,0:T(8,128)(2,1)S(1)}, u32[]{:S(2)}, u32[]{:S(2)}) collective-permute-start(bf16[6,2,4,2,80,128]{5,4,3,2,1,0:T(8,128)(2,1)} %relay.1), channel_id=1, source_target_pairs={{0,2},{2,0},{4,6},{6,4},{8,10},{10,8},{12,14},{14,12},{16,18},{18,... | collective-permute-start | bytes 5898248 | tf_op jit(solution)/shard_map/ppermute | solution.py:525
  85.0 0.0 copy-done.9
  85.0 1.1 collective-permute-start.9
  86.1 0.0 copy-done.8
  86.1 0.6 collective-permute-start.10
  86.7 0.0 copy-done.7
  86.7 1.1 collective-permute-start.11
  87.8 22.0 %collective-permute-done.8 = bf16[512,1280]{1,0:T(8,128)(2,1)} collective-permute-done((bf16[512,1280]{1,0:T(8,128)(2,1)}, bf16[512,1280]{1,0:T(8,128)(2,1)}, u32[]{:S(2)}, u32[]{:S(2)}) %collective-permute-start.8) | collective-permute-done | bytes 1310752 | tf_op jit(solution)/shard_map/ppermute | solution.py:519
  109.8 3.4 %add_convert_fusion = bf16[512,1280]{1,0:T(8,128)(2,1)} fusion(f32[512,1280]{1,0:T(8,128)} %get-tuple-element.35.refs_6_, bf16[512,1280]{1,0:T(8,128)(2,1)} %collective-permute-done.8), kind=kLoop, calls=%fused_computation | loop fusion | flops 1966080 | bytes 5242880 | tf_op jit(solution)/shard_map/convert_element_type | solution.py:561
  113.2 0.0 collective-permute-done.12.refs_6_
  113.2 1.3 copy-done.4
  114.5 5.4 %place.1.refs_3_ = bf16[32,4,2,80,128]{4,3,2,1,0:T(8,128)(2,1)} custom-call(s32[1,2,16]{2,1,0:T(2,128)} %bitcast.4, bf16[2,2,4,2,80,128]{5,4,3,2,1,0:T(8,128)(2,1)} %copy-done.1, bf16[2,2,4,2,80,128]{5,4,3,2,1,0:T(8,128)(2,1)} %copy-done.2, bf16[2,2,4,2,80,128]{5,4,3,2,1,0:T(8,128)(2,1)} %copy-done.3, ...), custom_call_target="tpu_custom_call" | custom-call | tf_op jit(solution)/shard_map/place/pallas_call | solution.py:169
  119.9 0.0 collective-permute-done.9.refs_0_
  119.9 3.4 %collective-permute-done.10.refs_1_ = bf16[1,2,4,2,80,128]{5,4,3,2,1,0:T(8,128)(2,1)S(1)} collective-permute-done((bf16[1,2,4,2,80,128]{5,4,3,2,1,0:T(8,128)(2,1)S(1)}, bf16[1,2,4,2,80,128]{5,4,3,2,1,0:T(8,128)(2,1)S(1)}, u32[]{:S(2)}, u32[]{:S(2)}) %collective-permute-start.10) | collective-permute-done | bytes 327712 | tf_op jit(solution)/shard_map/ppermute | solution.py:525
  123.3 6.2 %collective-permute-done.11.refs_2_ = bf16[1,2,4,2,80,128]{5,4,3,2,1,0:T(8,128)(2,1)S(1)} collective-permute-done((bf16[1,2,4,2,80,128]{5,4,3,2,1,0:T(8,128)(2,1)S(1)}, bf16[1,2,4,2,80,128]{5,4,3,2,1,0:T(8,128)(2,1)S(1)}, u32[]{:S(2)}, u32[]{:S(2)}) %collective-permute-start.11) | collective-permute-done | bytes 327712 | tf_op jit(solution)/shard_map/ppermute | solution.py:525
  129.4 0.0 copy-done
  129.4 1.6 %place_last.1 = bf16[32,4,2,80,128]{4,3,2,1,0:T(8,128)(2,1)} custom-call(s32[1,2,16]{2,1,0:T(2,128)S(1)} %bitcast.5, bf16[1,2,4,2,80,128]{5,4,3,2,1,0:T(8,128)(2,1)S(1)} %collective-permute-done.9.refs_0_, bf16[1,2,4,2,80,128]{5,4,3,2,1,0:T(8,128)(2,1)S(1)} %collective-permute-done.10.refs_1_, ...), custom_call_target="tpu_custom_call", output_to_operand_aliasing={{}: (4, {})} | custom-call | tf_op jit(solution)/shard_map/place_last/pallas_call | solution.py:201
  (9 shorter events, 0.0 us)
Async XLA Ops:
  0.6 40.2 %collective-permute-start.1 = (bf16[512,1280]{1,0:T(8,128)(2,1)}, bf16[512,1280]{1,0:T(8,128)(2,1)}, u32[]{:S(2)}, u32[]{:S(2)}) collective-permute-start(bf16[512,1280]{1,0:T(8,128)(2,1)} %refs_6_), channel_id=1, source_target_pairs={{1,0},{0,1},{3,2},{2,3},{5,4},{4,5},{7,6},{6,7},{9,8},{8,9},{11,10... | collective-permute-start | bytes 3932168 | tf_op jit(solution)/shard_map/ppermute | solution.py:516
  4.7 28.0 %collective-permute-start.2 = (bf16[2,2,4,2,80,128]{5,4,3,2,1,0:T(8,128)(2,1)}, bf16[2,2,4,2,80,128]{5,4,3,2,1,0:T(8,128)(2,1)S(1)}, u32[]{:S(2)}, u32[]{:S(2)}) collective-permute-start(bf16[2,2,4,2,80,128]{5,4,3,2,1,0:T(8,128)(2,1)} %pack.3.refs_4_), channel_id=1, source_target_pairs={{0,16},{2,18},{4,20},{6,22},{8,24},{10,26},{12,28},{14,30},{16,0},... | collective-permute-start | bytes 1966088 | tf_op jit(solution)/shard_map/ppermute | solution.py:525
  7.9 24.8 %collective-permute-start.3 = (bf16[2,2,4,2,80,128]{5,4,3,2,1,0:T(8,128)(2,1)}, bf16[2,2,4,2,80,128]{5,4,3,2,1,0:T(8,128)(2,1)S(1)}, u32[]{:S(2)}, u32[]{:S(2)}) collective-permute-start(bf16[2,2,4,2,80,128]{5,4,3,2,1,0:T(8,128)(2,1)} %get-tuple-element.32), channel_id=1, source_target_pairs={{0,4},{2,6},{4,0},{6,2},{8,12},{10,14},{12,8},{14,10},{16,20},{18,... | collective-permute-start | bytes 1966088 | tf_op jit(solution)/shard_map/ppermute | solution.py:525
  8.2 5.1 %copy-start.6 = (bf16[1280]{0:T(1024)(128)(2,1)S(1)}, bf16[1280]{0:T(1024)(128)(2,1)}, u32[]{:S(2)}) copy-start(bf16[1280]{0:T(1024)(128)(2,1)} %param.14) | copy-start | bytes 7684
  8.2 32.6 %collective-permute-start.4 = (bf16[2,2,4,2,80,128]{5,4,3,2,1,0:T(8,128)(2,1)}, bf16[2,2,4,2,80,128]{5,4,3,2,1,0:T(8,128)(2,1)S(1)}, u32[]{:S(2)}, u32[]{:S(2)}) collective-permute-start(bf16[2,2,4,2,80,128]{5,4,3,2,1,0:T(8,128)(2,1)} %get-tuple-element.29.refs_4_), channel_id=1, source_target_pairs={{0,8},{2,10},{4,12},{6,14},{8,0},{10,2},{12,4},{14,6},{16,24},{18,... | collective-permute-start | bytes 1966088 | tf_op jit(solution)/shard_map/ppermute | solution.py:525
  13.4 27.6 %copy-start.5 = (bf16[1,1280]{1,0:T(2,128)(2,1)}, bf16[1,1280]{1,0:T(2,128)(2,1)S(1)}, u32[]{:S(2)}) copy-start(bf16[1,1280]{1,0:T(2,128)(2,1)S(1)} %broadcast_in_dim.3.refs_4_) | copy-start | bytes 7684
  13.4 27.5 %collective-permute-start = (bf16[1,1280]{1,0:T(2,128)(2,1)S(1)}, bf16[1,1280]{1,0:T(2,128)(2,1)S(1)}, u32[]{:S(2)}, u32[]{:S(2)}) collective-permute-start(bf16[1,1280]{1,0:T(2,128)(2,1)S(1)} %broadcast_in_dim.3.refs_4_), channel_id=1, source_target_pairs={{1,0},{0,1},{3,2},{2,3},{5,4},{4,5},{7,6},{6,7},{9,8},{8,9},{11,10... | collective-permute-start | bytes 7688 | tf_op jit(solution)/shard_map/ppermute | solution.py:516
  32.7 45.5 %copy-start.1 = (bf16[2,2,4,2,80,128]{5,4,3,2,1,0:T(8,128)(2,1)}, bf16[2,2,4,2,80,128]{5,4,3,2,1,0:T(8,128)(2,1)S(1)}, u32[]{:S(2)}) copy-start(bf16[2,2,4,2,80,128]{5,4,3,2,1,0:T(8,128)(2,1)S(1)} %collective-permute-done.2.refs_0_) | copy-start | bytes 1966084
  32.7 45.5 %copy-start.2 = (bf16[2,2,4,2,80,128]{5,4,3,2,1,0:T(8,128)(2,1)}, bf16[2,2,4,2,80,128]{5,4,3,2,1,0:T(8,128)(2,1)S(1)}, u32[]{:S(2)}) copy-start(bf16[2,2,4,2,80,128]{5,4,3,2,1,0:T(8,128)(2,1)S(1)} %collective-permute-done.3.refs_1_) | copy-start | bytes 1966084
  32.7 45.5 %collective-permute-start.7 = (bf16[1,2,4,2,80,128]{5,4,3,2,1,0:T(8,128)(2,1)}, bf16[1,2,4,2,80,128]{5,4,3,2,1,0:T(8,128)(2,1)}, u32[]{:S(2)}, u32[]{:S(2)}) collective-permute-start(bf16[1,2,4,2,80,128]{5,4,3,2,1,0:T(8,128)(2,1)} %get-tuple-element.42), channel_id=1, source_target_pairs={{0,28},{2,30},{4,24},{6,26},{8,20},{10,22},{12,16},{14,18},{16,12}... | collective-permute-start | bytes 983048 | tf_op jit(solution)/shard_map/ppermute | solution.py:525
  35.9 44.6 %collective-permute-start.5 = (bf16[2,2,4,2,80,128]{5,4,3,2,1,0:T(8,128)(2,1)}, bf16[2,2,4,2,80,128]{5,4,3,2,1,0:T(8,128)(2,1)}, u32[]{:S(2)}, u32[]{:S(2)}) collective-permute-start(bf16[2,2,4,2,80,128]{5,4,3,2,1,0:T(8,128)(2,1)} %get-tuple-element.38), channel_id=1, source_target_pairs={{0,20},{2,22},{4,16},{6,18},{8,28},{10,30},{12,24},{14,26},{16,4},... | collective-permute-start | bytes 1966088 | tf_op jit(solution)/shard_map/ppermute | solution.py:525
  40.8 37.4 %copy-start.3 = (bf16[2,2,4,2,80,128]{5,4,3,2,1,0:T(8,128)(2,1)}, bf16[2,2,4,2,80,128]{5,4,3,2,1,0:T(8,128)(2,1)S(1)}, u32[]{:S(2)}) copy-start(bf16[2,2,4,2,80,128]{5,4,3,2,1,0:T(8,128)(2,1)S(1)} %collective-permute-done.4.refs_2_) | copy-start | bytes 1966084
  40.8 39.7 %collective-permute-start.6 = (bf16[2,2,4,2,80,128]{5,4,3,2,1,0:T(8,128)(2,1)}, bf16[2,2,4,2,80,128]{5,4,3,2,1,0:T(8,128)(2,1)}, u32[]{:S(2)}, u32[]{:S(2)}) collective-permute-start(bf16[2,2,4,2,80,128]{5,4,3,2,1,0:T(8,128)(2,1)} %get-tuple-element.40), channel_id=1, source_target_pairs={{0,12},{2,14},{4,8},{6,10},{8,4},{10,6},{12,0},{14,2},{16,28},{18,... | collective-permute-start | bytes 1966088 | tf_op jit(solution)/shard_map/ppermute | solution.py:525
  40.9 0.7 copy-start.10
  80.5 29.2 %collective-permute-start.8 = (bf16[512,1280]{1,0:T(8,128)(2,1)}, bf16[512,1280]{1,0:T(8,128)(2,1)}, u32[]{:S(2)}, u32[]{:S(2)}) collective-permute-start(bf16[512,1280]{1,0:T(8,128)(2,1)} %get-tuple-element.46), channel_id=1, source_target_pairs={{0,1},{1,0},{2,3},{3,2},{4,5},{5,4},{6,7},{7,6},{8,9},{9,8},{10,11... | collective-permute-start | bytes 3932168 | tf_op jit(solution)/shard_map/ppermute | solution.py:519
  80.8 4.2 %copy-start.9 = (bf16[1,2,4,2,80,128]{5,4,3,2,1,0:T(8,128)(2,1)S(1)}, bf16[1,2,4,2,80,128]{5,4,3,2,1,0:T(8,128)(2,1)}, u32[]{:S(2)}) copy-start(bf16[1,2,4,2,80,128]{5,4,3,2,1,0:T(8,128)(2,1)} %get-tuple-element.47) | copy-start | bytes 983044
  80.8 5.3 %copy-start.8 = (bf16[1,2,4,2,80,128]{5,4,3,2,1,0:T(8,128)(2,1)S(1)}, bf16[1,2,4,2,80,128]{5,4,3,2,1,0:T(8,128)(2,1)}, u32[]{:S(2)}) copy-start(bf16[1,2,4,2,80,128]{5,4,3,2,1,0:T(8,128)(2,1)} %get-tuple-element.48) | copy-start | bytes 983044
  80.8 5.9 %copy-start.7 = (bf16[1,2,4,2,80,128]{5,4,3,2,1,0:T(8,128)(2,1)S(1)}, bf16[1,2,4,2,80,128]{5,4,3,2,1,0:T(8,128)(2,1)}, u32[]{:S(2)}) copy-start(bf16[1,2,4,2,80,128]{5,4,3,2,1,0:T(8,128)(2,1)} %get-tuple-element.49) | copy-start | bytes 983044
  83.3 29.9 %collective-permute-start.12 = (bf16[6,2,4,2,80,128]{5,4,3,2,1,0:T(8,128)(2,1)}, bf16[6,2,4,2,80,128]{5,4,3,2,1,0:T(8,128)(2,1)S(1)}, u32[]{:S(2)}, u32[]{:S(2)}) collective-permute-start(bf16[6,2,4,2,80,128]{5,4,3,2,1,0:T(8,128)(2,1)} %relay.1), channel_id=1, source_target_pairs={{0,2},{2,0},{4,6},{6,4},{8,10},{10,8},{12,14},{14,12},{16,18},{18,... | collective-permute-start | bytes 5898248 | tf_op jit(solution)/shard_map/ppermute | solution.py:525
  85.0 34.9 %collective-permute-start.9 = (bf16[1,2,4,2,80,128]{5,4,3,2,1,0:T(8,128)(2,1)S(1)}, bf16[1,2,4,2,80,128]{5,4,3,2,1,0:T(8,128)(2,1)S(1)}, u32[]{:S(2)}, u32[]{:S(2)}) collective-permute-start(bf16[1,2,4,2,80,128]{5,4,3,2,1,0:T(8,128)(2,1)S(1)} %copy-done.9), channel_id=1, source_target_pairs={{0,24},{2,26},{4,28},{6,30},{8,16},{10,18},{12,20},{14,22},{16,8},... | collective-permute-start | bytes 983048 | tf_op jit(solution)/shard_map/ppermute | solution.py:525
  86.1 37.2 %collective-permute-start.10 = (bf16[1,2,4,2,80,128]{5,4,3,2,1,0:T(8,128)(2,1)S(1)}, bf16[1,2,4,2,80,128]{5,4,3,2,1,0:T(8,128)(2,1)S(1)}, u32[]{:S(2)}, u32[]{:S(2)}) collective-permute-start(bf16[1,2,4,2,80,128]{5,4,3,2,1,0:T(8,128)(2,1)S(1)} %copy-done.8), channel_id=1, source_target_pairs={{0,26},{2,24},{4,30},{6,28},{8,18},{10,16},{12,22},{14,20},{16,10}... | collective-permute-start | bytes 983048 | tf_op jit(solution)/shard_map/ppermute | solution.py:525
  86.7 42.8 %collective-permute-start.11 = (bf16[1,2,4,2,80,128]{5,4,3,2,1,0:T(8,128)(2,1)S(1)}, bf16[1,2,4,2,80,128]{5,4,3,2,1,0:T(8,128)(2,1)S(1)}, u32[]{:S(2)}, u32[]{:S(2)}) collective-permute-start(bf16[1,2,4,2,80,128]{5,4,3,2,1,0:T(8,128)(2,1)S(1)} %copy-done.7), channel_id=1, source_target_pairs={{0,30},{2,28},{4,26},{6,24},{8,22},{10,20},{12,18},{14,16},{16,14}... | collective-permute-start | bytes 983048 | tf_op jit(solution)/shard_map/ppermute | solution.py:525
  113.2 1.3 copy-start.4
  114.5 14.9 %copy-start = (s32[1,16,2]{1,2,0:T(2,128)S(1)}, s32[1,16,2]{1,2,0:T(2,128)}, u32[]{:S(2)}) copy-start(s32[1,16,2]{1,2,0:T(2,128)} %param.24) | copy-start | bytes 388

commit v3 on v2

--- a/solution.py
+++ b/solution.py
@@ -17,6 +17,7 @@
 THETA = 1000000.0
 MASKED = -1e30
 ROWS = 64
+BY_PERMUTE = 1
 SIDE_VMEM = 62 << 20
 LAYER_VMEM = 62 << 20
 NT = (((1,), (1,)), ((), ()))
@@ -34,13 +35,14 @@
     return pl.BlockSpec(memory_space=pl.ANY)
 
 
-def pack_body(hops, dest_ref, lens_ref, table_ref, cache_ref, *refs):
+def pack_body(hops, first, absolute, dest_ref, lens_ref, table_ref, cache_ref, *refs):
     outs = refs[: len(hops)]
     inverse, buf, sem_in, sem_out = refs[-4:]
     reqs = dest_ref.shape[1]
     per = table_ref.shape[1]
     block_len = cache_ref.shape[-1]
-    me = lax.axis_index("seq")
+    me = 0 if absolute else lax.axis_index("seq")
+    heads = outs[0].shape[2]
 
     def invert(r, carry):
         inverse[dest_ref[0, r]] = r
@@ -53,12 +55,17 @@
             for j in range(per):
                 steps.append((len(steps), ref, e, hop, j))
 
+    def toward(hop):
+        return hop if absolute else jnp.bitwise_xor(me, hop)
+
     def count_of(hop, j):
-        return lens_ref[0, inverse[jnp.bitwise_xor(me, hop)]] - j * block_len
+        return lens_ref[0, inverse[toward(hop)]] - j * block_len
 
     def fetch(i, hop, j):
-        row = table_ref[0, j, inverse[jnp.bitwise_xor(me, hop)]]
-        return pltpu.make_async_copy(cache_ref.at[row], buf.at[i], sem_in.at[i])
+        row = table_ref[0, j, inverse[toward(hop)]]
+        return pltpu.make_async_copy(
+            cache_ref.at[row, pl.ds(first, heads)], buf.at[i], sem_in.at[i]
+        )
 
     def ship(i, ref, e, j):
         return pltpu.make_async_copy(buf.at[i], ref.at[e, j], sem_out.at[i])
@@ -87,13 +94,13 @@
         ship(i, ref, e, j).wait()
 
 
-def pack(hops, dest, lens, table, cache, after):
+def pack(hops, dest, lens, table, cache, after, first, heads, absolute=False):
     per, reqs = table.shape[1], table.shape[2]
     count = sum(len(group) for group in hops) * per
-    tail = cache.shape[1:]
+    tail = (heads,) + cache.shape[2:]
 
     def body(*refs):
-        pack_body(hops, *refs[:4], *refs[4 + len(after) :])
+        pack_body(hops, first, absolute, *refs[:4], *refs[4 + len(after) :])
 
     return pl.pallas_call(
         body,
@@ -140,23 +147,25 @@
     )(*arrays, *after)
 
 
-def place(table, arrays, sources, rows):
+def place(table, arrays, sources, shape, first, made=(), absolute=False):
     per = table.shape[1]
-    count = len(sources) * per
     tail = arrays[0].shape[2:]
     moves = [(which, e, hop, j) for which, e, hop in sources for j in range(per)]
+    count = len(moves)
 
     def body(table_ref, *refs):
         ins = refs[: len(arrays)]
         out_ref, buf, sem_in, sem_out = refs[-4:]
-        me = lax.axis_index("seq")
+        me = 0 if absolute else lax.axis_index("seq")
 
         def fetch(i, which, e, j):
             return pltpu.make_async_copy(ins[which].at[e, j], buf.at[i], sem_in.at[i])
 
         def ship(i, hop, j):
-            row = table_ref[0, j, jnp.bitwise_xor(me, hop)]
-            return pltpu.make_async_copy(buf.at[i], out_ref.at[row], sem_out.at[i])
+            row = table_ref[0, j, hop if absolute else jnp.bitwise_xor(me, hop)]
+            return pltpu.make_async_copy(
+                buf.at[i], out_ref.at[row, pl.ds(first, tail[0])], sem_out.at[i]
+            )
 
         for i, (which, e, hop, j) in enumerate(moves):
             fetch(i, which, e, j).start()
@@ -168,17 +177,18 @@
 
     return pl.pallas_call(
         body,
-        out_shape=jax.ShapeDtypeStruct((rows,) + tail, arrays[0].dtype),
-        in_specs=[smem()] + [hbm()] * len(arrays),
+        out_shape=jax.ShapeDtypeStruct(shape, arrays[0].dtype),
+        in_specs=[smem()] + [hbm()] * (len(arrays) + len(made)),
         out_specs=hbm(),
         scratch_shapes=[
             pltpu.VMEM((count,) + tail, arrays[0].dtype),
             pltpu.SemaphoreType.DMA((count,)),
             pltpu.SemaphoreType.DMA((count,)),
         ],
+        input_output_aliases={1 + len(arrays): 0} if made else {},
         compiler_params=pltpu.CompilerParams(vmem_limit_bytes=SIDE_VMEM),
         name="place",
-    )(table, *arrays)
+    )(table, *arrays, *made)
 
 
 def place_last(table, arrays, hops, made):
@@ -191,7 +201,9 @@
 
         def ship(i, which, hop, j):
             row = table_ref[0, j, jnp.bitwise_xor(me, hop)]
-            return pltpu.make_async_copy(refs[which].at[0, j], out_ref.at[row], sem.at[i])
+            return pltpu.make_async_copy(
+                refs[which].at[0, j], out_ref.at[row, pl.ds(0, arrays[0].shape[2])], sem.at[i]
+            )
 
         for i, move in enumerate(moves):
             ship(i, *move).start()
@@ -527,47 +539,47 @@
     barrier = lax.optimization_barrier
     far = list(range(pairs // 2, pairs))
     near = list(range(1, pairs // 2))
+    pair = lambda k: (2 * k, 2 * k + 1)
+    begin = far[:2] + near[:1]
+    middle = near[1:]
+    late = [hop for k in far[2:] for hop in pair(k)]
     args = (dest_device, prior_lens, prior_table, prior_cache)
-    begin = [far[0]] + near[:-1]
-    middle = far[1:-2] + near[-1:]
-    direct = [2 * far[-1]]
-    late = [2 * far[-2], 2 * far[-2] + 1, 2 * far[-1] + 1]
-    pair = lambda k: (2 * k, 2 * k + 1)
+    heads = prior_cache.shape[1]
+    few = max(1, heads * BY_PERMUTE // 4)
     xs = [tokens] + [from_peer(tokens, t) for t in range(1, ways)]
-    begin_out = pack([pair(begin[0])], *args, [])
-    begin_out += pack([pair(k) for k in begin[1:]], *args, begin_out)
+    begin_out = pack([pair(k) for k in begin], *args, [], 0, few)
+    (bulk_out,) = pack(
+        [tuple(range(peers))], *args, begin_out[-1:], few, heads - few, absolute=True
+    )
+    hops = [pair(k) for k in middle] + [(hop,) for hop in late] + [(0, 1)]
+    rest = pack(hops, *args, [bulk_out], 0, few)
+    middle_out, late_out, own = rest[: len(middle)], rest[len(middle) : -1], rest[-1]
     begin_in = [to_hop(value, 2 * k) for k, value in zip(begin, begin_out)]
-    hops = [pair(k) for k in middle] + [(hop,) for hop in direct + late] + [(0, 1)]
-    rest = pack(hops, *args, begin_out[-1:])
-    own = rest[-1]
-    gain = barrier((norm_gain, own))[0][None, :]
+    bulk_in = lax.all_to_all(bulk_out, "seq", split_axis=0, concat_axis=0, tiled=True)
+    gain = barrier((norm_gain, bulk_out))[0][None, :]
     gains = [gain] + [from_peer(gain, t) for t in range(1, ways)]
-
-    ended = begin_in[:1] + [xs[-1]] + begin_in[1:]
-    middle_in = []
-    for i, value in enumerate(rest[: len(middle) + 1]):
-        value = barrier((value, ended[i % len(ended)]))[0]
-        middle_in.append(to_hop(value, hops[i][0]))
     xs, begin_in = barrier((xs, begin_in))
     base, sends = layer(
         ways, span_lens, prior_lens, prior_table, gains, xs,
         w_query, w_key, w_value, w_out, prior_cache,
     )
-    sends, middle_in, late_out = barrier((sends, middle_in, rest[len(middle) + 1 : -1]))
+    sends, middle_out, late_out = barrier((sends, middle_out, late_out))
+    middle_in = [to_hop(value, 2 * k) for k, value in zip(middle, middle_out)]
     late_in = [to_hop(value, hop) for hop, value in zip(late, late_out)]
     total = base
     for t in range(1, ways):
         total = total + to_peer(sends[t - 1], t).astype(jnp.float32)
     hidden = total.astype(jnp.bfloat16)
 
-    arrived = begin_in + middle_in[:-1]
-    other = to_hop(relay(arrived + [own], [base]), 1)
-    rows = prior_cache.shape[0]
+    arrived = begin_in + middle_in
+    other = to_hop(relay(arrived + [own], [hidden]), 1)
     reach = [2 * k for k in begin + middle] + [0]
     sources = [(i, 0, hop) for i, hop in enumerate(reach)]
     sources += [(len(reach), i, hop + 1) for i, hop in enumerate(reach)]
-    sources += [(len(reach) + 1, 0, direct[0])]
-    made = place(dest_table, arrived + [own, other, middle_in[-1]], sources, rows)
+    shape = prior_cache.shape
+    made = place(dest_table, arrived + [own, other], sources, shape, 0)
+    bulk = [(0, s, s) for s in range(peers)]
+    made = place(dest_table, [bulk_in], bulk, shape, few, [made], absolute=True)
     decode_cache = place_last(dest_table, late_in, late, made)
     return (hidden, decode_cache)
 

time: 133 us -> 126 us (0.947)
  waiting for transfers between devices: 53 us -> 38.5 us
  starting transfers between devices: 16.3 us -> 22.2 us
  Pallas kernels: 55.5 us -> 57 us
    ppermute x10, waiting for transfers between devices: 30.9 us -> 5.26 us  [to_hop(): return lax.ppermute(value, 'seq', [(d, d ^ hop) for d in range(peers)])]
    all_to_all x0 -> x1, starting transfers between devices: none -> 7.61 us  [local(): lax.all_to_all(bulk_out, 'seq', split_axis=0, concat_axis=0, tiled=True)]
    ppermute x2, waiting for transfers between devices: 0.01 us -> 6.74 us  [from_peer(): return lax.ppermute(value, 'tp', [((d + t) % ways, d) for d in range(ways)])]
    ppermute x1, waiting for transfers between devices: 22 us -> 26.5 us  [to_peer(): return lax.ppermute(value, 'tp', [(d, (d + t) % ways) for d in range(ways)])]
    ppermute x10, starting transfers between devices: 14.4 us -> 11.7 us  [to_hop(): return lax.ppermute(value, 'seq', [(d, d ^ hop) for d in range(peers)])]
    pallas_call x1 -> x2, Pallas kernels: 5.36 us -> 7.98 us  [place(): pl.pallas_call(body, out_shape=jax.ShapeDtypeStruct(shape, arrays[0].dtyp...]
    unnamed x22 -> x32, local copies, waits for them, and re-layouts: 2.01 us -> 2.85 us
  transfers between devices with their start and end apart: 13 -> 14, of which waited for: 5 -> 6; matrix products, arithmetic and copies ran while one was open for 3% -> 2% of each run, Pallas kernels for 41% -> 45%
where the time goes in v3:
time: 126 us; the launch traced here: 125 us
  Pallas kernels  57 us (45%)
  waiting for transfers between devices  38.5 us (31%)
  starting transfers between devices  22.2 us (18%)
  other arithmetic  3.1 us (2%)
  local copies, waits for them, and re-layouts  2.86 us (2%)
    pallas_call x1, Pallas kernels, layer(): pl.pallas_call(functools.partial(layer_body, ways, q_heads, kv_heads), ou...  35.7 us
    ppermute x1, waiting for transfers between devices, to_peer(): return lax.ppermute(value, 'tp', [(d, (d + t) % ways) for d in range(ways)])  26.5 us
    ppermute x10, starting transfers between devices, to_hop(): return lax.ppermute(value, 'seq', [(d, d ^ hop) for d in range(peers)])  11.7 us
    pallas_call x3, Pallas kernels, pack(): pl.pallas_call(body, out_shape=[jax.ShapeDtypeStruct((len(group), per) +...  10.2 us
    pallas_call x2, Pallas kernels, place(): pl.pallas_call(body, out_shape=jax.ShapeDtypeStruct(shape, arrays[0].dtyp...  7.98 us
    all_to_all x1, starting transfers between devices, local(): lax.all_to_all(bulk_out, 'seq', split_axis=0, concat_axis=0, tiled=True)  7.61 us
    ppermute x2, waiting for transfers between devices, from_peer(): return lax.ppermute(value, 'tp', [((d + t) % ways, d) for d in range(ways)])  6.74 us
    ppermute x10, waiting for transfers between devices, to_hop(): return lax.ppermute(value, 'seq', [(d, d ^ hop) for d in range(peers)])  5.26 us
  transfers between devices with their start and end apart: 14, of which 6 were waited for; matrix products, arithmetic and copies ran while one was open for 2% of the time, Pallas kernels for 45%

profile of v3, /device:TPU:19, one launch (start us, length us, event | category | flops | bytes accessed | tf_op | source)
XLA Modules:
  0.0 124.8 jit_solution(4082569600518140171)
XLA Ops:
  0.6 1.3 %collective-permute-start.1 = (bf16[512,1280]{1,0:T(8,128)(2,1)}, bf16[512,1280]{1,0:T(8,128)(2,1)S(1)}, u32[]{:S(2)}, u32[]{:S(2)}) collective-permute-start(bf16[512,1280]{1,0:T(8,128)(2,1)} %refs_6_), channel_id=1, source_target_pairs={{1,0},{0,1},{3,2},{2,3},{5,4},{4,5},{7,6},{6,7},{9,8},{8,9},{11,10... | collective-permute-start | bytes 3932168 | tf_op jit(solution)/shard_map/ppermute | solution.py:528
  1.9 2.7 %pack.3 = (bf16[2,2,1,2,80,128]{5,4,3,2,1,0:T(8,128)(2,1)}, bf16[2,2,1,2,80,128]{5,4,3,2,1,0:T(8,128)(2,1)}, bf16[2,2,1,2,80,128]{5,4,3,2,1,0:T(8,128)(2,1)}) custom-call(s32[1,16]{1,0:T(1,128)} %refs_0_.7, s32[1,16]{1,0:T(1,128)} %refs_1_.7, s32[1,2,16]{2,1,0:T(2,128)} %bitcast.7, bf16[32,4,2,80,128]{4,3,2,1,0:T(8,128)(2,1)} %refs_3_.6), custom_call_target="tpu_custom_call" | custom-call | tf_op jit(solution)/shard_map/pack/pallas_call | solution.py:105
  4.6 0.1 collective-permute-start.2
  4.8 2.3 %collective-permute-start.3 = (bf16[2,2,1,2,80,128]{5,4,3,2,1,0:T(8,128)(2,1)}, bf16[2,2,1,2,80,128]{5,4,3,2,1,0:T(8,128)(2,1)S(1)}, u32[]{:S(2)}, u32[]{:S(2)}) collective-permute-start(bf16[2,2,1,2,80,128]{5,4,3,2,1,0:T(8,128)(2,1)} %get-tuple-element.30), channel_id=1, source_target_pairs={{0,20},{2,22},{4,16},{6,18},{8,28},{10,30},{12,24},{14,26},{16,4},... | collective-permute-start | bytes 491528 | tf_op jit(solution)/shard_map/ppermute | solution.py:537
  7.1 1.2 collective-permute-start.4
  8.2 4.3 %pack.4.refs_4_ = bf16[16,2,3,2,80,128]{5,4,3,2,1,0:T(8,128)(2,1)} custom-call(s32[1,16]{1,0:T(1,128)} %refs_0_.7, s32[1,16]{1,0:T(1,128)} %refs_1_.7, s32[1,2,16]{2,1,0:T(2,128)} %bitcast.8, bf16[32,4,2,80,128]{4,3,2,1,0:T(8,128)(2,1)} %refs_3_.6, bf16[2,2,1,2,80,128]{5,4,3,2,1,0:T(8,128)(2,1)} %get-tuple-element.27.refs_4_), custom_call_target="tpu_custom_call" | custom-call | tf_op jit(solution)/shard_map/pack/pallas_call | solution.py:105
  12.6 0.0 copy-start.7
  12.6 0.3 collective-permute-start
  12.9 0.3 copy-done.7
  13.2 7.6 %all-to-all-start = ((bf16[16,2,3,2,80,128]{5,4,3,2,1,0:T(8,128)(2,1)}), bf16[16,2,3,2,80,128]{5,4,3,2,1,0:T(8,128)(2,1)}, u32[]{:S(2)}, u32[]{:S(2)}) async-start(bf16[16,2,3,2,80,128]{5,4,3,2,1,0:T(8,128)(2,1)} %pack.4.refs_4_), calls=%async_computation | async-start | bytes 7864320 | tf_op jit(solution)/shard_map/all_to_all | solution.py:558
  20.8 3.2 %pack.5 = (bf16[2,2,1,2,80,128]{5,4,3,2,1,0:T(8,128)(2,1)}, bf16[2,2,1,2,80,128]{5,4,3,2,1,0:T(8,128)(2,1)}, bf16[1,2,1,2,80,128]{5,4,3,2,1,0:T(8,128)(2,1)}, bf...) custom-call(s32[1,16]{1,0:T(1,128)} %refs_0_.7, ...), custom_call_target="tpu_custom_call" | custom-call | tf_op jit(solution)/shard_map/pack/pallas_call | solution.py:105
  24.0 0.0 collective-permute-done.2.refs_0_
  24.0 0.0 collective-permute-done.3.refs_1_
  24.0 0.0 copy-start.2
  24.0 0.0 collective-permute-done.4.refs_2_
  24.0 6.6 %collective-permute-done.1.refs_7_ = bf16[512,1280]{1,0:T(8,128)(2,1)S(1)} collective-permute-done((bf16[512,1280]{1,0:T(8,128)(2,1)}, bf16[512,1280]{1,0:T(8,128)(2,1)S(1)}, u32[]{:S(2)}, u32[]{:S(2)}) %collective-permute-start.1) | collective-permute-done | bytes 1310752 | tf_op jit(solution)/shard_map/ppermute | solution.py:528
  30.7 0.1 collective-permute-done.refs_5_
  30.8 0.9 copy-done.9
  31.7 35.7 %layer.1 = (f32[512,1280]{1,0:T(8,128)}, bf16[512,1280]{1,0:T(8,128)(2,1)}) custom-call(s32[1,16]{1,0:T(1,128)} %refs_0_.6, s32[1,16]{1,0:T(1,128)} %refs_1_.7, s32[1,2,16]{2,1,0:T(2,128)} %bitcast.10, f32[1,128]{1,0:T(1,128)} %constant.2.clone.refs_3_, bf16[1,1280]{1,0:T(2,128)(2,1)} %copy-done.7, bf16[1,1280]{1,0:T(2,128)(2,1)} %copy-done.15, ...), custom_call_target="tpu_custom_call" | custom-call | flops 671088640000 | bytes 13107200 | tf_op jit(solution)/shard_map/layer/pallas_call | solution.py:470
  67.5 1.3 %collective-permute-start.5 = (bf16[512,1280]{1,0:T(8,128)(2,1)}, bf16[512,1280]{1,0:T(8,128)(2,1)S(1)}, u32[]{:S(2)}, u32[]{:S(2)}) collective-permute-start(bf16[512,1280]{1,0:T(8,128)(2,1)} %get-tuple-element.41), channel_id=1, source_target_pairs={{0,1},{1,0},{2,3},{3,2},{4,5},{5,4},{6,7},{7,6},{8,9},{9,8},{10,11... | collective-permute-start | bytes 3932168 | tf_op jit(solution)/shard_map/ppermute | solution.py:531
  68.8 1.3 %collective-permute-start.10 = (bf16[2,2,1,2,80,128]{5,4,3,2,1,0:T(8,128)(2,1)}, bf16[2,2,1,2,80,128]{5,4,3,2,1,0:T(8,128)(2,1)S(1)}, u32[]{:S(2)}, u32[]{:S(2)}) collective-permute-start(bf16[2,2,1,2,80,128]{5,4,3,2,1,0:T(8,128)(2,1)} %get-tuple-element.49), channel_id=1, source_target_pairs={{0,8},{2,10},{4,12},{6,14},{8,0},{10,2},{12,4},{14,6},{16,24},{18,... | collective-permute-start | bytes 491528 | tf_op jit(solution)/shard_map/ppermute | solution.py:537
  70.1 0.0 collective-permute-start.11
  70.1 26.5 %collective-permute-done.5 = bf16[512,1280]{1,0:T(8,128)(2,1)S(1)} collective-permute-done((bf16[512,1280]{1,0:T(8,128)(2,1)}, bf16[512,1280]{1,0:T(8,128)(2,1)S(1)}, u32[]{:S(2)}, u32[]{:S(2)}) %collective-permute-start.5) | collective-permute-done | bytes 1310752 | tf_op jit(solution)/shard_map/ppermute | solution.py:531
  96.6 3.1 %add_convert_fusion.refs_6_ = bf16[512,1280]{1,0:T(8,128)(2,1)} fusion(f32[512,1280]{1,0:T(8,128)} %get-tuple-element.33, bf16[512,1280]{1,0:T(8,128)(2,1)S(1)} %collective-permute-done.5), kind=kLoop, calls=%fused_computation | loop fusion | flops 1966080 | bytes 5242880 | tf_op jit(solution)/shard_map/convert_element_type | solution.py:572
  99.8 0.0 collective-permute-done.10.refs_3_
  99.8 0.0 collective-permute-done.11.refs_4_
  99.8 0.0 copy-start.5
  99.8 0.6 copy-done.4
  100.4 0.1 copy-done.5
  100.5 1.8 %relay.1 = bf16[6,2,1,2,80,128]{5,4,3,2,1,0:T(8,128)(2,1)} custom-call(bf16[2,2,1,2,80,128]{5,4,3,2,1,0:T(8,128)(2,1)} %copy-done.1, bf16[2,2,1,2,80,128]{5,4,3,2,1,0:T(8,128)(2,1)} %copy-done.2, bf16[2,2,1,2,80,128]{5,4,3,2,1,0:T(8,128)(2,1)} %copy-done.3, bf16[2,2,1,2,80,128]{5,4,3,2,1,0:T(8,128)(2,1)} %copy-done.4, ...), custom_call_target="tpu_custom_call" | custom-call | tf_op jit(solution)/shard_map/relay/pallas_call | solution.py:135
  102.4 2.4 %collective-permute-start.12 = (bf16[6,2,1,2,80,128]{5,4,3,2,1,0:T(8,128)(2,1)}, bf16[6,2,1,2,80,128]{5,4,3,2,1,0:T(8,128)(2,1)S(1)}, u32[]{:S(2)}, u32[]{:S(2)}) collective-permute-start(bf16[6,2,1,2,80,128]{5,4,3,2,1,0:T(8,128)(2,1)} %relay.1), channel_id=1, source_target_pairs={{0,2},{2,0},{4,6},{6,4},{8,10},{10,8},{12,14},{14,12},{16,18},{18,... | collective-permute-start | bytes 1474568 | tf_op jit(solution)/shard_map/ppermute | solution.py:537
  104.8 0.0 collective-permute-start.6
  104.8 0.0 copy-done.13
  104.8 1.7 %collective-permute-start.7 = (bf16[1,2,1,2,80,128]{5,4,3,2,1,0:T(8,128)(2,1)S(1)}, bf16[1,2,1,2,80,128]{5,4,3,2,1,0:T(8,128)(2,1)S(1)}, u32[]{:S(2)}, u32[]{:S(2)}) collective-permute-start(bf16[1,2,1,2,80,128]{5,4,3,2,1,0:T(8,128)(2,1)S(1)} %copy-done.13), channel_id=1, source_target_pairs={{0,26},{2,24},{4,30},{6,28},{8,18},{10,16},{12,22},{14,20},{16,10}... | collective-permute-start | bytes 245768 | tf_op jit(solution)/shard_map/ppermute | solution.py:537
  106.5 0.0 copy-done.12
  106.5 0.1 collective-permute-start.8
  106.6 2.6 %collective-permute-start.9 = (bf16[1,2,1,2,80,128]{5,4,3,2,1,0:T(8,128)(2,1)S(1)}, bf16[1,2,1,2,80,128]{5,4,3,2,1,0:T(8,128)(2,1)S(1)}, u32[]{:S(2)}, u32[]{:S(2)}) collective-permute-start(bf16[1,2,1,2,80,128]{5,4,3,2,1,0:T(8,128)(2,1)S(1)} %copy-done.11), channel_id=1, source_target_pairs={{0,30},{2,28},{4,26},{6,24},{8,22},{10,20},{12,18},{14,16},{16,14}... | collective-permute-start | bytes 245768 | tf_op jit(solution)/shard_map/ppermute | solution.py:537
  109.2 0.0 collective-permute-done.12.refs_6_
  109.2 0.8 copy-done.6
  110.0 2.9 %place.2.refs_1_ = bf16[32,4,2,80,128]{4,3,2,1,0:T(8,128)(2,1)} custom-call(s32[1,2,16]{2,1,0:T(2,128)} %bitcast.4, bf16[2,2,1,2,80,128]{5,4,3,2,1,0:T(8,128)(2,1)} %copy-done.1, bf16[2,2,1,2,80,128]{5,4,3,2,1,0:T(8,128)(2,1)} %copy-done.2, bf16[2,2,1,2,80,128]{5,4,3,2,1,0:T(8,128)(2,1)} %copy-done.3, bf16[2,2,1,2,80,128]{5,4,3,2,1,0:T(8,128)(2,1)} %copy-done.4, ...), custom_call_target="tpu_custom_call" | custom-call | tf_op jit(solution)/shard_map/place/pallas_call | solution.py:178
  112.9 0.0 copy-start
  112.9 0.0 all-to-all-done.refs_0_
  112.9 5.1 %place.3.refs_4_ = bf16[32,4,2,80,128]{4,3,2,1,0:T(8,128)(2,1)} custom-call(s32[1,2,16]{2,1,0:T(2,128)} %bitcast.5, bf16[16,2,3,2,80,128]{5,4,3,2,1,0:T(8,128)(2,1)} %all-to-all-done.refs_0_, bf16[32,4,2,80,128]{4,3,2,1,0:T(8,128)(2,1)} %place.2.refs_1_), custom_call_target="tpu_custom_call", output_to_operand_aliasing={{}: (2, {})} | custom-call | tf_op jit(solution)/shard_map/place/pallas_call | solution.py:178
  118.0 0.0 collective-permute-done.6.refs_0_
  118.0 0.1 collective-permute-done.7.refs_1_
  118.2 3.2 %collective-permute-done.8.refs_2_ = bf16[1,2,1,2,80,128]{5,4,3,2,1,0:T(8,128)(2,1)S(1)} collective-permute-done((bf16[1,2,1,2,80,128]{5,4,3,2,1,0:T(8,128)(2,1)S(1)}, bf16[1,2,1,2,80,128]{5,4,3,2,1,0:T(8,128)(2,1)S(1)}, u32[]{:S(2)}, u32[]{:S(2)}) %collective-permute-start.8) | collective-permute-done | bytes 81952 | tf_op jit(solution)/shard_map/ppermute | solution.py:537
  121.4 1.9 %collective-permute-done.9.refs_3_ = bf16[1,2,1,2,80,128]{5,4,3,2,1,0:T(8,128)(2,1)S(1)} collective-permute-done((bf16[1,2,1,2,80,128]{5,4,3,2,1,0:T(8,128)(2,1)S(1)}, bf16[1,2,1,2,80,128]{5,4,3,2,1,0:T(8,128)(2,1)S(1)}, u32[]{:S(2)}, u32[]{:S(2)}) %collective-permute-start.9) | collective-permute-done | bytes 81952 | tf_op jit(solution)/shard_map/ppermute | solution.py:537
  123.3 1.3 %place_last.1 = bf16[32,4,2,80,128]{4,3,2,1,0:T(8,128)(2,1)} custom-call(s32[1,2,16]{2,1,0:T(2,128)S(1)} %bitcast.6, bf16[1,2,1,2,80,128]{5,4,3,2,1,0:T(8,128)(2,1)S(1)} %collective-permute-done.6.refs_0_, bf16[1,2,1,2,80,128]{5,4,3,2,1,0:T(8,128)(2,1)S(1)} %collective-permute-done.7.refs_1_, ...), custom_call_target="tpu_custom_call", output_to_operand_aliasing={{}: (5, {})} | custom-call | tf_op jit(solution)/shard_map/place_last/pallas_call | solution.py:213
  (22 shorter events, 0.0 us)
Async XLA Ops:
  0.6 30.0 %collective-permute-start.1 = (bf16[512,1280]{1,0:T(8,128)(2,1)}, bf16[512,1280]{1,0:T(8,128)(2,1)S(1)}, u32[]{:S(2)}, u32[]{:S(2)}) collective-permute-start(bf16[512,1280]{1,0:T(8,128)(2,1)} %refs_6_), channel_id=1, source_target_pairs={{1,0},{0,1},{3,2},{2,3},{5,4},{4,5},{7,6},{6,7},{9,8},{8,9},{11,10... | collective-permute-start | bytes 3932168 | tf_op jit(solution)/shard_map/ppermute | solution.py:528
  4.6 19.4 %collective-permute-start.2 = (bf16[2,2,1,2,80,128]{5,4,3,2,1,0:T(8,128)(2,1)}, bf16[2,2,1,2,80,128]{5,4,3,2,1,0:T(8,128)(2,1)S(1)}, u32[]{:S(2)}, u32[]{:S(2)}) collective-permute-start(bf16[2,2,1,2,80,128]{5,4,3,2,1,0:T(8,128)(2,1)} %get-tuple-element.29), channel_id=1, source_target_pairs={{0,16},{2,18},{4,20},{6,22},{8,24},{10,26},{12,28},{14,30},{16,0},... | collective-permute-start | bytes 491528 | tf_op jit(solution)/shard_map/ppermute | solution.py:537
  4.8 19.2 %collective-permute-start.3 = (bf16[2,2,1,2,80,128]{5,4,3,2,1,0:T(8,128)(2,1)}, bf16[2,2,1,2,80,128]{5,4,3,2,1,0:T(8,128)(2,1)S(1)}, u32[]{:S(2)}, u32[]{:S(2)}) collective-permute-start(bf16[2,2,1,2,80,128]{5,4,3,2,1,0:T(8,128)(2,1)} %get-tuple-element.30), channel_id=1, source_target_pairs={{0,20},{2,22},{4,16},{6,18},{8,28},{10,30},{12,24},{14,26},{16,4},... | collective-permute-start | bytes 491528 | tf_op jit(solution)/shard_map/ppermute | solution.py:537
  7.0 5.5 %copy-start.8 = (bf16[1280]{0:T(1024)(128)(2,1)S(1)}, bf16[1280]{0:T(1024)(128)(2,1)}, u32[]{:S(2)}) copy-start(bf16[1280]{0:T(1024)(128)(2,1)} %param.14) | copy-start | bytes 7684
  7.1 17.0 %collective-permute-start.4 = (bf16[2,2,1,2,80,128]{5,4,3,2,1,0:T(8,128)(2,1)}, bf16[2,2,1,2,80,128]{5,4,3,2,1,0:T(8,128)(2,1)S(1)}, u32[]{:S(2)}, u32[]{:S(2)}) collective-permute-start(bf16[2,2,1,2,80,128]{5,4,3,2,1,0:T(8,128)(2,1)} %get-tuple-element.27.refs_4_), channel_id=1, source_target_pairs={{0,4},{2,6},{4,0},{6,2},{8,12},{10,14},{12,8},{14,10},{16,20},{18,... | collective-permute-start | bytes 491528 | tf_op jit(solution)/shard_map/ppermute | solution.py:537
  12.6 0.6 copy-start.7
  12.6 18.2 %collective-permute-start = (bf16[1,1280]{1,0:T(2,128)(2,1)S(1)}, bf16[1,1280]{1,0:T(2,128)(2,1)S(1)}, u32[]{:S(2)}, u32[]{:S(2)}) collective-permute-start(bf16[1,1280]{1,0:T(2,128)(2,1)S(1)} %broadcast_in_dim.3.refs_4_), channel_id=1, source_target_pairs={{1,0},{0,1},{3,2},{2,3},{5,4},{4,5},{7,6},{6,7},{9,8},{8,9},{11,10... | collective-permute-start | bytes 7688 | tf_op jit(solution)/shard_map/ppermute | solution.py:528
  13.2 99.7 %all-to-all-start = ((bf16[16,2,3,2,80,128]{5,4,3,2,1,0:T(8,128)(2,1)}), bf16[16,2,3,2,80,128]{5,4,3,2,1,0:T(8,128)(2,1)}, u32[]{:S(2)}, u32[]{:S(2)}) async-start(bf16[16,2,3,2,80,128]{5,4,3,2,1,0:T(8,128)(2,1)} %pack.4.refs_4_), calls=%async_computation | async-start | bytes 7864320 | tf_op jit(solution)/shard_map/all_to_all | solution.py:558
  24.0 43.5 %copy-start.1 = (bf16[2,2,1,2,80,128]{5,4,3,2,1,0:T(8,128)(2,1)}, bf16[2,2,1,2,80,128]{5,4,3,2,1,0:T(8,128)(2,1)S(1)}, u32[]{:S(2)}) copy-start(bf16[2,2,1,2,80,128]{5,4,3,2,1,0:T(8,128)(2,1)S(1)} %collective-permute-done.2.refs_0_) | copy-start | bytes 491524
  24.0 43.5 %copy-start.2 = (bf16[2,2,1,2,80,128]{5,4,3,2,1,0:T(8,128)(2,1)}, bf16[2,2,1,2,80,128]{5,4,3,2,1,0:T(8,128)(2,1)S(1)}, u32[]{:S(2)}) copy-start(bf16[2,2,1,2,80,128]{5,4,3,2,1,0:T(8,128)(2,1)S(1)} %collective-permute-done.3.refs_1_) | copy-start | bytes 491524
  24.0 43.5 %copy-start.3 = (bf16[2,2,1,2,80,128]{5,4,3,2,1,0:T(8,128)(2,1)}, bf16[2,2,1,2,80,128]{5,4,3,2,1,0:T(8,128)(2,1)S(1)}, u32[]{:S(2)}) copy-start(bf16[2,2,1,2,80,128]{5,4,3,2,1,0:T(8,128)(2,1)S(1)} %collective-permute-done.4.refs_2_) | copy-start | bytes 491524
  30.7 1.1 copy-start.9
  30.8 0.9 copy-start.15
  31.7 38.4 %copy-start.10 = (bf16[2,2,1,2,80,128]{5,4,3,2,1,0:T(8,128)(2,1)S(1)}, bf16[2,2,1,2,80,128]{5,4,3,2,1,0:T(8,128)(2,1)}, u32[]{:S(2)}) copy-start(bf16[2,2,1,2,80,128]{5,4,3,2,1,0:T(8,128)(2,1)} %get-tuple-element.50) | copy-start | bytes 491524
  67.5 29.1 %collective-permute-start.5 = (bf16[512,1280]{1,0:T(8,128)(2,1)}, bf16[512,1280]{1,0:T(8,128)(2,1)S(1)}, u32[]{:S(2)}, u32[]{:S(2)}) collective-permute-start(bf16[512,1280]{1,0:T(8,128)(2,1)} %get-tuple-element.41), channel_id=1, source_target_pairs={{0,1},{1,0},{2,3},{3,2},{4,5},{5,4},{6,7},{7,6},{8,9},{9,8},{10,11... | collective-permute-start | bytes 3932168 | tf_op jit(solution)/shard_map/ppermute | solution.py:531
  68.8 31.0 %collective-permute-start.10 = (bf16[2,2,1,2,80,128]{5,4,3,2,1,0:T(8,128)(2,1)}, bf16[2,2,1,2,80,128]{5,4,3,2,1,0:T(8,128)(2,1)S(1)}, u32[]{:S(2)}, u32[]{:S(2)}) collective-permute-start(bf16[2,2,1,2,80,128]{5,4,3,2,1,0:T(8,128)(2,1)} %get-tuple-element.49), channel_id=1, source_target_pairs={{0,8},{2,10},{4,12},{6,14},{8,0},{10,2},{12,4},{14,6},{16,24},{18,... | collective-permute-start | bytes 491528 | tf_op jit(solution)/shard_map/ppermute | solution.py:537
  70.1 29.6 %collective-permute-start.11 = (bf16[2,2,1,2,80,128]{5,4,3,2,1,0:T(8,128)(2,1)S(1)}, bf16[2,2,1,2,80,128]{5,4,3,2,1,0:T(8,128)(2,1)S(1)}, u32[]{:S(2)}, u32[]{:S(2)}) collective-permute-start(bf16[2,2,1,2,80,128]{5,4,3,2,1,0:T(8,128)(2,1)S(1)} %copy-done.10), channel_id=1, source_target_pairs={{0,12},{2,14},{4,8},{6,10},{8,4},{10,6},{12,0},{14,2},{16,28},{18,... | collective-permute-start | bytes 491528 | tf_op jit(solution)/shard_map/ppermute | solution.py:537
  99.7 5.0 %copy-start.14 = (bf16[1,2,1,2,80,128]{5,4,3,2,1,0:T(8,128)(2,1)S(1)}, bf16[1,2,1,2,80,128]{5,4,3,2,1,0:T(8,128)(2,1)}, u32[]{:S(2)}) copy-start(bf16[1,2,1,2,80,128]{5,4,3,2,1,0:T(8,128)(2,1)} %get-tuple-element.42) | copy-start | bytes 245764
  99.8 5.0 %copy-start.13 = (bf16[1,2,1,2,80,128]{5,4,3,2,1,0:T(8,128)(2,1)S(1)}, bf16[1,2,1,2,80,128]{5,4,3,2,1,0:T(8,128)(2,1)}, u32[]{:S(2)}) copy-start(bf16[1,2,1,2,80,128]{5,4,3,2,1,0:T(8,128)(2,1)} %get-tuple-element.43) | copy-start | bytes 245764
  99.8 6.7 %copy-start.12 = (bf16[1,2,1,2,80,128]{5,4,3,2,1,0:T(8,128)(2,1)S(1)}, bf16[1,2,1,2,80,128]{5,4,3,2,1,0:T(8,128)(2,1)}, u32[]{:S(2)}) copy-start(bf16[1,2,1,2,80,128]{5,4,3,2,1,0:T(8,128)(2,1)} %get-tuple-element.44) | copy-start | bytes 245764
  99.8 6.9 %copy-start.11 = (bf16[1,2,1,2,80,128]{5,4,3,2,1,0:T(8,128)(2,1)S(1)}, bf16[1,2,1,2,80,128]{5,4,3,2,1,0:T(8,128)(2,1)}, u32[]{:S(2)}) copy-start(bf16[1,2,1,2,80,128]{5,4,3,2,1,0:T(8,128)(2,1)} %get-tuple-element.45) | copy-start | bytes 245764
  99.8 0.7 copy-start.4
  99.8 0.7 copy-start.5
  102.4 6.8 %collective-permute-start.12 = (bf16[6,2,1,2,80,128]{5,4,3,2,1,0:T(8,128)(2,1)}, bf16[6,2,1,2,80,128]{5,4,3,2,1,0:T(8,128)(2,1)S(1)}, u32[]{:S(2)}, u32[]{:S(2)}) collective-permute-start(bf16[6,2,1,2,80,128]{5,4,3,2,1,0:T(8,128)(2,1)} %relay.1), channel_id=1, source_target_pairs={{0,2},{2,0},{4,6},{6,4},{8,10},{10,8},{12,14},{14,12},{16,18},{18,... | collective-permute-start | bytes 1474568 | tf_op jit(solution)/shard_map/ppermute | solution.py:537
  104.8 13.3 %collective-permute-start.6 = (bf16[1,2,1,2,80,128]{5,4,3,2,1,0:T(8,128)(2,1)S(1)}, bf16[1,2,1,2,80,128]{5,4,3,2,1,0:T(8,128)(2,1)S(1)}, u32[]{:S(2)}, u32[]{:S(2)}) collective-permute-start(bf16[1,2,1,2,80,128]{5,4,3,2,1,0:T(8,128)(2,1)S(1)} %copy-done.14), channel_id=1, source_target_pairs={{0,24},{2,26},{4,28},{6,30},{8,16},{10,18},{12,20},{14,22},{16,8},... | collective-permute-start | bytes 245768 | tf_op jit(solution)/shard_map/ppermute | solution.py:537
  104.8 13.4 %collective-permute-start.7 = (bf16[1,2,1,2,80,128]{5,4,3,2,1,0:T(8,128)(2,1)S(1)}, bf16[1,2,1,2,80,128]{5,4,3,2,1,0:T(8,128)(2,1)S(1)}, u32[]{:S(2)}, u32[]{:S(2)}) collective-permute-start(bf16[1,2,1,2,80,128]{5,4,3,2,1,0:T(8,128)(2,1)S(1)} %copy-done.13), channel_id=1, source_target_pairs={{0,26},{2,24},{4,30},{6,28},{8,18},{10,16},{12,22},{14,20},{16,10}... | collective-permute-start | bytes 245768 | tf_op jit(solution)/shard_map/ppermute | solution.py:537
  106.5 14.9 %collective-permute-start.8 = (bf16[1,2,1,2,80,128]{5,4,3,2,1,0:T(8,128)(2,1)S(1)}, bf16[1,2,1,2,80,128]{5,4,3,2,1,0:T(8,128)(2,1)S(1)}, u32[]{:S(2)}, u32[]{:S(2)}) collective-permute-start(bf16[1,2,1,2,80,128]{5,4,3,2,1,0:T(8,128)(2,1)S(1)} %copy-done.12), channel_id=1, source_target_pairs={{0,28},{2,30},{4,24},{6,26},{8,20},{10,22},{12,16},{14,18},{16,12}... | collective-permute-start | bytes 245768 | tf_op jit(solution)/shard_map/ppermute | solution.py:537
  106.6 16.7 %collective-permute-start.9 = (bf16[1,2,1,2,80,128]{5,4,3,2,1,0:T(8,128)(2,1)S(1)}, bf16[1,2,1,2,80,128]{5,4,3,2,1,0:T(8,128)(2,1)S(1)}, u32[]{:S(2)}, u32[]{:S(2)}) collective-permute-start(bf16[1,2,1,2,80,128]{5,4,3,2,1,0:T(8,128)(2,1)S(1)} %copy-done.11), channel_id=1, source_target_pairs={{0,30},{2,28},{4,26},{6,24},{8,22},{10,20},{12,18},{14,16},{16,14}... | collective-permute-start | bytes 245768 | tf_op jit(solution)/shard_map/ppermute | solution.py:537
  109.2 0.8 copy-start.6
  112.9 10.4 %copy-start = (s32[1,16,2]{1,2,0:T(2,128)S(1)}, s32[1,16,2]{1,2,0:T(2,128)}, u32[]{:S(2)}) copy-start(s32[1,16,2]{1,2,0:T(2,128)} %param.24) | copy-start | bytes 388

commit v4 on v3

--- a/solution.py
+++ b/solution.py
@@ -147,48 +147,68 @@
     )(*arrays, *after)
 
 
-def place(table, arrays, sources, shape, first, made=(), absolute=False):
+def place(table, arrays, sources, bulk, shape):
     per = table.shape[1]
-    tail = arrays[0].shape[2:]
+    tail, bulk_tail = arrays[0].shape[2:], bulk.shape[2:]
     moves = [(which, e, hop, j) for which, e, hop in sources for j in range(per)]
-    count = len(moves)
+    bulk_moves = [(s, j) for s in range(bulk.shape[0]) for j in range(per)]
+    count, bulk_count = len(moves), len(bulk_moves)
 
     def body(table_ref, *refs):
-        ins = refs[: len(arrays)]
-        out_ref, buf, sem_in, sem_out = refs[-4:]
-        me = 0 if absolute else lax.axis_index("seq")
+        bulk_ref = refs[len(arrays)]
+        out_ref, buf, bulk_buf, sem_in, sem_out, bulk_sem_in, bulk_sem_out = refs[-7:]
+        me = lax.axis_index("seq")
 
         def fetch(i, which, e, j):
-            return pltpu.make_async_copy(ins[which].at[e, j], buf.at[i], sem_in.at[i])
+            return pltpu.make_async_copy(refs[which].at[e, j], buf.at[i], sem_in.at[i])
 
         def ship(i, hop, j):
-            row = table_ref[0, j, hop if absolute else jnp.bitwise_xor(me, hop)]
+            row = table_ref[0, j, jnp.bitwise_xor(me, hop)]
             return pltpu.make_async_copy(
-                buf.at[i], out_ref.at[row, pl.ds(first, tail[0])], sem_out.at[i]
+                buf.at[i], out_ref.at[row, pl.ds(0, tail[0])], sem_out.at[i]
             )
 
+        def bulk_fetch(i, s, j):
+            return pltpu.make_async_copy(bulk_ref.at[s, j], bulk_buf.at[i], bulk_sem_in.at[i])
+
+        def bulk_ship(i, s, j):
+            return pltpu.make_async_copy(
+                bulk_buf.at[i],
+                out_ref.at[table_ref[0, j, s], pl.ds(tail[0], bulk_tail[0])],
+                bulk_sem_out.at[i],
+            )
+
+        for i, move in enumerate(bulk_moves):
+            bulk_fetch(i, *move).start()
         for i, (which, e, hop, j) in enumerate(moves):
             fetch(i, which, e, j).start()
+        for i, move in enumerate(bulk_moves):
+            bulk_fetch(i, *move).wait()
+            bulk_ship(i, *move).start()
         for i, (which, e, hop, j) in enumerate(moves):
             fetch(i, which, e, j).wait()
             ship(i, hop, j).start()
+        for i, move in enumerate(bulk_moves):
+            bulk_ship(i, *move).wait()
         for i, (which, e, hop, j) in enumerate(moves):
             ship(i, hop, j).wait()
 
     return pl.pallas_call(
         body,
-        out_shape=jax.ShapeDtypeStruct(shape, arrays[0].dtype),
-        in_specs=[smem()] + [hbm()] * (len(arrays) + len(made)),
+        out_shape=jax.ShapeDtypeStruct(shape, bulk.dtype),
+        in_specs=[smem()] + [hbm()] * (len(arrays) + 1),
         out_specs=hbm(),
         scratch_shapes=[
-            pltpu.VMEM((count,) + tail, arrays[0].dtype),
+            pltpu.VMEM((count,) + tail, bulk.dtype),
+            pltpu.VMEM((bulk_count,) + bulk_tail, bulk.dtype),
             pltpu.SemaphoreType.DMA((count,)),
             pltpu.SemaphoreType.DMA((count,)),
+            pltpu.SemaphoreType.DMA((bulk_count,)),
+            pltpu.SemaphoreType.DMA((bulk_count,)),
         ],
-        input_output_aliases={1 + len(arrays): 0} if made else {},
         compiler_params=pltpu.CompilerParams(vmem_limit_bytes=SIDE_VMEM),
         name="place",
-    )(table, *arrays, *made)
+    )(table, *arrays, bulk)
 
 
 def place_last(table, arrays, hops, made):
@@ -566,20 +586,18 @@
     sends, middle_out, late_out = barrier((sends, middle_out, late_out))
     middle_in = [to_hop(value, 2 * k) for k, value in zip(middle, middle_out)]
     late_in = [to_hop(value, hop) for hop, value in zip(late, late_out)]
+    got = [to_peer(sends[t - 1], t) for t in range(1, ways)]
     total = base
-    for t in range(1, ways):
-        total = total + to_peer(sends[t - 1], t).astype(jnp.float32)
+    for value in got:
+        total = total + value.astype(jnp.float32)
     hidden = total.astype(jnp.bfloat16)
-
     arrived = begin_in + middle_in
     other = to_hop(relay(arrived + [own], [hidden]), 1)
     reach = [2 * k for k in begin + middle] + [0]
     sources = [(i, 0, hop) for i, hop in enumerate(reach)]
     sources += [(len(reach), i, hop + 1) for i, hop in enumerate(reach)]
     shape = prior_cache.shape
-    made = place(dest_table, arrived + [own, other], sources, shape, 0)
-    bulk = [(0, s, s) for s in range(peers)]
-    made = place(dest_table, [bulk_in], bulk, shape, few, [made], absolute=True)
+    made = place(dest_table, arrived + [own, other], sources, bulk_in, shape)
     decode_cache = place_last(dest_table, late_in, late, made)
     return (hidden, decode_cache)
 

time: 126 us -> 125 us (level)
  Pallas kernels: 57 us -> 55.1 us
  starting transfers between devices: 22.2 us -> 23.8 us
    ppermute x10, waiting for transfers between devices: 5.26 us -> 7.24 us  [to_hop(): return lax.ppermute(value, 'seq', [(d, d ^ hop) for d in range(peers)])]
    pallas_call x2 -> x1, Pallas kernels: 7.98 us -> 6.19 us  [place(): pl.pallas_call(body, out_shape=jax.ShapeDtypeStruct(shape, bulk.dtype), i...]
    ppermute x1, waiting for transfers between devices: 26.5 us -> 24.8 us  [to_peer(): return lax.ppermute(value, 'tp', [(d, (d + t) % ways) for d in range(ways)])]
    ppermute x10, starting transfers between devices: 11.7 us -> 13.4 us  [to_hop(): return lax.ppermute(value, 'seq', [(d, d ^ hop) for d in range(peers)])]
  transfers between devices with their start and end apart: 14 -> 14, of which waited for: 6 -> 6; matrix products, arithmetic and copies ran while one was open for 2% -> 2% of each run, Pallas kernels for 45% -> 43%
where the time goes in v4:
time: 125 us
  Pallas kernels  55.1 us (44%)
  waiting for transfers between devices  39 us (31%)
  starting transfers between devices  23.8 us (19%)
  other arithmetic  3.1 us (2%)
  local copies, waits for them, and re-layouts  2.77 us (2%)
    pallas_call x1, Pallas kernels, layer(): pl.pallas_call(functools.partial(layer_body, ways, q_heads, kv_heads), ou...  35.6 us
    ppermute x1, waiting for transfers between devices, to_peer(): return lax.ppermute(value, 'tp', [(d, (d + t) % ways) for d in range(ways)])  24.8 us
    ppermute x10, starting transfers between devices, to_hop(): return lax.ppermute(value, 'seq', [(d, d ^ hop) for d in range(peers)])  13.4 us
    pallas_call x3, Pallas kernels, pack(): pl.pallas_call(body, out_shape=[jax.ShapeDtypeStruct((len(group), per) +...  10.1 us
    all_to_all x1, starting transfers between devices, local(): lax.all_to_all(bulk_out, 'seq', split_axis=0, concat_axis=0, tiled=True)  7.48 us
    ppermute x10, waiting for transfers between devices, to_hop(): return lax.ppermute(value, 'seq', [(d, d ^ hop) for d in range(peers)])  7.24 us
    ppermute x2, waiting for transfers between devices, from_peer(): return lax.ppermute(value, 'tp', [((d + t) % ways, d) for d in range(ways)])  6.88 us
    pallas_call x1, Pallas kernels, place(): pl.pallas_call(body, out_shape=jax.ShapeDtypeStruct(shape, bulk.dtype), i...  6.19 us
  transfers between devices with their start and end apart: 14, of which 6 were waited for; matrix products, arithmetic and copies ran while one was open for 2% of the time, Pallas kernels for 43%

profile of v4, /device:TPU:19, one launch (start us, length us, event | category | flops | bytes accessed | tf_op | source)
XLA Modules:
  0.0 124.7 jit_solution(11130263560678919602)
XLA Ops:
  0.6 1.3 %collective-permute-start.1 = (bf16[512,1280]{1,0:T(8,128)(2,1)}, bf16[512,1280]{1,0:T(8,128)(2,1)S(1)}, u32[]{:S(2)}, u32[]{:S(2)}) collective-permute-start(bf16[512,1280]{1,0:T(8,128)(2,1)} %refs_6_), channel_id=1, source_target_pairs={{1,0},{0,1},{3,2},{2,3},{5,4},{4,5},{7,6},{6,7},{9,8},{8,9},{11,10... | collective-permute-start | bytes 3932168 | tf_op jit(solution)/shard_map/ppermute | solution.py:548
  1.9 2.7 %pack.3 = (bf16[2,2,1,2,80,128]{5,4,3,2,1,0:T(8,128)(2,1)}, bf16[2,2,1,2,80,128]{5,4,3,2,1,0:T(8,128)(2,1)}, bf16[2,2,1,2,80,128]{5,4,3,2,1,0:T(8,128)(2,1)}) custom-call(s32[1,16]{1,0:T(1,128)} %refs_0_.7, s32[1,16]{1,0:T(1,128)} %refs_1_.7, s32[1,2,16]{2,1,0:T(2,128)} %bitcast.6, bf16[32,4,2,80,128]{4,3,2,1,0:T(8,128)(2,1)} %refs_3_.6), custom_call_target="tpu_custom_call" | custom-call | tf_op jit(solution)/shard_map/pack/pallas_call | solution.py:105
  4.6 0.1 collective-permute-start.2
  4.7 2.3 %collective-permute-start.3 = (bf16[2,2,1,2,80,128]{5,4,3,2,1,0:T(8,128)(2,1)}, bf16[2,2,1,2,80,128]{5,4,3,2,1,0:T(8,128)(2,1)S(1)}, u32[]{:S(2)}, u32[]{:S(2)}) collective-permute-start(bf16[2,2,1,2,80,128]{5,4,3,2,1,0:T(8,128)(2,1)} %get-tuple-element.30), channel_id=1, source_target_pairs={{0,20},{2,22},{4,16},{6,18},{8,28},{10,30},{12,24},{14,26},{16,4},... | collective-permute-start | bytes 491528 | tf_op jit(solution)/shard_map/ppermute | solution.py:557
  7.0 1.2 collective-permute-start.4
  8.2 4.3 %pack.4.refs_4_ = bf16[16,2,3,2,80,128]{5,4,3,2,1,0:T(8,128)(2,1)} custom-call(s32[1,16]{1,0:T(1,128)} %refs_0_.7, s32[1,16]{1,0:T(1,128)} %refs_1_.7, s32[1,2,16]{2,1,0:T(2,128)} %bitcast.7, bf16[32,4,2,80,128]{4,3,2,1,0:T(8,128)(2,1)} %refs_3_.6, bf16[2,2,1,2,80,128]{5,4,3,2,1,0:T(8,128)(2,1)} %get-tuple-element.27.refs_4_), custom_call_target="tpu_custom_call" | custom-call | tf_op jit(solution)/shard_map/pack/pallas_call | solution.py:105
  12.6 0.3 collective-permute-start
  12.9 0.3 copy-done.7
  13.2 7.5 %all-to-all-start = ((bf16[16,2,3,2,80,128]{5,4,3,2,1,0:T(8,128)(2,1)}), bf16[16,2,3,2,80,128]{5,4,3,2,1,0:T(8,128)(2,1)}, u32[]{:S(2)}, u32[]{:S(2)}) async-start(bf16[16,2,3,2,80,128]{5,4,3,2,1,0:T(8,128)(2,1)} %pack.4.refs_4_), calls=%async_computation | async-start | bytes 7864320 | tf_op jit(solution)/shard_map/all_to_all | solution.py:578
  20.7 3.1 %pack.5 = (bf16[2,2,1,2,80,128]{5,4,3,2,1,0:T(8,128)(2,1)}, bf16[2,2,1,2,80,128]{5,4,3,2,1,0:T(8,128)(2,1)}, bf16[1,2,1,2,80,128]{5,4,3,2,1,0:T(8,128)(2,1)}, bf...) custom-call(s32[1,16]{1,0:T(1,128)} %refs_0_.7, ...), custom_call_target="tpu_custom_call" | custom-call | tf_op jit(solution)/shard_map/pack/pallas_call | solution.py:105
  23.8 0.0 collective-permute-done.2.refs_0_
  23.8 0.0 copy-start.1
  23.8 0.0 collective-permute-done.3.refs_1_
  23.9 0.0 collective-permute-done.4.refs_2_
  23.9 6.8 %collective-permute-done.1.refs_7_ = bf16[512,1280]{1,0:T(8,128)(2,1)S(1)} collective-permute-done((bf16[512,1280]{1,0:T(8,128)(2,1)}, bf16[512,1280]{1,0:T(8,128)(2,1)S(1)}, u32[]{:S(2)}, u32[]{:S(2)}) %collective-permute-start.1) | collective-permute-done | bytes 1310752 | tf_op jit(solution)/shard_map/ppermute | solution.py:548
  30.7 0.1 collective-permute-done.refs_5_
  30.8 0.9 copy-done.9
  31.7 35.6 %layer.1 = (f32[512,1280]{1,0:T(8,128)}, bf16[512,1280]{1,0:T(8,128)(2,1)}) custom-call(s32[1,16]{1,0:T(1,128)} %refs_0_.6, s32[1,16]{1,0:T(1,128)} %refs_1_.7, s32[1,2,16]{2,1,0:T(2,128)} %bitcast.9, f32[1,128]{1,0:T(1,128)} %constant.2.clone.refs_3_, bf16[1,1280]{1,0:T(2,128)(2,1)} %copy-done.7, bf16[1,1280]{1,0:T(2,128)(2,1)} %copy-done.15, ...), custom_call_target="tpu_custom_call" | custom-call | flops 671088640000 | bytes 13107200 | tf_op jit(solution)/shard_map/layer/pallas_call | solution.py:490
  67.3 0.0 copy-done.1
  67.3 0.0 copy-done.2
  67.3 0.0 copy-done.3
  67.3 1.3 %collective-permute-start.5 = (bf16[512,1280]{1,0:T(8,128)(2,1)}, bf16[512,1280]{1,0:T(8,128)(2,1)S(1)}, u32[]{:S(2)}, u32[]{:S(2)}) collective-permute-start(bf16[512,1280]{1,0:T(8,128)(2,1)} %get-tuple-element.41), channel_id=1, source_target_pairs={{0,1},{1,0},{2,3},{3,2},{4,5},{5,4},{6,7},{7,6},{8,9},{9,8},{10,11... | collective-permute-start | bytes 3932168 | tf_op jit(solution)/shard_map/ppermute | solution.py:551
  68.6 1.4 %collective-permute-start.10 = (bf16[2,2,1,2,80,128]{5,4,3,2,1,0:T(8,128)(2,1)}, bf16[2,2,1,2,80,128]{5,4,3,2,1,0:T(8,128)(2,1)S(1)}, u32[]{:S(2)}, u32[]{:S(2)}) collective-permute-start(bf16[2,2,1,2,80,128]{5,4,3,2,1,0:T(8,128)(2,1)} %get-tuple-element.49), channel_id=1, source_target_pairs={{0,8},{2,10},{4,12},{6,14},{8,0},{10,2},{12,4},{14,6},{16,24},{18,... | collective-permute-start | bytes 491528 | tf_op jit(solution)/shard_map/ppermute | solution.py:557
  70.1 0.1 collective-permute-start.11
  70.2 24.8 %collective-permute-done.5 = bf16[512,1280]{1,0:T(8,128)(2,1)S(1)} collective-permute-done((bf16[512,1280]{1,0:T(8,128)(2,1)}, bf16[512,1280]{1,0:T(8,128)(2,1)S(1)}, u32[]{:S(2)}, u32[]{:S(2)}) %collective-permute-start.5) | collective-permute-done | bytes 1310752 | tf_op jit(solution)/shard_map/ppermute | solution.py:551
  95.0 3.1 %add_convert_fusion.refs_6_ = bf16[512,1280]{1,0:T(8,128)(2,1)} fusion(f32[512,1280]{1,0:T(8,128)} %get-tuple-element.33, bf16[512,1280]{1,0:T(8,128)(2,1)S(1)} %collective-permute-done.5), kind=kLoop, calls=%fused_computation | loop fusion | flops 1966080 | bytes 5242880 | tf_op jit(solution)/shard_map/convert_element_type | solution.py:593
  98.1 0.0 collective-permute-done.10.refs_3_
  98.2 0.0 collective-permute-done.11.refs_4_
  98.2 0.0 copy-start.5
  98.2 0.6 copy-done.4
  98.8 0.1 copy-done.5
  98.9 1.8 %relay.1 = bf16[6,2,1,2,80,128]{5,4,3,2,1,0:T(8,128)(2,1)} custom-call(bf16[2,2,1,2,80,128]{5,4,3,2,1,0:T(8,128)(2,1)} %copy-done.1, bf16[2,2,1,2,80,128]{5,4,3,2,1,0:T(8,128)(2,1)} %copy-done.2, bf16[2,2,1,2,80,128]{5,4,3,2,1,0:T(8,128)(2,1)} %copy-done.3, bf16[2,2,1,2,80,128]{5,4,3,2,1,0:T(8,128)(2,1)} %copy-done.4, ...), custom_call_target="tpu_custom_call" | custom-call | tf_op jit(solution)/shard_map/relay/pallas_call | solution.py:135
  100.7 3.8 %collective-permute-start.12 = (bf16[6,2,1,2,80,128]{5,4,3,2,1,0:T(8,128)(2,1)}, bf16[6,2,1,2,80,128]{5,4,3,2,1,0:T(8,128)(2,1)S(1)}, u32[]{:S(2)}, u32[]{:S(2)}) collective-permute-start(bf16[6,2,1,2,80,128]{5,4,3,2,1,0:T(8,128)(2,1)} %relay.1), channel_id=1, source_target_pairs={{0,2},{2,0},{4,6},{6,4},{8,10},{10,8},{12,14},{14,12},{16,18},{18,... | collective-permute-start | bytes 1474568 | tf_op jit(solution)/shard_map/ppermute | solution.py:557
  104.5 0.0 copy-done.14
  104.5 1.0 collective-permute-start.6
  105.6 0.7 collective-permute-start.7
  106.3 0.0 collective-permute-start.8
  106.3 0.0 copy-done.11
  106.3 2.7 %collective-permute-start.9 = (bf16[1,2,1,2,80,128]{5,4,3,2,1,0:T(8,128)(2,1)S(1)}, bf16[1,2,1,2,80,128]{5,4,3,2,1,0:T(8,128)(2,1)S(1)}, u32[]{:S(2)}, u32[]{:S(2)}) collective-permute-start(bf16[1,2,1,2,80,128]{5,4,3,2,1,0:T(8,128)(2,1)S(1)} %copy-done.11), channel_id=1, source_target_pairs={{0,30},{2,28},{4,26},{6,24},{8,22},{10,20},{12,18},{14,16},{16,14}... | collective-permute-start | bytes 245768 | tf_op jit(solution)/shard_map/ppermute | solution.py:557
  109.0 0.0 collective-permute-done.12.refs_6_
  109.0 0.0 all-to-all-done.refs_7_
  109.0 0.8 copy-done.6
  109.8 6.2 %place.1.refs_4_ = bf16[32,4,2,80,128]{4,3,2,1,0:T(8,128)(2,1)} custom-call(s32[1,2,16]{2,1,0:T(2,128)} %bitcast.4, bf16[2,2,1,2,80,128]{5,4,3,2,1,0:T(8,128)(2,1)} %copy-done.1, bf16[2,2,1,2,80,128]{5,4,3,2,1,0:T(8,128)(2,1)} %copy-done.2, bf16[2,2,1,2,80,128]{5,4,3,2,1,0:T(8,128)(2,1)} %copy-done.3, bf16[2,2,1,2,80,128]{5,4,3,2,1,0:T(8,128)(2,1)} %copy-done.4, ...), custom_call_target="tpu_custom_call" | custom-call | tf_op jit(solution)/shard_map/place/pallas_call | solution.py:196
  115.9 0.0 collective-permute-done.6.refs_0_
  116.0 2.0 %collective-permute-done.7.refs_1_ = bf16[1,2,1,2,80,128]{5,4,3,2,1,0:T(8,128)(2,1)S(1)} collective-permute-done((bf16[1,2,1,2,80,128]{5,4,3,2,1,0:T(8,128)(2,1)S(1)}, bf16[1,2,1,2,80,128]{5,4,3,2,1,0:T(8,128)(2,1)S(1)}, u32[]{:S(2)}, u32[]{:S(2)}) %collective-permute-start.7) | collective-permute-done | bytes 81952 | tf_op jit(solution)/shard_map/ppermute | solution.py:557
  118.0 3.3 %collective-permute-done.8.refs_2_ = bf16[1,2,1,2,80,128]{5,4,3,2,1,0:T(8,128)(2,1)S(1)} collective-permute-done((bf16[1,2,1,2,80,128]{5,4,3,2,1,0:T(8,128)(2,1)S(1)}, bf16[1,2,1,2,80,128]{5,4,3,2,1,0:T(8,128)(2,1)S(1)}, u32[]{:S(2)}, u32[]{:S(2)}) %collective-permute-start.8) | collective-permute-done | bytes 81952 | tf_op jit(solution)/shard_map/ppermute | solution.py:557
  121.2 1.9 %collective-permute-done.9.refs_3_ = bf16[1,2,1,2,80,128]{5,4,3,2,1,0:T(8,128)(2,1)S(1)} collective-permute-done((bf16[1,2,1,2,80,128]{5,4,3,2,1,0:T(8,128)(2,1)S(1)}, bf16[1,2,1,2,80,128]{5,4,3,2,1,0:T(8,128)(2,1)S(1)}, u32[]{:S(2)}, u32[]{:S(2)}) %collective-permute-start.9) | collective-permute-done | bytes 81952 | tf_op jit(solution)/shard_map/ppermute | solution.py:557
  123.2 1.3 %place_last.1 = bf16[32,4,2,80,128]{4,3,2,1,0:T(8,128)(2,1)} custom-call(s32[1,2,16]{2,1,0:T(2,128)S(1)} %bitcast.5, bf16[1,2,1,2,80,128]{5,4,3,2,1,0:T(8,128)(2,1)S(1)} %collective-permute-done.6.refs_0_, bf16[1,2,1,2,80,128]{5,4,3,2,1,0:T(8,128)(2,1)S(1)} %collective-permute-done.7.refs_1_, ...), custom_call_target="tpu_custom_call", output_to_operand_aliasing={{}: (5, {})} | custom-call | tf_op jit(solution)/shard_map/place_last/pallas_call | solution.py:233
  (21 shorter events, 0.0 us)
Async XLA Ops:
  0.6 30.0 %collective-permute-start.1 = (bf16[512,1280]{1,0:T(8,128)(2,1)}, bf16[512,1280]{1,0:T(8,128)(2,1)S(1)}, u32[]{:S(2)}, u32[]{:S(2)}) collective-permute-start(bf16[512,1280]{1,0:T(8,128)(2,1)} %refs_6_), channel_id=1, source_target_pairs={{1,0},{0,1},{3,2},{2,3},{5,4},{4,5},{7,6},{6,7},{9,8},{8,9},{11,10... | collective-permute-start | bytes 3932168 | tf_op jit(solution)/shard_map/ppermute | solution.py:548
  4.6 19.2 %collective-permute-start.2 = (bf16[2,2,1,2,80,128]{5,4,3,2,1,0:T(8,128)(2,1)}, bf16[2,2,1,2,80,128]{5,4,3,2,1,0:T(8,128)(2,1)S(1)}, u32[]{:S(2)}, u32[]{:S(2)}) collective-permute-start(bf16[2,2,1,2,80,128]{5,4,3,2,1,0:T(8,128)(2,1)} %get-tuple-element.29), channel_id=1, source_target_pairs={{0,16},{2,18},{4,20},{6,22},{8,24},{10,26},{12,28},{14,30},{16,0},... | collective-permute-start | bytes 491528 | tf_op jit(solution)/shard_map/ppermute | solution.py:557
  4.7 19.1 %collective-permute-start.3 = (bf16[2,2,1,2,80,128]{5,4,3,2,1,0:T(8,128)(2,1)}, bf16[2,2,1,2,80,128]{5,4,3,2,1,0:T(8,128)(2,1)S(1)}, u32[]{:S(2)}, u32[]{:S(2)}) collective-permute-start(bf16[2,2,1,2,80,128]{5,4,3,2,1,0:T(8,128)(2,1)} %get-tuple-element.30), channel_id=1, source_target_pairs={{0,20},{2,22},{4,16},{6,18},{8,28},{10,30},{12,24},{14,26},{16,4},... | collective-permute-start | bytes 491528 | tf_op jit(solution)/shard_map/ppermute | solution.py:557
  7.0 5.5 %copy-start.8 = (bf16[1280]{0:T(1024)(128)(2,1)S(1)}, bf16[1280]{0:T(1024)(128)(2,1)}, u32[]{:S(2)}) copy-start(bf16[1280]{0:T(1024)(128)(2,1)} %param.14) | copy-start | bytes 7684
  7.0 16.8 %collective-permute-start.4 = (bf16[2,2,1,2,80,128]{5,4,3,2,1,0:T(8,128)(2,1)}, bf16[2,2,1,2,80,128]{5,4,3,2,1,0:T(8,128)(2,1)S(1)}, u32[]{:S(2)}, u32[]{:S(2)}) collective-permute-start(bf16[2,2,1,2,80,128]{5,4,3,2,1,0:T(8,128)(2,1)} %get-tuple-element.27.refs_4_), channel_id=1, source_target_pairs={{0,4},{2,6},{4,0},{6,2},{8,12},{10,14},{12,8},{14,10},{16,20},{18,... | collective-permute-start | bytes 491528 | tf_op jit(solution)/shard_map/ppermute | solution.py:557
  12.6 0.6 copy-start.7
  12.6 18.2 %collective-permute-start = (bf16[1,1280]{1,0:T(2,128)(2,1)S(1)}, bf16[1,1280]{1,0:T(2,128)(2,1)S(1)}, u32[]{:S(2)}, u32[]{:S(2)}) collective-permute-start(bf16[1,1280]{1,0:T(2,128)(2,1)S(1)} %broadcast_in_dim.3.refs_4_), channel_id=1, source_target_pairs={{1,0},{0,1},{3,2},{2,3},{5,4},{4,5},{7,6},{6,7},{9,8},{8,9},{11,10... | collective-permute-start | bytes 7688 | tf_op jit(solution)/shard_map/ppermute | solution.py:548
  13.2 95.8 %all-to-all-start = ((bf16[16,2,3,2,80,128]{5,4,3,2,1,0:T(8,128)(2,1)}), bf16[16,2,3,2,80,128]{5,4,3,2,1,0:T(8,128)(2,1)}, u32[]{:S(2)}, u32[]{:S(2)}) async-start(bf16[16,2,3,2,80,128]{5,4,3,2,1,0:T(8,128)(2,1)} %pack.4.refs_4_), calls=%async_computation | async-start | bytes 7864320 | tf_op jit(solution)/shard_map/all_to_all | solution.py:578
  23.8 43.5 %copy-start.1 = (bf16[2,2,1,2,80,128]{5,4,3,2,1,0:T(8,128)(2,1)}, bf16[2,2,1,2,80,128]{5,4,3,2,1,0:T(8,128)(2,1)S(1)}, u32[]{:S(2)}) copy-start(bf16[2,2,1,2,80,128]{5,4,3,2,1,0:T(8,128)(2,1)S(1)} %collective-permute-done.2.refs_0_) | copy-start | bytes 491524
  23.8 43.5 %copy-start.2 = (bf16[2,2,1,2,80,128]{5,4,3,2,1,0:T(8,128)(2,1)}, bf16[2,2,1,2,80,128]{5,4,3,2,1,0:T(8,128)(2,1)S(1)}, u32[]{:S(2)}) copy-start(bf16[2,2,1,2,80,128]{5,4,3,2,1,0:T(8,128)(2,1)S(1)} %collective-permute-done.3.refs_1_) | copy-start | bytes 491524
  23.9 43.5 %copy-start.3 = (bf16[2,2,1,2,80,128]{5,4,3,2,1,0:T(8,128)(2,1)}, bf16[2,2,1,2,80,128]{5,4,3,2,1,0:T(8,128)(2,1)S(1)}, u32[]{:S(2)}) copy-start(bf16[2,2,1,2,80,128]{5,4,3,2,1,0:T(8,128)(2,1)S(1)} %collective-permute-done.4.refs_2_) | copy-start | bytes 491524
  30.7 1.1 copy-start.9
  30.8 0.9 copy-start.15
  31.7 38.4 %copy-start.10 = (bf16[2,2,1,2,80,128]{5,4,3,2,1,0:T(8,128)(2,1)S(1)}, bf16[2,2,1,2,80,128]{5,4,3,2,1,0:T(8,128)(2,1)}, u32[]{:S(2)}) copy-start(bf16[2,2,1,2,80,128]{5,4,3,2,1,0:T(8,128)(2,1)} %get-tuple-element.50) | copy-start | bytes 491524
  67.3 27.7 %collective-permute-start.5 = (bf16[512,1280]{1,0:T(8,128)(2,1)}, bf16[512,1280]{1,0:T(8,128)(2,1)S(1)}, u32[]{:S(2)}, u32[]{:S(2)}) collective-permute-start(bf16[512,1280]{1,0:T(8,128)(2,1)} %get-tuple-element.41), channel_id=1, source_target_pairs={{0,1},{1,0},{2,3},{3,2},{4,5},{5,4},{6,7},{7,6},{8,9},{9,8},{10,11... | collective-permute-start | bytes 3932168 | tf_op jit(solution)/shard_map/ppermute | solution.py:551
  68.6 29.5 %collective-permute-start.10 = (bf16[2,2,1,2,80,128]{5,4,3,2,1,0:T(8,128)(2,1)}, bf16[2,2,1,2,80,128]{5,4,3,2,1,0:T(8,128)(2,1)S(1)}, u32[]{:S(2)}, u32[]{:S(2)}) collective-permute-start(bf16[2,2,1,2,80,128]{5,4,3,2,1,0:T(8,128)(2,1)} %get-tuple-element.49), channel_id=1, source_target_pairs={{0,8},{2,10},{4,12},{6,14},{8,0},{10,2},{12,4},{14,6},{16,24},{18,... | collective-permute-start | bytes 491528 | tf_op jit(solution)/shard_map/ppermute | solution.py:557
  70.1 28.1 %collective-permute-start.11 = (bf16[2,2,1,2,80,128]{5,4,3,2,1,0:T(8,128)(2,1)S(1)}, bf16[2,2,1,2,80,128]{5,4,3,2,1,0:T(8,128)(2,1)S(1)}, u32[]{:S(2)}, u32[]{:S(2)}) collective-permute-start(bf16[2,2,1,2,80,128]{5,4,3,2,1,0:T(8,128)(2,1)S(1)} %copy-done.10), channel_id=1, source_target_pairs={{0,12},{2,14},{4,8},{6,10},{8,4},{10,6},{12,0},{14,2},{16,28},{18,... | collective-permute-start | bytes 491528 | tf_op jit(solution)/shard_map/ppermute | solution.py:557
  98.1 6.4 %copy-start.14 = (bf16[1,2,1,2,80,128]{5,4,3,2,1,0:T(8,128)(2,1)S(1)}, bf16[1,2,1,2,80,128]{5,4,3,2,1,0:T(8,128)(2,1)}, u32[]{:S(2)}) copy-start(bf16[1,2,1,2,80,128]{5,4,3,2,1,0:T(8,128)(2,1)} %get-tuple-element.42) | copy-start | bytes 245764
  98.1 7.4 %copy-start.13 = (bf16[1,2,1,2,80,128]{5,4,3,2,1,0:T(8,128)(2,1)S(1)}, bf16[1,2,1,2,80,128]{5,4,3,2,1,0:T(8,128)(2,1)}, u32[]{:S(2)}) copy-start(bf16[1,2,1,2,80,128]{5,4,3,2,1,0:T(8,128)(2,1)} %get-tuple-element.43) | copy-start | bytes 245764
  98.1 8.1 %copy-start.12 = (bf16[1,2,1,2,80,128]{5,4,3,2,1,0:T(8,128)(2,1)S(1)}, bf16[1,2,1,2,80,128]{5,4,3,2,1,0:T(8,128)(2,1)}, u32[]{:S(2)}) copy-start(bf16[1,2,1,2,80,128]{5,4,3,2,1,0:T(8,128)(2,1)} %get-tuple-element.44) | copy-start | bytes 245764
  98.1 8.1 %copy-start.11 = (bf16[1,2,1,2,80,128]{5,4,3,2,1,0:T(8,128)(2,1)S(1)}, bf16[1,2,1,2,80,128]{5,4,3,2,1,0:T(8,128)(2,1)}, u32[]{:S(2)}) copy-start(bf16[1,2,1,2,80,128]{5,4,3,2,1,0:T(8,128)(2,1)} %get-tuple-element.45) | copy-start | bytes 245764
  98.2 0.7 copy-start.4
  98.2 0.7 copy-start.5
  100.7 8.3 %collective-permute-start.12 = (bf16[6,2,1,2,80,128]{5,4,3,2,1,0:T(8,128)(2,1)}, bf16[6,2,1,2,80,128]{5,4,3,2,1,0:T(8,128)(2,1)S(1)}, u32[]{:S(2)}, u32[]{:S(2)}) collective-permute-start(bf16[6,2,1,2,80,128]{5,4,3,2,1,0:T(8,128)(2,1)} %relay.1), channel_id=1, source_target_pairs={{0,2},{2,0},{4,6},{6,4},{8,10},{10,8},{12,14},{14,12},{16,18},{18,... | collective-permute-start | bytes 1474568 | tf_op jit(solution)/shard_map/ppermute | solution.py:557
  104.5 11.4 %collective-permute-start.6 = (bf16[1,2,1,2,80,128]{5,4,3,2,1,0:T(8,128)(2,1)S(1)}, bf16[1,2,1,2,80,128]{5,4,3,2,1,0:T(8,128)(2,1)S(1)}, u32[]{:S(2)}, u32[]{:S(2)}) collective-permute-start(bf16[1,2,1,2,80,128]{5,4,3,2,1,0:T(8,128)(2,1)S(1)} %copy-done.14), channel_id=1, source_target_pairs={{0,24},{2,26},{4,28},{6,30},{8,16},{10,18},{12,20},{14,22},{16,8},... | collective-permute-start | bytes 245768 | tf_op jit(solution)/shard_map/ppermute | solution.py:557
  105.6 12.4 %collective-permute-start.7 = (bf16[1,2,1,2,80,128]{5,4,3,2,1,0:T(8,128)(2,1)S(1)}, bf16[1,2,1,2,80,128]{5,4,3,2,1,0:T(8,128)(2,1)S(1)}, u32[]{:S(2)}, u32[]{:S(2)}) collective-permute-start(bf16[1,2,1,2,80,128]{5,4,3,2,1,0:T(8,128)(2,1)S(1)} %copy-done.13), channel_id=1, source_target_pairs={{0,26},{2,24},{4,30},{6,28},{8,18},{10,16},{12,22},{14,20},{16,10}... | collective-permute-start | bytes 245768 | tf_op jit(solution)/shard_map/ppermute | solution.py:557
  106.3 15.0 %collective-permute-start.8 = (bf16[1,2,1,2,80,128]{5,4,3,2,1,0:T(8,128)(2,1)S(1)}, bf16[1,2,1,2,80,128]{5,4,3,2,1,0:T(8,128)(2,1)S(1)}, u32[]{:S(2)}, u32[]{:S(2)}) collective-permute-start(bf16[1,2,1,2,80,128]{5,4,3,2,1,0:T(8,128)(2,1)S(1)} %copy-done.12), channel_id=1, source_target_pairs={{0,28},{2,30},{4,24},{6,26},{8,20},{10,22},{12,16},{14,18},{16,12}... | collective-permute-start | bytes 245768 | tf_op jit(solution)/shard_map/ppermute | solution.py:557
  106.3 16.9 %collective-permute-start.9 = (bf16[1,2,1,2,80,128]{5,4,3,2,1,0:T(8,128)(2,1)S(1)}, bf16[1,2,1,2,80,128]{5,4,3,2,1,0:T(8,128)(2,1)S(1)}, u32[]{:S(2)}, u32[]{:S(2)}) collective-permute-start(bf16[1,2,1,2,80,128]{5,4,3,2,1,0:T(8,128)(2,1)S(1)} %copy-done.11), channel_id=1, source_target_pairs={{0,30},{2,28},{4,26},{6,24},{8,22},{10,20},{12,18},{14,16},{16,14}... | collective-permute-start | bytes 245768 | tf_op jit(solution)/shard_map/ppermute | solution.py:557
  109.0 0.8 copy-start.6
  109.8 13.4 %copy-start = (s32[1,16,2]{1,2,0:T(2,128)S(1)}, s32[1,16,2]{1,2,0:T(2,128)}, u32[]{:S(2)}) copy-start(s32[1,16,2]{1,2,0:T(2,128)} %param.24) | copy-start | bytes 388

commit v5 on v3

--- a/solution.py
+++ b/solution.py
@@ -566,17 +566,18 @@
     sends, middle_out, late_out = barrier((sends, middle_out, late_out))
     middle_in = [to_hop(value, 2 * k) for k, value in zip(middle, middle_out)]
     late_in = [to_hop(value, hop) for hop, value in zip(late, late_out)]
-    total = base
-    for t in range(1, ways):
-        total = total + to_peer(sends[t - 1], t).astype(jnp.float32)
-    hidden = total.astype(jnp.bfloat16)
-
+    got = [to_peer(sends[t - 1], t) for t in range(1, ways)]
     arrived = begin_in + middle_in
-    other = to_hop(relay(arrived + [own], [hidden]), 1)
+    other = to_hop(relay(arrived + [own], got), 1)
     reach = [2 * k for k in begin + middle] + [0]
     sources = [(i, 0, hop) for i, hop in enumerate(reach)]
     sources += [(len(reach), i, hop + 1) for i, hop in enumerate(reach)]
     shape = prior_cache.shape
+    got, other = barrier((got, other))
+    total = base
+    for value in got:
+        total = total + value.astype(jnp.float32)
+    hidden = total.astype(jnp.bfloat16)
     made = place(dest_table, arrived + [own, other], sources, shape, 0)
     bulk = [(0, s, s) for s in range(peers)]
     made = place(dest_table, [bulk_in], bulk, shape, few, [made], absolute=True)

time: 126 us -> 125 us (level)
  starting transfers between devices: 22.2 us -> 24.4 us
  waiting for transfers between devices: 38.5 us -> 37.2 us
    ppermute x1, waiting for transfers between devices: 26.5 us -> 0.5 us  [to_peer(): return lax.ppermute(value, 'tp', [(d, (d + t) % ways) for d in range(ways)])]
    ppermute x10, waiting for transfers between devices: 5.26 us -> 30 us  [to_hop(): return lax.ppermute(value, 'seq', [(d, d ^ hop) for d in range(peers)])]
    ppermute x10, starting transfers between devices: 11.7 us -> 13.9 us  [to_hop(): return lax.ppermute(value, 'seq', [(d, d ^ hop) for d in range(peers)])]
    unnamed x32 -> x34, local copies, waits for them, and re-layouts: 2.85 us -> 2.35 us
  transfers between devices with their start and end apart: 14 -> 14, of which waited for: 6 -> 7; matrix products, arithmetic and copies ran while one was open for 2% -> 3% of each run, Pallas kernels for 45% -> 44%
where the time goes in v5:
time: 125 us
  Pallas kernels  56.2 us (45%)
  waiting for transfers between devices  37.2 us (30%)
  starting transfers between devices  24.4 us (20%)
  other arithmetic  3.6 us (3%)
  local copies, waits for them, and re-layouts  2.35 us (2%)
    pallas_call x1, Pallas kernels, layer(): pl.pallas_call(functools.partial(layer_body, ways, q_heads, kv_heads), ou...  35 us
    ppermute x10, waiting for transfers between devices, to_hop(): return lax.ppermute(value, 'seq', [(d, d ^ hop) for d in range(peers)])  30 us
    ppermute x10, starting transfers between devices, to_hop(): return lax.ppermute(value, 'seq', [(d, d ^ hop) for d in range(peers)])  13.9 us
    pallas_call x3, Pallas kernels, pack(): pl.pallas_call(body, out_shape=[jax.ShapeDtypeStruct((len(group), per) +...  10.1 us
    pallas_call x2, Pallas kernels, place(): pl.pallas_call(body, out_shape=jax.ShapeDtypeStruct(shape, arrays[0].dtyp...  7.98 us
    all_to_all x1, starting transfers between devices, local(): lax.all_to_all(bulk_out, 'seq', split_axis=0, concat_axis=0, tiled=True)  7.63 us
    ppermute x2, waiting for transfers between devices, from_peer(): return lax.ppermute(value, 'tp', [((d + t) % ways, d) for d in range(ways)])  6.73 us
    convert_element_type x1, other arithmetic, local(): hidden = total.astype(jnp.bfloat16)  3.6 us
  transfers between devices with their start and end apart: 14, of which 7 were waited for; matrix products, arithmetic and copies ran while one was open for 3% of the time, Pallas kernels for 44%

profile of v5, /device:TPU:19, one launch (start us, length us, event | category | flops | bytes accessed | tf_op | source)
XLA Modules:
  0.0 124.8 jit_solution(15576353772163928518)
XLA Ops:
  0.6 1.3 %collective-permute-start.1 = (bf16[512,1280]{1,0:T(8,128)(2,1)}, bf16[512,1280]{1,0:T(8,128)(2,1)S(1)}, u32[]{:S(2)}, u32[]{:S(2)}) collective-permute-start(bf16[512,1280]{1,0:T(8,128)(2,1)} %refs_6_), channel_id=1, source_target_pairs={{1,0},{0,1},{3,2},{2,3},{5,4},{4,5},{7,6},{6,7},{9,8},{8,9},{11,10... | collective-permute-start | bytes 3932168 | tf_op jit(solution)/shard_map/ppermute | solution.py:528
  1.9 2.7 %pack.3 = (bf16[2,2,1,2,80,128]{5,4,3,2,1,0:T(8,128)(2,1)}, bf16[2,2,1,2,80,128]{5,4,3,2,1,0:T(8,128)(2,1)}, bf16[2,2,1,2,80,128]{5,4,3,2,1,0:T(8,128)(2,1)}) custom-call(s32[1,16]{1,0:T(1,128)} %refs_0_.7, s32[1,16]{1,0:T(1,128)} %refs_1_.7, s32[1,2,16]{2,1,0:T(2,128)} %bitcast.7, bf16[32,4,2,80,128]{4,3,2,1,0:T(8,128)(2,1)} %refs_3_.6), custom_call_target="tpu_custom_call" | custom-call | tf_op jit(solution)/shard_map/pack/pallas_call | solution.py:105
  4.6 0.1 collective-permute-start.2
  4.8 2.3 %collective-permute-start.3 = (bf16[2,2,1,2,80,128]{5,4,3,2,1,0:T(8,128)(2,1)}, bf16[2,2,1,2,80,128]{5,4,3,2,1,0:T(8,128)(2,1)S(1)}, u32[]{:S(2)}, u32[]{:S(2)}) collective-permute-start(bf16[2,2,1,2,80,128]{5,4,3,2,1,0:T(8,128)(2,1)} %get-tuple-element.32), channel_id=1, source_target_pairs={{0,20},{2,22},{4,16},{6,18},{8,28},{10,30},{12,24},{14,26},{16,4},... | collective-permute-start | bytes 491528 | tf_op jit(solution)/shard_map/ppermute | solution.py:537
  7.1 1.2 collective-permute-start.4
  8.3 4.3 %pack.4.refs_4_ = bf16[16,2,3,2,80,128]{5,4,3,2,1,0:T(8,128)(2,1)} custom-call(s32[1,16]{1,0:T(1,128)} %refs_0_.7, s32[1,16]{1,0:T(1,128)} %refs_1_.7, s32[1,2,16]{2,1,0:T(2,128)} %bitcast.8, bf16[32,4,2,80,128]{4,3,2,1,0:T(8,128)(2,1)} %refs_3_.6, bf16[2,2,1,2,80,128]{5,4,3,2,1,0:T(8,128)(2,1)} %get-tuple-element.29.refs_4_), custom_call_target="tpu_custom_call" | custom-call | tf_op jit(solution)/shard_map/pack/pallas_call | solution.py:105
  12.6 0.3 collective-permute-start
  12.9 0.3 copy-done.8
  13.2 7.6 %all-to-all-start = ((bf16[16,2,3,2,80,128]{5,4,3,2,1,0:T(8,128)(2,1)}), bf16[16,2,3,2,80,128]{5,4,3,2,1,0:T(8,128)(2,1)}, u32[]{:S(2)}, u32[]{:S(2)}) async-start(bf16[16,2,3,2,80,128]{5,4,3,2,1,0:T(8,128)(2,1)} %pack.4.refs_4_), calls=%async_computation | async-start | bytes 7864320 | tf_op jit(solution)/shard_map/all_to_all | solution.py:558
  20.8 3.2 %pack.5 = (bf16[2,2,1,2,80,128]{5,4,3,2,1,0:T(8,128)(2,1)}, bf16[2,2,1,2,80,128]{5,4,3,2,1,0:T(8,128)(2,1)}, bf16[1,2,1,2,80,128]{5,4,3,2,1,0:T(8,128)(2,1)}, bf...) custom-call(s32[1,16]{1,0:T(1,128)} %refs_0_.7, ...), custom_call_target="tpu_custom_call" | custom-call | tf_op jit(solution)/shard_map/pack/pallas_call | solution.py:105
  24.0 0.0 collective-permute-done.2.refs_0_
  24.0 0.0 collective-permute-done.3.refs_1_
  24.0 0.0 collective-permute-done.4.refs_2_
  24.0 6.6 %collective-permute-done.1.refs_7_ = bf16[512,1280]{1,0:T(8,128)(2,1)S(1)} collective-permute-done((bf16[512,1280]{1,0:T(8,128)(2,1)}, bf16[512,1280]{1,0:T(8,128)(2,1)S(1)}, u32[]{:S(2)}, u32[]{:S(2)}) %collective-permute-start.1) | collective-permute-done | bytes 1310752 | tf_op jit(solution)/shard_map/ppermute | solution.py:528
  30.7 0.1 collective-permute-done.refs_5_
  30.8 0.9 copy-done.10
  31.7 35.0 %layer.1 = (f32[512,1280]{1,0:T(8,128)}, bf16[512,1280]{1,0:T(8,128)(2,1)}) custom-call(s32[1,16]{1,0:T(1,128)} %refs_0_.6, s32[1,16]{1,0:T(1,128)} %refs_1_.7, s32[1,2,16]{2,1,0:T(2,128)} %bitcast.10, f32[1,128]{1,0:T(1,128)} %constant.2.clone.refs_3_, bf16[1,1280]{1,0:T(2,128)(2,1)} %copy-done.8, bf16[1,1280]{1,0:T(2,128)(2,1)} %copy-done.16, ...), custom_call_target="tpu_custom_call" | custom-call | flops 671088640000 | bytes 13107200 | tf_op jit(solution)/shard_map/layer/pallas_call | solution.py:470
  66.7 0.0 copy-done.2
  66.7 0.0 copy-done.3
  66.7 0.0 copy-done.4
  66.7 0.0 copy-start.13
  66.7 0.0 copy-start.12
  66.7 1.3 %collective-permute-start.5 = (bf16[512,1280]{1,0:T(8,128)(2,1)}, bf16[512,1280]{1,0:T(8,128)(2,1)S(1)}, u32[]{:S(2)}, u32[]{:S(2)}) collective-permute-start(bf16[512,1280]{1,0:T(8,128)(2,1)} %get-tuple-element.43), channel_id=1, source_target_pairs={{0,1},{1,0},{2,3},{3,2},{4,5},{5,4},{6,7},{7,6},{8,9},{9,8},{10,11... | collective-permute-start | bytes 3932168 | tf_op jit(solution)/shard_map/ppermute | solution.py:531
  68.0 2.0 %collective-permute-start.6 = (bf16[2,2,1,2,80,128]{5,4,3,2,1,0:T(8,128)(2,1)}, bf16[2,2,1,2,80,128]{5,4,3,2,1,0:T(8,128)(2,1)S(1)}, u32[]{:S(2)}, u32[]{:S(2)}) collective-permute-start(bf16[2,2,1,2,80,128]{5,4,3,2,1,0:T(8,128)(2,1)} %get-tuple-element.47), channel_id=1, source_target_pairs={{0,8},{2,10},{4,12},{6,14},{8,0},{10,2},{12,4},{14,6},{16,24},{18,... | collective-permute-start | bytes 491528 | tf_op jit(solution)/shard_map/ppermute | solution.py:537
  70.0 1.0 collective-permute-start.7
  71.0 19.1 %collective-permute-done.6.refs_3_ = bf16[2,2,1,2,80,128]{5,4,3,2,1,0:T(8,128)(2,1)S(1)} collective-permute-done((bf16[2,2,1,2,80,128]{5,4,3,2,1,0:T(8,128)(2,1)}, bf16[2,2,1,2,80,128]{5,4,3,2,1,0:T(8,128)(2,1)S(1)}, u32[]{:S(2)}, u32[]{:S(2)}) %collective-permute-start.6) | collective-permute-done | bytes 163872 | tf_op jit(solution)/shard_map/ppermute | solution.py:537
  90.1 5.2 %collective-permute-done.7.refs_4_ = bf16[2,2,1,2,80,128]{5,4,3,2,1,0:T(8,128)(2,1)S(1)} collective-permute-done((bf16[2,2,1,2,80,128]{5,4,3,2,1,0:T(8,128)(2,1)S(1)}, bf16[2,2,1,2,80,128]{5,4,3,2,1,0:T(8,128)(2,1)S(1)}, u32[]{:S(2)}, u32[]{:S(2)}) %collective-permute-start.7) | collective-permute-done | bytes 163872 | tf_op jit(solution)/shard_map/ppermute | solution.py:537
  95.3 0.5 collective-permute-done.5.refs_6_
  95.8 0.0 copy-done.5
  95.8 0.1 copy-done.6
  96.0 0.9 copy-done.1
  96.9 1.8 %relay.1 = bf16[6,2,1,2,80,128]{5,4,3,2,1,0:T(8,128)(2,1)} custom-call(bf16[2,2,1,2,80,128]{5,4,3,2,1,0:T(8,128)(2,1)} %copy-done.2, bf16[2,2,1,2,80,128]{5,4,3,2,1,0:T(8,128)(2,1)} %copy-done.3, bf16[2,2,1,2,80,128]{5,4,3,2,1,0:T(8,128)(2,1)} %copy-done.4, bf16[2,2,1,2,80,128]{5,4,3,2,1,0:T(8,128)(2,1)} %copy-done.5, ...), custom_call_target="tpu_custom_call" | custom-call | tf_op jit(solution)/shard_map/relay/pallas_call | solution.py:135
  98.7 2.5 %collective-permute-start.8 = (bf16[6,2,1,2,80,128]{5,4,3,2,1,0:T(8,128)(2,1)}, bf16[6,2,1,2,80,128]{5,4,3,2,1,0:T(8,128)(2,1)S(1)}, u32[]{:S(2)}, u32[]{:S(2)}) collective-permute-start(bf16[6,2,1,2,80,128]{5,4,3,2,1,0:T(8,128)(2,1)} %relay.1), channel_id=1, source_target_pairs={{0,2},{2,0},{4,6},{6,4},{8,10},{10,8},{12,14},{14,12},{16,18},{18,... | collective-permute-start | bytes 1474568 | tf_op jit(solution)/shard_map/ppermute | solution.py:537
  101.1 1.9 %collective-permute-start.9 = (bf16[1,2,1,2,80,128]{5,4,3,2,1,0:T(8,128)(2,1)S(1)}, bf16[1,2,1,2,80,128]{5,4,3,2,1,0:T(8,128)(2,1)S(1)}, u32[]{:S(2)}, u32[]{:S(2)}) collective-permute-start(bf16[1,2,1,2,80,128]{5,4,3,2,1,0:T(8,128)(2,1)S(1)} %copy-done.15), channel_id=1, source_target_pairs={{0,24},{2,26},{4,28},{6,30},{8,16},{10,18},{12,20},{14,22},{16,8},... | collective-permute-start | bytes 245768 | tf_op jit(solution)/shard_map/ppermute | solution.py:537
  103.0 0.0 collective-permute-start.10
  103.1 1.1 collective-permute-start.11
  104.2 1.9 %collective-permute-start.12 = (bf16[1,2,1,2,80,128]{5,4,3,2,1,0:T(8,128)(2,1)S(1)}, bf16[1,2,1,2,80,128]{5,4,3,2,1,0:T(8,128)(2,1)S(1)}, u32[]{:S(2)}, u32[]{:S(2)}) collective-permute-start(bf16[1,2,1,2,80,128]{5,4,3,2,1,0:T(8,128)(2,1)S(1)} %copy-done.12), channel_id=1, source_target_pairs={{0,30},{2,28},{4,26},{6,24},{8,22},{10,20},{12,18},{14,16},{16,14}... | collective-permute-start | bytes 245768 | tf_op jit(solution)/shard_map/ppermute | solution.py:537
  106.0 0.0 collective-permute-done.8.refs_6_
  106.0 3.6 %add_convert_fusion = bf16[512,1280]{1,0:T(8,128)(2,1)} fusion(f32[512,1280]{1,0:T(8,128)} %get-tuple-element.35, bf16[512,1280]{1,0:T(8,128)(2,1)} %copy-done.1), kind=kLoop, calls=%fused_computation | loop fusion | flops 1966080 | bytes 5242880 | tf_op jit(solution)/shard_map/convert_element_type | solution.py:580
  109.6 2.9 %place.2.refs_1_ = bf16[32,4,2,80,128]{4,3,2,1,0:T(8,128)(2,1)} custom-call(s32[1,2,16]{2,1,0:T(2,128)} %bitcast.4, bf16[2,2,1,2,80,128]{5,4,3,2,1,0:T(8,128)(2,1)} %copy-done.2, bf16[2,2,1,2,80,128]{5,4,3,2,1,0:T(8,128)(2,1)} %copy-done.3, bf16[2,2,1,2,80,128]{5,4,3,2,1,0:T(8,128)(2,1)} %copy-done.4, bf16[2,2,1,2,80,128]{5,4,3,2,1,0:T(8,128)(2,1)} %copy-done.5, ...), custom_call_target="tpu_custom_call" | custom-call | tf_op jit(solution)/shard_map/place/pallas_call | solution.py:178
  112.5 0.0 copy-start
  112.6 0.0 all-to-all-done.refs_0_
  112.6 5.1 %place.3.refs_4_ = bf16[32,4,2,80,128]{4,3,2,1,0:T(8,128)(2,1)} custom-call(s32[1,2,16]{2,1,0:T(2,128)} %bitcast.5, bf16[16,2,3,2,80,128]{5,4,3,2,1,0:T(8,128)(2,1)} %all-to-all-done.refs_0_, bf16[32,4,2,80,128]{4,3,2,1,0:T(8,128)(2,1)} %place.2.refs_1_), custom_call_target="tpu_custom_call", output_to_operand_aliasing={{}: (2, {})} | custom-call | tf_op jit(solution)/shard_map/place/pallas_call | solution.py:178
  117.6 0.0 collective-permute-done.9.refs_0_
  117.7 0.0 collective-permute-done.10.refs_1_
  117.7 3.7 %collective-permute-done.11.refs_2_ = bf16[1,2,1,2,80,128]{5,4,3,2,1,0:T(8,128)(2,1)S(1)} collective-permute-done((bf16[1,2,1,2,80,128]{5,4,3,2,1,0:T(8,128)(2,1)S(1)}, bf16[1,2,1,2,80,128]{5,4,3,2,1,0:T(8,128)(2,1)S(1)}, u32[]{:S(2)}, u32[]{:S(2)}) %collective-permute-start.11) | collective-permute-done | bytes 81952 | tf_op jit(solution)/shard_map/ppermute | solution.py:537
  121.4 1.9 %collective-permute-done.12.refs_3_ = bf16[1,2,1,2,80,128]{5,4,3,2,1,0:T(8,128)(2,1)S(1)} collective-permute-done((bf16[1,2,1,2,80,128]{5,4,3,2,1,0:T(8,128)(2,1)S(1)}, bf16[1,2,1,2,80,128]{5,4,3,2,1,0:T(8,128)(2,1)S(1)}, u32[]{:S(2)}, u32[]{:S(2)}) %collective-permute-start.12) | collective-permute-done | bytes 81952 | tf_op jit(solution)/shard_map/ppermute | solution.py:537
  123.3 1.3 %place_last.1 = bf16[32,4,2,80,128]{4,3,2,1,0:T(8,128)(2,1)} custom-call(s32[1,2,16]{2,1,0:T(2,128)S(1)} %bitcast.6, bf16[1,2,1,2,80,128]{5,4,3,2,1,0:T(8,128)(2,1)S(1)} %collective-permute-done.9.refs_0_, bf16[1,2,1,2,80,128]{5,4,3,2,1,0:T(8,128)(2,1)S(1)} %collective-permute-done.10.refs_1_, ...), custom_call_target="tpu_custom_call", output_to_operand_aliasing={{}: (5, {})} | custom-call | tf_op jit(solution)/shard_map/place_last/pallas_call | solution.py:213
  (24 shorter events, 0.0 us)
Async XLA Ops:
  0.6 30.0 %collective-permute-start.1 = (bf16[512,1280]{1,0:T(8,128)(2,1)}, bf16[512,1280]{1,0:T(8,128)(2,1)S(1)}, u32[]{:S(2)}, u32[]{:S(2)}) collective-permute-start(bf16[512,1280]{1,0:T(8,128)(2,1)} %refs_6_), channel_id=1, source_target_pairs={{1,0},{0,1},{3,2},{2,3},{5,4},{4,5},{7,6},{6,7},{9,8},{8,9},{11,10... | collective-permute-start | bytes 3932168 | tf_op jit(solution)/shard_map/ppermute | solution.py:528
  4.6 19.3 %collective-permute-start.2 = (bf16[2,2,1,2,80,128]{5,4,3,2,1,0:T(8,128)(2,1)}, bf16[2,2,1,2,80,128]{5,4,3,2,1,0:T(8,128)(2,1)S(1)}, u32[]{:S(2)}, u32[]{:S(2)}) collective-permute-start(bf16[2,2,1,2,80,128]{5,4,3,2,1,0:T(8,128)(2,1)} %get-tuple-element.31), channel_id=1, source_target_pairs={{0,16},{2,18},{4,20},{6,22},{8,24},{10,26},{12,28},{14,30},{16,0},... | collective-permute-start | bytes 491528 | tf_op jit(solution)/shard_map/ppermute | solution.py:537
  4.8 19.2 %collective-permute-start.3 = (bf16[2,2,1,2,80,128]{5,4,3,2,1,0:T(8,128)(2,1)}, bf16[2,2,1,2,80,128]{5,4,3,2,1,0:T(8,128)(2,1)S(1)}, u32[]{:S(2)}, u32[]{:S(2)}) collective-permute-start(bf16[2,2,1,2,80,128]{5,4,3,2,1,0:T(8,128)(2,1)} %get-tuple-element.32), channel_id=1, source_target_pairs={{0,20},{2,22},{4,16},{6,18},{8,28},{10,30},{12,24},{14,26},{16,4},... | collective-permute-start | bytes 491528 | tf_op jit(solution)/shard_map/ppermute | solution.py:537
  7.0 5.5 %copy-start.9 = (bf16[1280]{0:T(1024)(128)(2,1)S(1)}, bf16[1280]{0:T(1024)(128)(2,1)}, u32[]{:S(2)}) copy-start(bf16[1280]{0:T(1024)(128)(2,1)} %param.14) | copy-start | bytes 7684
  7.1 17.0 %collective-permute-start.4 = (bf16[2,2,1,2,80,128]{5,4,3,2,1,0:T(8,128)(2,1)}, bf16[2,2,1,2,80,128]{5,4,3,2,1,0:T(8,128)(2,1)S(1)}, u32[]{:S(2)}, u32[]{:S(2)}) collective-permute-start(bf16[2,2,1,2,80,128]{5,4,3,2,1,0:T(8,128)(2,1)} %get-tuple-element.29.refs_4_), channel_id=1, source_target_pairs={{0,4},{2,6},{4,0},{6,2},{8,12},{10,14},{12,8},{14,10},{16,20},{18,... | collective-permute-start | bytes 491528 | tf_op jit(solution)/shard_map/ppermute | solution.py:537
  12.6 0.6 copy-start.8
  12.6 18.2 %collective-permute-start = (bf16[1,1280]{1,0:T(2,128)(2,1)S(1)}, bf16[1,1280]{1,0:T(2,128)(2,1)S(1)}, u32[]{:S(2)}, u32[]{:S(2)}) collective-permute-start(bf16[1,1280]{1,0:T(2,128)(2,1)S(1)} %broadcast_in_dim.3.refs_4_), channel_id=1, source_target_pairs={{1,0},{0,1},{3,2},{2,3},{5,4},{4,5},{7,6},{6,7},{9,8},{8,9},{11,10... | collective-permute-start | bytes 7688 | tf_op jit(solution)/shard_map/ppermute | solution.py:528
  13.2 99.4 %all-to-all-start = ((bf16[16,2,3,2,80,128]{5,4,3,2,1,0:T(8,128)(2,1)}), bf16[16,2,3,2,80,128]{5,4,3,2,1,0:T(8,128)(2,1)}, u32[]{:S(2)}, u32[]{:S(2)}) async-start(bf16[16,2,3,2,80,128]{5,4,3,2,1,0:T(8,128)(2,1)} %pack.4.refs_4_), calls=%async_computation | async-start | bytes 7864320 | tf_op jit(solution)/shard_map/all_to_all | solution.py:558
  24.0 42.7 %copy-start.2 = (bf16[2,2,1,2,80,128]{5,4,3,2,1,0:T(8,128)(2,1)}, bf16[2,2,1,2,80,128]{5,4,3,2,1,0:T(8,128)(2,1)S(1)}, u32[]{:S(2)}) copy-start(bf16[2,2,1,2,80,128]{5,4,3,2,1,0:T(8,128)(2,1)S(1)} %collective-permute-done.2.refs_0_) | copy-start | bytes 491524
  24.0 42.7 %copy-start.3 = (bf16[2,2,1,2,80,128]{5,4,3,2,1,0:T(8,128)(2,1)}, bf16[2,2,1,2,80,128]{5,4,3,2,1,0:T(8,128)(2,1)S(1)}, u32[]{:S(2)}) copy-start(bf16[2,2,1,2,80,128]{5,4,3,2,1,0:T(8,128)(2,1)S(1)} %collective-permute-done.3.refs_1_) | copy-start | bytes 491524
  24.0 42.7 %copy-start.4 = (bf16[2,2,1,2,80,128]{5,4,3,2,1,0:T(8,128)(2,1)}, bf16[2,2,1,2,80,128]{5,4,3,2,1,0:T(8,128)(2,1)S(1)}, u32[]{:S(2)}) copy-start(bf16[2,2,1,2,80,128]{5,4,3,2,1,0:T(8,128)(2,1)S(1)} %collective-permute-done.4.refs_2_) | copy-start | bytes 491524
  30.7 1.1 copy-start.10
  30.8 0.9 copy-start.16
  31.7 38.3 %copy-start.11 = (bf16[2,2,1,2,80,128]{5,4,3,2,1,0:T(8,128)(2,1)S(1)}, bf16[2,2,1,2,80,128]{5,4,3,2,1,0:T(8,128)(2,1)}, u32[]{:S(2)}) copy-start(bf16[2,2,1,2,80,128]{5,4,3,2,1,0:T(8,128)(2,1)} %get-tuple-element.48) | copy-start | bytes 491524
  66.7 36.4 %copy-start.13 = (bf16[1,2,1,2,80,128]{5,4,3,2,1,0:T(8,128)(2,1)S(1)}, bf16[1,2,1,2,80,128]{5,4,3,2,1,0:T(8,128)(2,1)}, u32[]{:S(2)}) copy-start(bf16[1,2,1,2,80,128]{5,4,3,2,1,0:T(8,128)(2,1)} %get-tuple-element.53) | copy-start | bytes 245764
  66.7 37.4 %copy-start.12 = (bf16[1,2,1,2,80,128]{5,4,3,2,1,0:T(8,128)(2,1)S(1)}, bf16[1,2,1,2,80,128]{5,4,3,2,1,0:T(8,128)(2,1)}, u32[]{:S(2)}) copy-start(bf16[1,2,1,2,80,128]{5,4,3,2,1,0:T(8,128)(2,1)} %get-tuple-element.54) | copy-start | bytes 245764
  66.7 29.1 %collective-permute-start.5 = (bf16[512,1280]{1,0:T(8,128)(2,1)}, bf16[512,1280]{1,0:T(8,128)(2,1)S(1)}, u32[]{:S(2)}, u32[]{:S(2)}) collective-permute-start(bf16[512,1280]{1,0:T(8,128)(2,1)} %get-tuple-element.43), channel_id=1, source_target_pairs={{0,1},{1,0},{2,3},{3,2},{4,5},{5,4},{6,7},{7,6},{8,9},{9,8},{10,11... | collective-permute-start | bytes 3932168 | tf_op jit(solution)/shard_map/ppermute | solution.py:531
  68.0 22.0 %collective-permute-start.6 = (bf16[2,2,1,2,80,128]{5,4,3,2,1,0:T(8,128)(2,1)}, bf16[2,2,1,2,80,128]{5,4,3,2,1,0:T(8,128)(2,1)S(1)}, u32[]{:S(2)}, u32[]{:S(2)}) collective-permute-start(bf16[2,2,1,2,80,128]{5,4,3,2,1,0:T(8,128)(2,1)} %get-tuple-element.47), channel_id=1, source_target_pairs={{0,8},{2,10},{4,12},{6,14},{8,0},{10,2},{12,4},{14,6},{16,24},{18,... | collective-permute-start | bytes 491528 | tf_op jit(solution)/shard_map/ppermute | solution.py:537
  70.0 25.3 %collective-permute-start.7 = (bf16[2,2,1,2,80,128]{5,4,3,2,1,0:T(8,128)(2,1)S(1)}, bf16[2,2,1,2,80,128]{5,4,3,2,1,0:T(8,128)(2,1)S(1)}, u32[]{:S(2)}, u32[]{:S(2)}) collective-permute-start(bf16[2,2,1,2,80,128]{5,4,3,2,1,0:T(8,128)(2,1)S(1)} %copy-done.11), channel_id=1, source_target_pairs={{0,12},{2,14},{4,8},{6,10},{8,4},{10,6},{12,0},{14,2},{16,28},{18,... | collective-permute-start | bytes 491528 | tf_op jit(solution)/shard_map/ppermute | solution.py:537
  90.1 5.8 %copy-start.5 = (bf16[2,2,1,2,80,128]{5,4,3,2,1,0:T(8,128)(2,1)}, bf16[2,2,1,2,80,128]{5,4,3,2,1,0:T(8,128)(2,1)S(1)}, u32[]{:S(2)}) copy-start(bf16[2,2,1,2,80,128]{5,4,3,2,1,0:T(8,128)(2,1)S(1)} %collective-permute-done.6.refs_3_) | copy-start | bytes 491524
  95.3 0.7 copy-start.6
  95.3 5.8 %copy-start.15 = (bf16[1,2,1,2,80,128]{5,4,3,2,1,0:T(8,128)(2,1)S(1)}, bf16[1,2,1,2,80,128]{5,4,3,2,1,0:T(8,128)(2,1)}, u32[]{:S(2)}) copy-start(bf16[1,2,1,2,80,128]{5,4,3,2,1,0:T(8,128)(2,1)} %get-tuple-element.51) | copy-start | bytes 245764
  95.3 7.7 %copy-start.14 = (bf16[1,2,1,2,80,128]{5,4,3,2,1,0:T(8,128)(2,1)S(1)}, bf16[1,2,1,2,80,128]{5,4,3,2,1,0:T(8,128)(2,1)}, u32[]{:S(2)}) copy-start(bf16[1,2,1,2,80,128]{5,4,3,2,1,0:T(8,128)(2,1)} %get-tuple-element.52) | copy-start | bytes 245764
  95.8 1.1 copy-start.1
  98.7 7.3 %collective-permute-start.8 = (bf16[6,2,1,2,80,128]{5,4,3,2,1,0:T(8,128)(2,1)}, bf16[6,2,1,2,80,128]{5,4,3,2,1,0:T(8,128)(2,1)S(1)}, u32[]{:S(2)}, u32[]{:S(2)}) collective-permute-start(bf16[6,2,1,2,80,128]{5,4,3,2,1,0:T(8,128)(2,1)} %relay.1), channel_id=1, source_target_pairs={{0,2},{2,0},{4,6},{6,4},{8,10},{10,8},{12,14},{14,12},{16,18},{18,... | collective-permute-start | bytes 1474568 | tf_op jit(solution)/shard_map/ppermute | solution.py:537
  101.1 16.5 %collective-permute-start.9 = (bf16[1,2,1,2,80,128]{5,4,3,2,1,0:T(8,128)(2,1)S(1)}, bf16[1,2,1,2,80,128]{5,4,3,2,1,0:T(8,128)(2,1)S(1)}, u32[]{:S(2)}, u32[]{:S(2)}) collective-permute-start(bf16[1,2,1,2,80,128]{5,4,3,2,1,0:T(8,128)(2,1)S(1)} %copy-done.15), channel_id=1, source_target_pairs={{0,24},{2,26},{4,28},{6,30},{8,16},{10,18},{12,20},{14,22},{16,8},... | collective-permute-start | bytes 245768 | tf_op jit(solution)/shard_map/ppermute | solution.py:537
  103.0 14.6 %collective-permute-start.10 = (bf16[1,2,1,2,80,128]{5,4,3,2,1,0:T(8,128)(2,1)S(1)}, bf16[1,2,1,2,80,128]{5,4,3,2,1,0:T(8,128)(2,1)S(1)}, u32[]{:S(2)}, u32[]{:S(2)}) collective-permute-start(bf16[1,2,1,2,80,128]{5,4,3,2,1,0:T(8,128)(2,1)S(1)} %copy-done.14), channel_id=1, source_target_pairs={{0,26},{2,24},{4,30},{6,28},{8,18},{10,16},{12,22},{14,20},{16,10}... | collective-permute-start | bytes 245768 | tf_op jit(solution)/shard_map/ppermute | solution.py:537
  103.1 18.3 %collective-permute-start.11 = (bf16[1,2,1,2,80,128]{5,4,3,2,1,0:T(8,128)(2,1)S(1)}, bf16[1,2,1,2,80,128]{5,4,3,2,1,0:T(8,128)(2,1)S(1)}, u32[]{:S(2)}, u32[]{:S(2)}) collective-permute-start(bf16[1,2,1,2,80,128]{5,4,3,2,1,0:T(8,128)(2,1)S(1)} %copy-done.13), channel_id=1, source_target_pairs={{0,28},{2,30},{4,24},{6,26},{8,20},{10,22},{12,16},{14,18},{16,12}... | collective-permute-start | bytes 245768 | tf_op jit(solution)/shard_map/ppermute | solution.py:537
  104.2 19.1 %collective-permute-start.12 = (bf16[1,2,1,2,80,128]{5,4,3,2,1,0:T(8,128)(2,1)S(1)}, bf16[1,2,1,2,80,128]{5,4,3,2,1,0:T(8,128)(2,1)S(1)}, u32[]{:S(2)}, u32[]{:S(2)}) collective-permute-start(bf16[1,2,1,2,80,128]{5,4,3,2,1,0:T(8,128)(2,1)S(1)} %copy-done.12), channel_id=1, source_target_pairs={{0,30},{2,28},{4,26},{6,24},{8,22},{10,20},{12,18},{14,16},{16,14}... | collective-permute-start | bytes 245768 | tf_op jit(solution)/shard_map/ppermute | solution.py:537
  106.0 3.6 %copy-start.7 = (bf16[6,2,1,2,80,128]{5,4,3,2,1,0:T(8,128)(2,1)}, bf16[6,2,1,2,80,128]{5,4,3,2,1,0:T(8,128)(2,1)S(1)}, u32[]{:S(2)}) copy-start(bf16[6,2,1,2,80,128]{5,4,3,2,1,0:T(8,128)(2,1)S(1)} %collective-permute-done.8.refs_6_) | copy-start | bytes 1474564
  112.5 10.7 %copy-start = (s32[1,16,2]{1,2,0:T(2,128)S(1)}, s32[1,16,2]{1,2,0:T(2,128)}, u32[]{:S(2)}) copy-start(s32[1,16,2]{1,2,0:T(2,128)} %param.24) | copy-start | bytes 388
